TPU v7x, 32 devices: a whole 2x2x4 slice. The times are simulated.
32 devices in a mesh: fsdp: 4 (over y, x), ctx: 4 (over z), tp: 2 (over core).
Axes of the slice: x: 2, y: 2, z: 4, core: 2. Of those that a mesh axis runs over, the one named last changes fastest.
Arguments:
- tokens: bfloat16 [8, 1568, 1024], P('fsdp', 'ctx'), may hold values from -6 to 6
- clip_mask: int32 [8], P('fsdp'), may hold values 0 or 1
- cotangent: bfloat16 [8, 1568, 1024], P('fsdp', 'ctx'), may hold values from -6 to 6
- first_gain: float32 [1024], replicated, may hold values from 0.1 to 1.9
- first_shift: float32 [1024], replicated, may hold values from -1.75 to 1.75
- joint_weight: bfloat16 [1024, 3, 1024], P('fsdp', None, 'tp'), may hold values from -0.1875 to 0.1875
- joint_bias: float32 [2, 1024], P(None, 'tp'), may hold values from -0.625 to 0.625
- mixer_weight: bfloat16 [1024, 1024], P('fsdp', 'tp'), may hold values from -2 to 2
- mixer_bias: float32 [1024], replicated, may hold values from -1.75 to 1.75
- second_gain: float32 [1024], replicated, may hold values from 0.1 to 1.9
- second_shift: float32 [1024], replicated, may hold values from -1.75 to 1.75
- expand_weight: bfloat16 [1024, 4096], P('fsdp', 'tp'), may hold values from -0.1875 to 0.1875
- expand_bias: float32 [4096], P('tp'), may hold values from -1.75 to 1.75
- reduce_weight: bfloat16 [1024, 4096], P('fsdp', 'tp'), may hold values from -0.09375 to 0.09375
- reduce_bias: float32 [1024], replicated, may hold values from -1.75 to 1.75
Outputs:
- result: bfloat16 [8, 1568, 1024], P('fsdp', 'ctx')
- tokens_grad: float32 [8, 1568, 1024], P('fsdp', 'ctx')
- grad_first_gain: float32 [1024], P('fsdp')
- grad_first_shift: float32 [1024], P('fsdp')
- grad_joint_weight: float32 [1024, 3, 1024], P('fsdp', None, 'tp')
- grad_joint_bias: float32 [2, 1024], P(None, ('tp', 'fsdp'))
- grad_mixer_weight: float32 [1024, 1024], P('fsdp', 'tp')
- grad_mixer_bias: float32 [1024], P('fsdp')
- grad_second_gain: float32 [1024], P('fsdp')
- grad_second_shift: float32 [1024], P('fsdp')
- grad_expand_weight: float32 [1024, 4096], P('fsdp', 'tp')
- grad_expand_bias: float32 [4096], P(('tp', 'fsdp'))
- grad_reduce_weight: float32 [1024, 4096], P('fsdp', 'tp')
- grad_reduce_bias: float32 [1024], P('fsdp')
Inputs may be any that keep to these rules, and one draw needn't show every extreme that they name: `clip_mask`: 1 marks a real clip, 0 a padding clip.
All inputs are finite; a program needn't handle non-finite values. No bound on the sum of `clip_mask` on one device may be relied on, other than what follows from the above.
Results may differ from a plain program's by a relative error of at most 0.02.
Values may be sent and summed in bfloat16 or wider, within the bound.
No kernel may reach another device: no remote copies, remote signals or barrier semaphores. Data moves between devices by JAX's collectives and lax.ppermute only.
A program may use at most 192 MiB of HBM per device.

v0:
```python
from functools import partial

import jax
import jax.numpy as jnp
from jax import lax
from jax.sharding import PartitionSpec as P

HEAD_DIM = 64


EPSILON = 1e-06
NEGATIVE = -1e30


def normalize(value_rows):
    center = value_rows - jnp.mean(value_rows, axis=-1, keepdims=True)
    inverse = lax.rsqrt(jnp.mean(center * center, axis=-1, keepdims=True) + EPSILON)
    return (center * inverse, inverse)


def norm_back(upstream, gain, scaled, inverse):
    weighted = upstream * gain
    return inverse * (
        weighted
        - jnp.mean(weighted, axis=-1, keepdims=True)
        - scaled * jnp.mean(weighted * scaled, axis=-1, keepdims=True)
    )


def split_heads(value_rows, head_width):
    return value_rows.reshape(value_rows.shape[0], value_rows.shape[1], -1, head_width)


def fold_keys(queries, score_scale, carry, piece):
    running_max, running_sum, total = carry
    keys_piece, values_piece = piece
    head_width = queries.shape[3]
    attention_scores = (
        jnp.einsum(
            "clhd,cphd->chlp",
            queries,
            split_heads(keys_piece, head_width),
            preferred_element_type=jnp.float32,
        )
        * score_scale
    )
    new_max = jnp.maximum(running_max, jnp.max(attention_scores, axis=-1))
    weights = jnp.exp(attention_scores - new_max[..., None])
    running_sum = jnp.sum(weights, axis=-1)
    total = jnp.einsum(
        "chlp,cphd->chld",
        weights.astype(jnp.bfloat16),
        split_heads(values_piece, head_width),
        preferred_element_type=jnp.float32,
    )
    return (new_max, running_sum, total)


def per_device(
    tokens,
    clip_mask,
    cotangent,
    first_gain,
    first_shift,
    joint_weight,
    joint_bias,
    mixer_weight,
    mixer_bias,
    second_gain,
    second_shift,
    expand_weight,
    expand_bias,
    reduce_weight,
    reduce_bias,
):
    score_scale = HEAD_DIM ** (-0.5)
    clips_here, rows_here, model_width = tokens.shape
    inputs = tokens.astype(jnp.float32)
    valid = clip_mask.astype(jnp.float32)[:, None, None]
    joint_full, mixer_full, expand_full, reduce_full = (
        lax.all_gather(joint_weight, "fsdp", axis=0, tiled=True),
        lax.all_gather(mixer_weight, "fsdp", axis=0, tiled=True),
        lax.all_gather(expand_weight, "fsdp", axis=0, tiled=True),
        lax.all_gather(reduce_weight, "fsdp", axis=0, tiled=True),
    )
    first_scaled, first_inverse = normalize(inputs)
    first_normed = (first_scaled * first_gain + first_shift).astype(jnp.bfloat16)
    joint_out = jnp.einsum(
        "cld,dte->clte", first_normed, joint_full, preferred_element_type=jnp.float32
    )
    queries = (joint_out[:, :, 0] + joint_bias[0]).astype(jnp.bfloat16)
    keys_local = joint_out[:, :, 1].astype(jnp.bfloat16)
    values_local = (joint_out[:, :, 2] + joint_bias[1]).astype(jnp.bfloat16)
    query_heads = split_heads(queries, HEAD_DIM)
    heads_here = query_heads.shape[2]
    start_carry = (
        jnp.full((clips_here, heads_here, rows_here), NEGATIVE, jnp.float32),
        jnp.zeros((clips_here, heads_here, rows_here), jnp.float32),
        jnp.zeros((clips_here, heads_here, rows_here, HEAD_DIM), jnp.float32),
    )
    running_max, running_sum, total = fold_keys(
        query_heads,
        score_scale,
        start_carry,
        (
            lax.all_gather(keys_local, "ctx", axis=1, tiled=True),
            lax.all_gather(values_local, "ctx", axis=1, tiled=True),
        ),
    )
    attended = total / running_sum[..., None]
    log_total = running_max + jnp.log(running_sum)
    mixed_in = (
        attended.transpose(0, 2, 1, 3).reshape(clips_here, rows_here, -1).astype(jnp.bfloat16)
    )
    mixer_part = jnp.einsum("cle,de->cld", mixed_in, mixer_full, preferred_element_type=jnp.float32)
    mixer_out = lax.psum(mixer_part.astype(jnp.bfloat16), "tp").astype(jnp.float32) + mixer_bias
    first_sum = inputs + mixer_out
    second_scaled, second_inverse = normalize(first_sum)
    second_normed = (second_scaled * second_gain + second_shift).astype(jnp.bfloat16)
    expanded = (
        jnp.einsum("cld,df->clf", second_normed, expand_full, preferred_element_type=jnp.float32)
        + expand_bias
    )
    activated, gelu_back = jax.vjp(partial(jax.nn.gelu, approximate=False), expanded)
    activated_low = activated.astype(jnp.bfloat16)
    reduce_part = jnp.einsum(
        "clf,df->cld", activated_low, reduce_full, preferred_element_type=jnp.float32
    )
    reduce_out = lax.psum(reduce_part.astype(jnp.bfloat16), "tp").astype(jnp.float32) + reduce_bias
    result = (inputs + valid * (mixer_out + reduce_out)).astype(jnp.bfloat16)
    outer = cotangent.astype(jnp.float32)
    branch_slope = outer * valid
    reduce_slope = branch_slope.astype(jnp.bfloat16)
    reduce_bias_grad = jnp.sum(reduce_slope.astype(jnp.float32), axis=(0, 1))
    reduce_grad = jnp.einsum(
        "cld,clf->df", reduce_slope, activated_low, preferred_element_type=jnp.float32
    )
    activated_slope = jnp.einsum(
        "cld,df->clf", reduce_slope, reduce_full, preferred_element_type=jnp.float32
    )
    expand_slope = gelu_back(activated_slope)[0].astype(jnp.bfloat16)
    expand_bias_grad = jnp.sum(expand_slope.astype(jnp.float32), axis=(0, 1))
    expand_grad = jnp.einsum(
        "cld,clf->df", second_normed, expand_slope, preferred_element_type=jnp.float32
    )
    second_part = jnp.einsum(
        "clf,df->cld", expand_slope, expand_full, preferred_element_type=jnp.float32
    )
    second_slope = lax.psum(second_part.astype(jnp.bfloat16), "tp").astype(jnp.float32)
    second_gain_grad = jnp.sum(second_slope * second_scaled, axis=(0, 1))
    second_shift_grad = jnp.sum(second_slope, axis=(0, 1))
    first_sum_back = norm_back(second_slope, second_gain, second_scaled, second_inverse)
    mixer_slope = (branch_slope + first_sum_back).astype(jnp.bfloat16)
    mixer_bias_grad = jnp.sum(mixer_slope.astype(jnp.float32), axis=(0, 1))
    mixer_grad = jnp.einsum(
        "cld,cle->de", mixer_slope, mixed_in, preferred_element_type=jnp.float32
    )
    attended_slope = jnp.einsum(
        "cld,de->cle", mixer_slope, mixer_full, preferred_element_type=jnp.float32
    ).astype(jnp.bfloat16)
    keys_whole, values_whole = (
        lax.all_gather(keys_local, "ctx", axis=1, tiled=True),
        lax.all_gather(values_local, "ctx", axis=1, tiled=True),
    )
    key_heads = split_heads(keys_whole, HEAD_DIM)
    value_heads = split_heads(values_whole, HEAD_DIM)
    attention_scores = (
        jnp.einsum("clhd,ckhd->chlk", query_heads, key_heads, preferred_element_type=jnp.float32)
        * score_scale
    )
    attention_probs = jnp.exp(attention_scores - log_total[..., None])
    probs_low = attention_probs.astype(jnp.bfloat16)
    slope_heads = split_heads(attended_slope, HEAD_DIM)
    row_delta = jnp.einsum("clhd,chld->chl", slope_heads.astype(jnp.float32), attended)
    prob_slope = jnp.einsum(
        "clhd,ckhd->chlk", slope_heads, value_heads, preferred_element_type=jnp.float32
    )
    score_slope = (attention_probs * (prob_slope - row_delta[..., None])).astype(jnp.bfloat16)
    query_slope = (
        jnp.einsum("chlk,ckhd->clhd", score_slope, key_heads, preferred_element_type=jnp.float32)
        * score_scale
    )
    feature_half = queries.shape[2]
    count = rows_here * lax.axis_size("ctx")
    key_part = (
        jnp.einsum("chlk,clhd->kchd", score_slope, query_heads, preferred_element_type=jnp.float32)
        * score_scale
    )
    value_part = jnp.einsum(
        "chlk,clhd->kchd", probs_low, slope_heads, preferred_element_type=jnp.float32
    )
    pair_slope = lax.psum_scatter(
        jnp.concatenate(
            [key_part.reshape(count, clips_here, -1), value_part.reshape(count, clips_here, -1)],
            axis=-1,
        ).astype(jnp.bfloat16),
        "ctx",
        scatter_dimension=0,
        tiled=True,
    ).astype(jnp.float32)
    key_flat = pair_slope[:, :, :feature_half].transpose(1, 0, 2)
    value_flat = pair_slope[:, :, feature_half:].transpose(1, 0, 2)
    joint_slope = jnp.stack(
        [query_slope.reshape(clips_here, rows_here, -1), key_flat, value_flat], axis=2
    ).astype(jnp.bfloat16)
    joint_bias_grad = jnp.sum(joint_slope[:, :, 0::2].astype(jnp.float32), axis=(0, 1))
    joint_grad = jnp.einsum(
        "cld,clte->dte", first_normed, joint_slope, preferred_element_type=jnp.float32
    )
    first_part = jnp.einsum(
        "clte,dte->cld", joint_slope, joint_full, preferred_element_type=jnp.float32
    )
    first_slope = lax.psum(first_part.astype(jnp.bfloat16), "tp").astype(jnp.float32)
    first_gain_grad = jnp.sum(first_slope * first_scaled, axis=(0, 1))
    first_shift_grad = jnp.sum(first_slope, axis=(0, 1))
    tokens_grad = (
        outer + first_sum_back + norm_back(first_slope, first_gain, first_scaled, first_inverse)
    )
    (
        joint_rows,
        mixer_rows,
        expand_rows,
        reduce_rows,
        first_gain_rows,
        first_shift_rows,
        joint_bias_rows,
        mixer_bias_rows,
        second_gain_rows,
        second_shift_rows,
        expand_bias_rows,
        reduce_bias_rows,
    ) = (
        lax.psum_scatter(
            joint_grad.astype(jnp.bfloat16), "fsdp", scatter_dimension=0, tiled=True
        ).astype(jnp.float32),
        lax.psum_scatter(
            mixer_grad.astype(jnp.bfloat16), "fsdp", scatter_dimension=0, tiled=True
        ).astype(jnp.float32),
        lax.psum_scatter(
            expand_grad.astype(jnp.bfloat16), "fsdp", scatter_dimension=0, tiled=True
        ).astype(jnp.float32),
        lax.psum_scatter(
            reduce_grad.astype(jnp.bfloat16), "fsdp", scatter_dimension=0, tiled=True
        ).astype(jnp.float32),
        lax.psum_scatter(
            first_gain_grad.astype(jnp.bfloat16), "fsdp", scatter_dimension=0, tiled=True
        ).astype(jnp.float32),
        lax.psum_scatter(
            first_shift_grad.astype(jnp.bfloat16), "fsdp", scatter_dimension=0, tiled=True
        ).astype(jnp.float32),
        lax.psum_scatter(
            joint_bias_grad.astype(jnp.bfloat16), "fsdp", scatter_dimension=1, tiled=True
        ).astype(jnp.float32),
        lax.psum_scatter(
            mixer_bias_grad.astype(jnp.bfloat16), "fsdp", scatter_dimension=0, tiled=True
        ).astype(jnp.float32),
        lax.psum_scatter(
            second_gain_grad.astype(jnp.bfloat16), "fsdp", scatter_dimension=0, tiled=True
        ).astype(jnp.float32),
        lax.psum_scatter(
            second_shift_grad.astype(jnp.bfloat16), "fsdp", scatter_dimension=0, tiled=True
        ).astype(jnp.float32),
        lax.psum_scatter(
            expand_bias_grad.astype(jnp.bfloat16), "fsdp", scatter_dimension=0, tiled=True
        ).astype(jnp.float32),
        lax.psum_scatter(
            reduce_bias_grad.astype(jnp.bfloat16), "fsdp", scatter_dimension=0, tiled=True
        ).astype(jnp.float32),
    )
    summed = (
        lax.psum(joint_rows.astype(jnp.bfloat16), "ctx").astype(jnp.float32),
        lax.psum(mixer_rows.astype(jnp.bfloat16), "ctx").astype(jnp.float32),
        lax.psum(expand_rows.astype(jnp.bfloat16), "ctx").astype(jnp.float32),
        lax.psum(reduce_rows.astype(jnp.bfloat16), "ctx").astype(jnp.float32),
        lax.psum(first_gain_rows.astype(jnp.bfloat16), "ctx").astype(jnp.float32),
        lax.psum(first_shift_rows.astype(jnp.bfloat16), "ctx").astype(jnp.float32),
        lax.psum(joint_bias_rows.astype(jnp.bfloat16), "ctx").astype(jnp.float32),
        lax.psum(mixer_bias_rows.astype(jnp.bfloat16), "ctx").astype(jnp.float32),
        lax.psum(second_gain_rows.astype(jnp.bfloat16), "ctx").astype(jnp.float32),
        lax.psum(second_shift_rows.astype(jnp.bfloat16), "ctx").astype(jnp.float32),
        lax.psum(expand_bias_rows.astype(jnp.bfloat16), "ctx").astype(jnp.float32),
        lax.psum(reduce_bias_rows.astype(jnp.bfloat16), "ctx").astype(jnp.float32),
    )
    return (
        result,
        tokens_grad,
        summed[4],
        summed[5],
        summed[0],
        summed[6],
        summed[1],
        summed[7],
        summed[8],
        summed[9],
        summed[2],
        summed[10],
        summed[3],
        summed[11],
    )


def solution(mesh):
    return jax.shard_map(
        per_device,
        mesh=mesh,
        in_specs=(
            P("fsdp", "ctx", None),
            P("fsdp"),
            P("fsdp", "ctx", None),
            P(),
            P(),
            P("fsdp", None, "tp"),
            P(None, "tp"),
            P("fsdp", "tp"),
            P(),
            P(),
            P(),
            P("fsdp", "tp"),
            P("tp"),
            P("fsdp", "tp"),
            P(),
        ),
        out_specs=(
            P("fsdp", "ctx", None),
            P("fsdp", "ctx", None),
            P("fsdp"),
            P("fsdp"),
            P("fsdp", None, "tp"),
            P(None, ("tp", "fsdp")),
            P("fsdp", "tp"),
            P("fsdp"),
            P("fsdp"),
            P("fsdp"),
            P("fsdp", "tp"),
            P(("tp", "fsdp")),
            P("fsdp", "tp"),
            P("fsdp"),
        ),
        check_vma=False,
    )
```

profile of v0, /device:TPU:0, one launch (start us, length us, event | category | flops | bytes accessed | tf_op | source)
XLA Modules:
  0.0 982.7 jit_solution(4219917974807375144)
XLA Ops:
  10.4 46.2 %all-gather.8.cloned.1.call-done = bf16[1024,3,512]{2,0,1:T(8,128)(2,1)} async-done(((bf16[256,3,512]{2,0,1:T(8,128)(2,1)}), bf16[1024,3,512]{2,0,1:T(8,128)(2,1)}) %all-gather.8.cloned.1.call-update) | async-done | bytes 3145744 | tf_op jit(solution)/shard_map/all_gather | solution.py:81
  70.5 58.9 %all-gather.18.cloned.1.call-done = bf16[2,1568,1,512]{3,1,2,0:T(8,128)(2,1)} async-done(((bf16[2,392,1,512]{3,1,2,0:T(8,128)(2,1)}), bf16[2,1568,1,512]{3,1,2,0:T(8,128)(2,1)}) %all-gather.18.cloned.1.call-update) | async-done | bytes 3211280 | tf_op jit(solution)/shard_map/all_gather | solution.py:106
  134.8 22.9 %fusion.85 = (f32[2,8,392]{2,1,0:T(8,128)S(1)}, f32[2,8,392,1568]{3,2,1,0:T(8,128)}) fusion(bf16[2,1568,8,64]{1,3,2,0:T(8,128)(2,1)} %bitcast.118, f32[2,392,8,64]{1,3,2,0:T(8,128)} %bitcast.122, f32[8,64]{1,0:T(8,128)S(1)} %add.163), kind=kOutput, calls=%fused_computation.130 | convolution fusion | flops 1279281024 | bytes 44182016 | tf_op jit(solution)/shard_map/clhd,cphd->chlp/dot_general | solution.py:39
  157.7 15.8 %fusion = f32[2,8,392]{2,1,0:T(8,128)S(1)} fusion(f32[2,8,392,1568]{3,2,1,0:T(8,128)} %get-tuple-element.56, f32[2,8,392]{2,1,0:T(8,128)S(1)} %broadcast_maximum_fusion), kind=kLoop, calls=%fused_computation.4 | loop fusion | flops 19662720 | bytes 39388160 | tf_op jit(solution)/shard_map/reduce_sum | solution.py:49
  173.5 21.4 %all-gather.10.cloned.1.call-done = bf16[2,1568,512]{2,1,0:T(8,128)(2,1)} async-done(((bf16[2,392,512]{2,1,0:T(8,128)(2,1)}), bf16[2,1568,512]{2,1,0:T(8,128)(2,1)}) %all-gather.10.cloned.1.call-update) | async-done | bytes 3211280 | tf_op jit(solution)/shard_map/all_gather | solution.py:107
  200.2 18.1 %fusion.60 = (bf16[2,392,8,64]{1,3,2,0:T(8,128)(2,1)S(1)}, f32[2,8,392,64]{2,3,1,0:T(8,128)}) fusion(f32[2,392,8]{1,2,0:T(8,128)S(1)} %bitcast.138, bf16[2,1568,8,64]{1,3,2,0:T(8,128)(2,1)} %bitcast.120, f32[2,8,392,1568]{3,2,1,0:T(8,128)} %get-tuple-element.56, f32[2,8,392]{2,1,0:T(8,128)S(1)} %broadcast_maximum_fusion), kind=kOutput, calls=%fused_computation.97 | convolution fusion | flops 1279287296 | bytes 45007872 | tf_op jit(solution)/shard_map/chlp,cphd->chld/dot_general | solution.py:50
  227.4 18.9 %all-reduce.16.cloned.1.call-done = bf16[2,392,1024]{2,1,0:T(8,128)(2,1)} async-done(((bf16[2,392,1024]{2,1,0:T(8,128)(2,1)}), bf16[2,392,1024]{2,1,0:T(8,128)(2,1)}) %all-reduce.16.cloned.1.call-update) | async-done | bytes 1605648 | tf_op jit(solution)/shard_map/psum | solution.py:116
  249.3 52.6 %all-gather.14.cloned.1.call-done = bf16[1024,2048]{1,0:T(8,128)(2,1)} async-done(((bf16[256,2048]{1,0:T(8,128)(2,1)}), bf16[1024,2048]{1,0:T(8,128)(2,1)}) %all-gather.14.cloned.1.call-update) | async-done | bytes 4194320 | tf_op jit(solution)/shard_map/all_gather | solution.py:83
  301.9 8.1 fusion.73
  313.0 16.2 %multiply_convert_fusion.2 = (bf16[2,392,2048]{2,1,0:T(8,128)(2,1)}, f32[2,392,2048]{2,1,0:T(8,128)}) fusion(f32[2,392,2048]{2,1,0:T(8,128)S(1)} %get-tuple-element.59, f32[2048]{0:T(1024)S(1)} %copy-done.29, u8[392,2048]{1,0:T(8,128)(4,1)S(1)} %get-tuple-element.15, u8[392,2048]{1,0:T(8,128)(4,1)S(1)} %get-tuple-element.14), kind=kLoop, calls=%fused_computation.23 | loop fusion | flops 113999872 | bytes 17670144 | tf_op jit(solution)/shard_map/convert_element_type | solution.py:125
  329.2 27.3 %all-gather.16.cloned.1.call-done = bf16[1024,2048]{1,0:T(8,128)(2,1)} async-done(((bf16[256,2048]{1,0:T(8,128)(2,1)}), bf16[1024,2048]{1,0:T(8,128)(2,1)}) %all-gather.16.cloned.1.call-update) | async-done | bytes 4194320 | tf_op jit(solution)/shard_map/all_gather | solution.py:84
  356.5 12.7 %fusion.86 = (bf16[2048]{0:T(1024)(128)(2,1)}, bf16[2,392,2048]{2,1,0:T(8,128)(2,1)S(1)}) fusion(f32[2,392,2048]{2,1,0:T(8,128)} %get-tuple-element.46, bf16[1024,2048]{1,0:T(8,128)(2,1)} %all-gather.16.cloned.1.call-done, bf16[2,392,1024]{2,1,0:T(8,128)(2,1)} %param.17, f32[2]{0:T(128)S(1)} %convert_element_type.176, f32[2,392,2048]{2,1,0:T(8,128)} %copy-done.6, ...), kind=kOutput, calls=%fused_computation.131 | convolution fusion | flops 3316430848 | bytes 21868552 | tf_op jit(solution)/shard_map/cld,df->clf/dot_general | solution.py:138
  375.7 20.5 %all-reduce.18.cloned.1.call-done = bf16[2,392,1024]{2,1,0:T(8,128)(2,1)} async-done(((bf16[2,392,1024]{2,1,0:T(8,128)(2,1)}), bf16[2,392,1024]{2,1,0:T(8,128)(2,1)}) %all-reduce.18.cloned.1.call-update) | async-done | bytes 1605648 | tf_op jit(solution)/shard_map/psum | solution.py:149
  410.9 18.5 %fusion.35 = bf16[2,8,64,1568]{3,2,1,0:T(8,128)(2,1)} fusion(bf16[2,392,8,64]{1,3,2,0:T(8,128)(2,1)} %bitcast.124, f32[2,8,392,1568]{3,2,1,0:T(8,128)} %get-tuple-element.56, f32[2,8,392]{2,1,0:T(8,128)S(1)} %log_add_fusion), kind=kOutput, calls=%fused_computation.67 | convolution fusion | flops 1280090112 | bytes 43377152 | tf_op jit(solution)/shard_map/chlk,clhd->kchd/dot_general | solution.py:189
  429.4 23.1 %multiply_convert_fusion = bf16[2,8,392,1568]{3,2,1,0:T(8,128)(2,1)} fusion(bf16[2,392,8,64]{1,3,2,0:T(8,128)(2,1)} %bitcast.125, bf16[2,1568,8,64]{1,3,2,0:T(8,128)(2,1)} %bitcast.121, f32[2,8,392,1568]{3,2,1,0:T(8,128)} %get-tuple-element.56, f32[2,8,392]{2,1,0:T(8,128)S(1)} %fusion.59, f32[2,8,392]{2,1,0:T(8,128)S(1)} %log_add_fusion), kind=kOutput, calls=%fused_computation | convolution fusion | flops 1298153472 | bytes 63071232 | tf_op jit(solution)/shard_map/clhd,ckhd->chlk/dot_general | solution.py:175
  452.5 12.4 %multiply_convert_fusion.1 = bf16[2,8,64,1568]{3,2,1,0:T(8,128)(2,1)} fusion(bf16[2,8,392,1568]{3,2,1,0:T(8,128)(2,1)} %multiply_convert_fusion, f32[2,392,8,64]{1,3,2,0:T(8,128)S(1)} %bitcast.123, f32[8,64]{1,0:T(8,128)S(1)} %add.163), kind=kOutput, calls=%fused_computation.14 | convolution fusion | flops 1262829568 | bytes 24487936 | tf_op jit(solution)/shard_map/chlk,clhd->kchd/dot_general | solution.py:186
  465.0 5.6 copy.59
  487.4 9.1 bitcast_convert_fusion
  496.6 8.6 bitcast_convert_fusion.1
  505.3 12.2 %multiply_convert_fusion.3 = bf16[2,8,64,392]{3,2,1,0:T(8,128)(2,1)} fusion(bf16[2,1568,8,64]{1,3,2,0:T(8,128)(2,1)} %bitcast.119, bf16[2,8,392,1568]{3,2,1,0:T(8,128)(2,1)} %multiply_convert_fusion), kind=kOutput, calls=%fused_computation.98 | convolution fusion | flops 1259618304 | bytes 23683072 | tf_op jit(solution)/shard_map/chlk,ckhd->clhd/dot_general | solution.py:180
  519.7 77.8 %reduce-scatter.19.cloned.1.call-done = bf16[392,2048]{1,0:T(8,128)(2,1)} async-done(((bf16[1568,2048]{1,0:T(8,128)(2,1)}), bf16[392,2048]{1,0:T(8,128)(2,1)}) %reduce-scatter.19.cloned.1.call-update) | async-done | bytes 1605648
  612.3 8.1 fusion.66
  622.1 6.6 bitcast_convert_fusion.3
  629.1 56.0 %reduce-scatter.17.cloned.1.call-done = bf16[256,2048]{1,0:T(8,128)(2,1)} async-done(((bf16[1024,2048]{1,0:T(8,128)(2,1)}), bf16[256,2048]{1,0:T(8,128)(2,1)}) %reduce-scatter.17.cloned.1.call-update) | async-done | bytes 1048592 | tf_op jit(solution)/shard_map/reduce_scatter | solution.py:242
  685.1 55.5 %reduce-scatter.15.cloned.1.call-done = bf16[256,2048]{1,0:T(8,128)(2,1)} async-done(((bf16[1024,2048]{1,0:T(8,128)(2,1)}), bf16[256,2048]{1,0:T(8,128)(2,1)}) %reduce-scatter.15.cloned.1.call-update) | async-done | bytes 1048592 | tf_op jit(solution)/shard_map/reduce_scatter | solution.py:239
  740.6 47.2 %reduce-scatter.11.cloned.1.call-done = bf16[256,3,512]{2,0,1:T(8,128)(2,1)} async-done(((bf16[1024,3,512]{2,0,1:T(8,128)(2,1)}), bf16[256,3,512]{2,0,1:T(8,128)(2,1)}) %reduce-scatter.11.cloned.1.call-update) | async-done | bytes 786448 | tf_op jit(solution)/shard_map/reduce_scatter | solution.py:233
  789.9 25.2 %reduce-scatter.21.cloned.1.call-done = bf16[128,2]{1,0:T(8,128)(2,1)} async-done(((bf16[512,2]{1,0:T(8,128)(2,1)}), bf16[128,2]{1,0:T(8,128)(2,1)}) %reduce-scatter.21.cloned.1.call-update) | async-done | bytes 528
  815.9 26.0 %all-reduce.22.cloned.1.call-done = (bf16[2,392,1024]{2,1,0:T(8,128)(2,1)}, bf16[2,392,1024]{2,1,0:T(8,128)(2,1)}) async-done(((bf16[2,392,1024]{2,1,0:T(8,128)(2,1)}, bf16[2,392,1024]{2,1,0:T(8,128)(2,1)}), (bf16[2,392,1024]{2,1,0:T(8,128)(2,1)}, bf16[2,392,1024]{2,1,0:T(8,128)(2,1)})) %all-reduce.22.cloned.1.call-update) | async-done | bytes 3211280 | tf_op jit(solution)/shard_map/psum | solution.py:129
  846.8 16.3 %all-reduce.9 = (bf16[1024]{0:T(1024)(128)(2,1)S(1)}, bf16[1024]{0:T(1024)(128)(2,1)S(1)}, bf16[1024]{0:T(1024)(128)(2,1)S(1)}, bf16[1024]{0:T(1024)(128)(2,1)S(...) all-reduce(bf16[1024]{0:T(1024)(128)(2,1)S(1)} %get-tuple-element.1, ...), channel_id=4, replica_groups=mesh['fsdp'=4,'ctx'=4,'tp'=2] {'fsdp'}, use_global_device_ids=true, to_apply=%region_16.0.clone | all-reduce | flops 8192 | bytes 32768
  863.6 12.7 %all-reduce.7 = (bf16[256]{0:T(256)(128)(2,1)S(1)}, bf16[256]{0:T(256)(128)(2,1)S(1)}, bf16[2,128]{1,0:T(2,128)(2,1)S(1)}, bf16[256]{0:T(256)(128)(2,1)S(1)}, bf...) all-reduce(bf16[256]{0:T(256)(128)(2,1)S(1)} %dynamic-slice.1, ...), channel_id=1, replica_groups=mesh['fsdp'=4,'ctx'=4,'tp'=2] {'ctx'}, use_global_device_ids=true, to_apply=%region_17.0 | all-reduce | flops 2304 | bytes 9216 | tf_op jit(solution)/shard_map/psum | solution.py:275
  880.9 7.2 fusion.42
  888.2 80.2 %all-reduce.20.cloned.1.call-done = (bf16[256,3,512]{2,0,1:T(8,128)(2,1)}, bf16[256,512]{1,0:T(8,128)(2,1)}, bf16[256,2048]{1,0:T(8,128)(2,1)}, bf16[256,2048]{1,0:T(8,128)(2,1)}) async-done(((bf16[256,3,512]{2,0,1:T(8,128)(2,1)}, bf16[256,512]{1,0:T(8,128)(2,1)}, bf16[256,2048]{1,0:T(8,128)(2,1)}, bf16[256,2048]{1,0:T(8,128)(2,1)}), (bf16[256,3,512]{2,0,1:T(8,128)(2,1)}, bf16[256,512]{1,0:T(8,128)(2,1)}, ...) | async-done | bytes 3145744 | tf_op jit(solution)/shard_map/psum | solution.py:271
  (191 shorter events, 118.4 us)
Async XLA Ops:
  7.2 49.4 %copy-start.27 = (f32[1024]{0:T(1024)S(1)}, f32[1024]{0:T(1024)}, u32[]{:S(2)}) copy-start(f32[1024]{0:T(1024)} %param.18) | copy-start | bytes 12292
  7.2 49.4 %all-gather.8.cloned.1.call-start = ((), (), s32[]{:S(2)}) async-start(), calls=%async_computation.6 | async-start | bytes 3932160 | tf_op jit(solution)/shard_map/all_gather | solution.py:81
  7.9 121.5 %all-gather.18.cloned.1.call-start = ((), (), s32[]{:S(2)}) async-start(), calls=%async_computation.17 | async-start | bytes 4014080 | tf_op jit(solution)/shard_map/all_gather | solution.py:106
  9.7 51.8 %copy-start.18 = (f32[2,392]{1,0:T(2,128)}, f32[2,392]{1,0:T(2,128)S(1)}, u32[]{:S(2)}) copy-start(f32[2,392]{1,0:T(2,128)S(1)} %broadcast_multiply_fusion.5) | copy-start | bytes 9412
  10.3 51.2 %copy-start.25 = (f32[2,392]{1,0:T(2,128)}, f32[2,392]{1,0:T(2,128)S(1)}, u32[]{:S(2)}) copy-start(f32[2,392]{1,0:T(2,128)S(1)} %add_rsqrt_fusion.1) | copy-start | bytes 9412
  10.3 54.4 %copy-start.35 = (f32[2,512]{1,0:T(2,128)S(1)}, f32[2,512]{1,0:T(2,128)}, u32[]{:S(2)}) copy-start(f32[2,512]{1,0:T(2,128)} %param.21) | copy-start | bytes 12292
  64.7 130.1 %all-gather.10.cloned.1.call-start = ((), (), s32[]{:S(2)}) async-start(), calls=%async_computation.7 | async-start | bytes 4014080 | tf_op jit(solution)/shard_map/all_gather | solution.py:107
  67.5 154.5 %all-gather.12.cloned.1.call-start = ((), (), s32[]{:S(2)}) async-start(), calls=%async_computation.8 | async-start | bytes 1310720 | tf_op jit(solution)/shard_map/all_gather | solution.py:82
  68.1 178.2 %all-reduce.16.cloned.1.call-start = ((), (), s32[]{:S(2)}) async-start(), calls=%async_computation.9 | async-start | bytes 3211264 | tf_op jit(solution)/shard_map/psum | solution.py:116
  225.8 76.2 %all-gather.14.cloned.1.call-start = ((), (), s32[]{:S(2)}) async-start(), calls=%async_computation.10 | async-start | bytes 5242880 | tf_op jit(solution)/shard_map/all_gather | solution.py:83
  226.3 130.1 %all-gather.16.cloned.1.call-start = ((), (), s32[]{:S(2)}) async-start(), calls=%async_computation.11 | async-start | bytes 5242880 | tf_op jit(solution)/shard_map/all_gather | solution.py:84
  227.1 169.1 %all-reduce.18.cloned.1.call-start = ((), (), s32[]{:S(2)}) async-start(), calls=%async_computation.12 | async-start | bytes 3211264 | tf_op jit(solution)/shard_map/psum | solution.py:149
  227.3 74.6 %copy-start.24 = (f32[1024]{0:T(1024)S(1)}, f32[1024]{0:T(1024)}, u32[]{:S(2)}) copy-start(f32[1024]{0:T(1024)} %param.24) | copy-start | bytes 12292
  227.3 74.6 %copy-start.29 = (f32[2048]{0:T(1024)S(1)}, f32[2048]{0:T(1024)}, u32[]{:S(2)}) copy-start(f32[2048]{0:T(1024)} %param.27) | copy-start | bytes 24580
  227.4 74.6 %copy-start.39 = (f32[1024]{0:T(1024)S(1)}, f32[1024]{0:T(1024)}, u32[]{:S(2)}) copy-start(f32[1024]{0:T(1024)} %param.25) | copy-start | bytes 12292
  375.6 221.9 %reduce-scatter.19.cloned.1.call-start = ((), (), s32[]{:S(2)}) async-start(), calls=%async_computation.18 | async-start | bytes 8028160
  483.3 145.8 %reduce-scatter.13.cloned.1.call-start = ((), (), s32[]{:S(2)}) async-start(), calls=%async_computation.14 | async-start | bytes 1310720 | tf_op jit(solution)/shard_map/reduce_scatter | solution.py:236
  487.4 197.7 %reduce-scatter.17.cloned.1.call-start = ((), (), s32[]{:S(2)}) async-start(), calls=%async_computation.16 | async-start | bytes 5242880 | tf_op jit(solution)/shard_map/reduce_scatter | solution.py:242
  496.5 244.1 %reduce-scatter.15.cloned.1.call-start = ((), (), s32[]{:S(2)}) async-start(), calls=%async_computation.15 | async-start | bytes 5242880 | tf_op jit(solution)/shard_map/reduce_scatter | solution.py:239
  505.2 282.6 %reduce-scatter.11.cloned.1.call-start = ((), (), s32[]{:S(2)}) async-start(), calls=%async_computation.13 | async-start | bytes 3932160 | tf_op jit(solution)/shard_map/reduce_scatter | solution.py:233
  612.2 202.9 %reduce-scatter.21.cloned.1.call-start = ((), (), s32[]{:S(2)}) async-start(), calls=%async_computation.19 | async-start | bytes 163840
  621.8 220.1 %all-reduce.22.cloned.1.call-start = ((), (), s32[]{:S(2)}) async-start(), calls=%async_computation.21 | async-start | bytes 6422528 | tf_op jit(solution)/shard_map/psum | solution.py:129
  628.8 159.2 %copy-start.43 = (u32[32]{0:T(128)S(1)}, u32[32]{0:T(128)}, u32[]{:S(2)}) copy-start(u32[32]{0:T(128)} %constant.96) | copy-start | bytes 388
  628.8 339.5 %all-reduce.20.cloned.1.call-start = ((), (), s32[]{:S(2)}) async-start(), calls=%async_computation.20 | async-start | bytes 6291456 | tf_op jit(solution)/shard_map/psum | solution.py:271
  787.9 58.9 %copy-start.30 = (bf16[1024]{0:T(1024)(128)(2,1)S(1)}, bf16[1024]{0:T(1024)(128)(2,1)}, u32[]{:S(2)}) copy-start(bf16[1024]{0:T(1024)(128)(2,1)} %get-tuple-element.16) | copy-start | bytes 6148
  787.9 58.9 %copy-start.31 = (bf16[1024]{0:T(1024)(128)(2,1)S(1)}, bf16[1024]{0:T(1024)(128)(2,1)}, u32[]{:S(2)}) copy-start(bf16[1024]{0:T(1024)(128)(2,1)} %get-tuple-element.43) | copy-start | bytes 6148
  787.9 58.9 %copy-start.32 = (bf16[1024]{0:T(1024)(128)(2,1)S(1)}, bf16[1024]{0:T(1024)(128)(2,1)}, u32[]{:S(2)}) copy-start(bf16[1024]{0:T(1024)(128)(2,1)} %get-tuple-element.49) | copy-start | bytes 6148
  787.9 58.9 %copy-start.33 = (bf16[1024]{0:T(1024)(128)(2,1)S(1)}, bf16[1024]{0:T(1024)(128)(2,1)}, u32[]{:S(2)}) copy-start(bf16[1024]{0:T(1024)(128)(2,1)} %get-tuple-element.50) | copy-start | bytes 6148
  787.9 58.9 %copy-start.36 = (bf16[2048]{0:T(1024)(128)(2,1)S(1)}, bf16[2048]{0:T(1024)(128)(2,1)}, u32[]{:S(2)}) copy-start(bf16[2048]{0:T(1024)(128)(2,1)} %get-tuple-element.60) | copy-start | bytes 12292
  787.9 93.0 %copy-start.21 = (f32[2,392]{1,0:T(2,128)S(1)}, f32[2,392]{1,0:T(2,128)}, u32[]{:S(2)}) copy-start(f32[2,392]{1,0:T(2,128)} %copy-done.20) | copy-start | bytes 9412
  787.9 93.0 %copy-start.23 = (f32[2,392]{1,0:T(2,128)S(1)}, f32[2,392]{1,0:T(2,128)}, u32[]{:S(2)}) copy-start(f32[2,392]{1,0:T(2,128)} %copy-done.22) | copy-start | bytes 9412
  788.0 93.0 %copy-start.34 = (f32[1024]{0:T(1024)S(1)}, f32[1024]{0:T(1024)}, u32[]{:S(2)}) copy-start(f32[1024]{0:T(1024)} %param.29) | copy-start | bytes 12292
  (30 other events, 215.9 us)
Sparse Core Ops, SparseCore 0:
  9.9 46.6 all-gather.7
  64.9 64.5 all-gather.17
  131.6 63.2 all-gather.9
  196.6 25.3 all-gather.11
  225.9 20.3 all-reduce.15
  248.0 53.8 all-gather.13
  303.7 52.6 all-gather.15
  375.7 20.4 all-reduce.17
  483.4 114.0 reduce-scatter.18
  600.8 28.2 reduce-scatter.12
  632.3 52.6 reduce-scatter.16
  687.9 52.6 reduce-scatter.14
  743.9 43.9 reduce-scatter.10
  791.2 23.8 reduce-scatter.20
  818.5 23.3 all-reduce.21
  844.6 123.7 all-reduce.19
where the time goes:
time: 987 us; the launch traced here: 983 us
  waiting for transfers between devices  620 us (63%)
  matrix products  185 us (19%)
  other arithmetic  77.8 us (8%)
  local copies, waits for them, and re-layouts  52.6 us (5%)
  blocking collectives  29 us (3%)
  between operations  16.1 us (2%)
    unnamed x18, waiting for transfers between devices  106 us
    psum x1, waiting for transfers between devices, per_device(): lax.psum(joint_rows.astype(jnp.bfloat16), 'ctx').astype(jnp.float32)  80.2 us
    all_gather x1, waiting for transfers between devices, per_device(): lax.all_gather(keys_local, 'ctx', axis=1, tiled=True)  58.9 us
    reduce_scatter x1, waiting for transfers between devices, per_device(): lax.psum_scatter(reduce_grad.astype(jnp.bfloat16), 'fsdp', scatter_dimens...  56 us
    reduce_scatter x1, waiting for transfers between devices, per_device(): lax.psum_scatter(expand_grad.astype(jnp.bfloat16), 'fsdp', scatter_dimens...  55.5 us
    all_gather x1, waiting for transfers between devices, per_device(): lax.all_gather(expand_weight, 'fsdp', axis=0, tiled=True)  52.6 us
    reduce_scatter x1, waiting for transfers between devices, per_device(): lax.psum_scatter(joint_grad.astype(jnp.bfloat16), 'fsdp', scatter_dimensi...  47.2 us
    all_gather x1, waiting for transfers between devices, per_device(): lax.all_gather(joint_weight, 'fsdp', axis=0, tiled=True)  46.2 us
  transfers between devices with their start and end apart: 16, of which 16 were waited for; matrix products, arithmetic and copies ran while one was open for 19% of the time, Pallas kernels for 0%

commit v1 on v0

v1 whole, which is shorter than its diff:
```python
from functools import partial

import jax
import jax.numpy as jnp
from jax import lax
from jax.experimental import pallas as pl
from jax.experimental.pallas import tpu as pltpu
from jax.sharding import PartitionSpec as P

HEAD_DIM = 64
EPSILON = 1e-06
LOW = jnp.bfloat16
FULL = jnp.float32

ROW_BY_ROW = (((1,), (1,)), ((), ()))
PLAIN = (((1,), (0,)), ((), ()))
COLUMN_BY_COLUMN = (((0,), (0,)), ((), ()))


def product(left, right, dims):
    return lax.dot_general(left, right, dims, preferred_element_type=FULL)


def normalize(value_rows):
    center = value_rows - jnp.mean(value_rows, axis=-1, keepdims=True)
    inverse = lax.rsqrt(jnp.mean(center * center, axis=-1, keepdims=True) + EPSILON)
    return (center * inverse, inverse)


def norm_back(upstream, gain, scaled, inverse):
    weighted = upstream * gain
    return inverse * (
        weighted
        - jnp.mean(weighted, axis=-1, keepdims=True)
        - scaled * jnp.mean(weighted * scaled, axis=-1, keepdims=True)
    )


def attention_forward_kernel(q_ref, k_ref, v_ref, o_ref, lse_ref):
    rows, width = q_ref.shape
    scale = jnp.asarray(HEAD_DIM ** (-0.5), LOW)
    lane = lax.broadcasted_iota(jnp.int32, (rows, 128), 1)
    lse = jnp.zeros((rows, 128), FULL)
    for pair in range(width // 128):
        columns = slice(128 * pair, 128 * pair + 128)
        q = q_ref[:, columns] * scale
        k = k_ref[:, columns]
        v = v_ref[:, columns]
        out = None
        for side in range(2):
            mask = (lane // HEAD_DIM) == side
            scores = product(jnp.where(mask, q, jnp.zeros_like(q)), k, ROW_BY_ROW)
            top = jnp.max(scores, axis=-1, keepdims=True)
            weights = jnp.exp(scores - top)
            total = jnp.sum(weights, axis=-1, keepdims=True)
            part = product(weights.astype(LOW), v, PLAIN) / total
            out = part if side == 0 else jnp.where(mask, part, out)
            lse = jnp.where(lane == 2 * pair + side, top + jnp.log(total), lse)
        o_ref[:, columns] = out.astype(LOW)
    lse_ref[0] = lse.T[: lse_ref.shape[1]]


def row_chunk(count):
    for chunk in range(256, 0, -16):
        if count % chunk == 0:
            return chunk
    raise ValueError("rows")


def attention_forward(q, k, v):
    count, width = q.shape
    chunk = row_chunk(count)
    steps = count // chunk
    part = pl.BlockSpec((chunk, width), lambda i: (i, 0))
    whole = pl.BlockSpec((count, width), lambda i: (0, 0))
    out, lse = pl.pallas_call(
        attention_forward_kernel,
        grid=(steps,),
        in_specs=[part, whole, whole],
        out_specs=[part, pl.BlockSpec((1, 8, chunk), lambda i: (i, 0, 0))],
        out_shape=[
            jax.ShapeDtypeStruct((count, width), LOW),
            jax.ShapeDtypeStruct((steps, 8, chunk), FULL),
        ],
        compiler_params=pltpu.CompilerParams(vmem_limit_bytes=48 << 20),
        name="attention_forward",
    )(q, k, v)
    return out, lse.transpose(1, 0, 2).reshape(8, count)


def attention_backward_kernel(
    q_ref, k_ref, v_ref, da_ref, o_ref, lse_ref, dq_ref, dk_ref, dv_ref,
    q_heads, da_heads, delta_ref, dq_total,
):
    count, width = q_ref.shape
    chunk = k_ref.shape[0]
    step = pl.program_id(0)
    scale = jnp.asarray(HEAD_DIM ** (-0.5), LOW)

    @pl.when(step == 0)
    def _():
        lane = lax.broadcasted_iota(jnp.int32, (count, 128), 1)
        delta = jnp.zeros((count, 128), FULL)
        for pair in range(width // 128):
            columns = slice(128 * pair, 128 * pair + 128)
            q = q_ref[:, columns] * scale
            da = da_ref[:, columns]
            both = da.astype(FULL) * o_ref[:, columns].astype(FULL)
            for side in range(2):
                head = 2 * pair + side
                mask = (lane // HEAD_DIM) == side
                q_heads[head] = jnp.where(mask, q, jnp.zeros_like(q))
                da_heads[head] = jnp.where(mask, da, jnp.zeros_like(da))
                row = jnp.sum(jnp.where(mask, both, 0.0), axis=-1, keepdims=True)
                delta = jnp.where(lane == head, row, delta)
        delta_ref[...] = delta.T[:8]
        dq_total[...] = jnp.zeros_like(dq_total)

    lane = lax.broadcasted_iota(jnp.int32, (chunk, 128), 1)
    for pair in range(width // 128):
        columns = slice(128 * pair, 128 * pair + 128)
        k = k_ref[:, columns]
        v = v_ref[:, columns]
        scaled_k = k * scale
        dk = dv = None
        for side in range(2):
            head = 2 * pair + side
            q = q_heads[head]
            da = da_heads[head]
            probs = jnp.exp(product(k, q, ROW_BY_ROW) - lse_ref[head : head + 1, :])
            slope = probs * (product(v, da, ROW_BY_ROW) - delta_ref[head : head + 1, :])
            slope = slope.astype(LOW)
            dv_part = product(probs.astype(LOW), da, PLAIN)
            dk_part = product(slope, q, PLAIN)
            dv = dv_part if dv is None else dv + dv_part
            dk = dk_part if dk is None else dk + dk_part
            one_k = jnp.where((lane // HEAD_DIM) == side, scaled_k, jnp.zeros_like(k))
            dq_total[:, columns] += product(slope, one_k, COLUMN_BY_COLUMN)
        dk_ref[:, columns] = dk.astype(LOW)
        dv_ref[:, columns] = dv.astype(LOW)

    @pl.when(step == pl.num_programs(0) - 1)
    def _():
        dq_ref[...] = dq_total[...].astype(LOW)


def attention_backward(q, k, v, da, out, lse):
    count, width = q.shape
    chunk = row_chunk(count)
    heads = width // HEAD_DIM
    part = pl.BlockSpec((chunk, width), lambda i: (i, 0))
    whole = pl.BlockSpec((count, width), lambda i: (0, 0))
    grad = jax.ShapeDtypeStruct((count, width), LOW)
    return pl.pallas_call(
        attention_backward_kernel,
        grid=(count // chunk,),
        in_specs=[whole, part, part, whole, whole, pl.BlockSpec((8, count), lambda i: (0, 0))],
        out_specs=[whole, part, part],
        out_shape=[grad, grad, grad],
        scratch_shapes=[
            pltpu.VMEM((heads, count, 128), LOW),
            pltpu.VMEM((heads, count, 128), LOW),
            pltpu.VMEM((8, count), FULL),
            pltpu.VMEM((count, width), FULL),
        ],
        compiler_params=pltpu.CompilerParams(vmem_limit_bytes=56 << 20),
        name="attention_backward",
    )(q, k, v, da, out, lse)


def swap(value, axis, distance):
    size = lax.axis_size(axis)
    return lax.ppermute(value, axis, [(i, i ^ distance) for i in range(size)])


def gather_rows(rows_here):
    size = lax.axis_size("fsdp")
    if size != 4:
        return lax.all_gather(rows_here, "fsdp", axis=0, tiled=True)
    me = lax.axis_index("fsdp")
    count, width = rows_here.shape
    half = count // 2
    near = swap(rows_here, "fsdp", 1)
    side = swap(rows_here, "fsdp", 2)
    far_top = swap(side[:half], "fsdp", 1)
    far_low = swap(near[half:], "fsdp", 2)
    out = jnp.zeros((4 * count, width), rows_here.dtype)
    out = lax.dynamic_update_slice(out, rows_here, (me * count, 0))
    out = lax.dynamic_update_slice(out, near, ((me ^ 1) * count, 0))
    out = lax.dynamic_update_slice(out, side, ((me ^ 2) * count, 0))
    out = lax.dynamic_update_slice(out, far_top, ((me ^ 3) * count, 0))
    return lax.dynamic_update_slice(out, far_low, ((me ^ 3) * count + half, 0))


def sum_rows(left, right):
    size = lax.axis_size("fsdp")
    if size != 4:
        whole = product(left, right, COLUMN_BY_COLUMN).astype(LOW)
        return lax.psum_scatter(whole, "fsdp", scatter_dimension=0, tiled=True).astype(FULL)
    me = lax.axis_index("fsdp")
    count = left.shape[1] // 4
    half = count // 2

    def block(distance):
        piece = lax.dynamic_slice_in_dim(left, (me ^ distance) * count, count, 1)
        return product(piece, right, COLUMN_BY_COLUMN)

    far = block(3).astype(LOW)
    far_top = swap(far[:half], "fsdp", 1)
    far_low = swap(far[half:], "fsdp", 2)
    near = block(1)
    side = block(2)
    near_top = swap(near[:half].astype(LOW), "fsdp", 1)
    side_low = swap(side[half:].astype(LOW), "fsdp", 2)
    near_low = swap((near[half:] + far_low.astype(FULL)).astype(LOW), "fsdp", 1)
    side_top = swap((side[:half] + far_top.astype(FULL)).astype(LOW), "fsdp", 2)
    own = block(0)
    top = own[:half] + (near_top.astype(FULL) + side_top.astype(FULL))
    low = own[half:] + (near_low.astype(FULL) + side_low.astype(FULL))
    return jnp.concatenate([top, low], axis=0)


def in_order(bit, mine, other):
    return jnp.where(
        bit == 0,
        jnp.concatenate([mine, other], axis=0),
        jnp.concatenate([other, mine], axis=0),
    )


def sum_blocks(value):
    me = lax.axis_index("ctx")
    low_bit = me & 1
    high_bit = me >> 1
    half = value.shape[0] // 2
    keep = lax.dynamic_slice_in_dim(value, low_bit * half, half, 0)
    send = lax.dynamic_slice_in_dim(value, (1 - low_bit) * half, half, 0).astype(LOW)
    value = keep + swap(send, "ctx", 1).astype(FULL)
    half = half // 2
    keep = lax.dynamic_slice_in_dim(value, high_bit * half, half, 0)
    send = lax.dynamic_slice_in_dim(value, (1 - high_bit) * half, half, 0).astype(LOW)
    value = (keep + swap(send, "ctx", 2).astype(FULL)).astype(LOW)
    value = in_order(high_bit, value, swap(value, "ctx", 2))
    value = in_order(low_bit, value, swap(value, "ctx", 1))
    return value.astype(FULL)


def sum_pairwise(value, axis):
    near = value + swap(value, axis, 1)
    far = swap(value, axis, 2) + swap(value, axis, 3)
    return near + far


def sum_cores(part):
    part = part.astype(LOW)
    return part.astype(FULL) + swap(part, "tp", 1).astype(FULL)


def per_device(
    tokens,
    clip_mask,
    cotangent,
    first_gain,
    first_shift,
    joint_weight,
    joint_bias,
    mixer_weight,
    mixer_bias,
    second_gain,
    second_shift,
    expand_weight,
    expand_bias,
    reduce_weight,
    reduce_bias,
):
    clips_here, rows_here, width = tokens.shape
    if lax.axis_size("ctx") != 4 or lax.axis_size("tp") != 2 or clips_here != 2:
        raise ValueError("mesh")
    shard = lax.axis_index("fsdp")
    block = lax.axis_index("ctx")
    core = lax.axis_index("tp")
    clip_at = block >> 1
    part_at = block & 1
    width_half = width // 2
    features = joint_weight.shape[2]
    part_width = features // 2
    tokens_here = clips_here * rows_here

    inputs = tokens.astype(FULL)
    first_scaled, first_inverse = normalize(inputs)
    first_normed = (first_scaled * first_gain + first_shift).astype(LOW)
    mine = lax.dynamic_slice_in_dim(first_normed, core * width_half, width_half, 2)
    other_side = lax.dynamic_slice_in_dim(first_normed, (1 - core) * width_half, width_half, 2)
    own_clip = lax.dynamic_index_in_dim(mine, clip_at, 0, False)
    other_clip = lax.dynamic_index_in_dim(mine, 1 - clip_at, 0, False)
    near_rows = swap(own_clip, "ctx", 1)
    across_rows = swap(other_clip, "ctx", 2)
    far_rows = swap(other_clip, "ctx", 3)
    normed_mine = jnp.concatenate([own_clip, near_rows, across_rows, far_rows], axis=0)
    normed_other = jnp.concatenate(
        [
            lax.dynamic_index_in_dim(other_side, clip_at, 0, False),
            swap(near_rows, "tp", 1),
            swap(across_rows, "tp", 1),
            swap(far_rows, "tp", 1),
        ],
        axis=0,
    )
    normed_clip = jnp.concatenate([normed_mine, normed_other], axis=1)

    joint_part = lax.dynamic_slice_in_dim(joint_weight, part_at * part_width, part_width, 2)
    joint_part = jnp.concatenate([joint_part[:, kind] for kind in range(3)], axis=1)
    joint_rows = gather_rows(joint_part)
    joint_full = jnp.concatenate(
        [
            lax.dynamic_slice_in_dim(joint_rows, core * width_half, width_half, 0),
            lax.dynamic_slice_in_dim(joint_rows, (1 - core) * width_half, width_half, 0),
        ],
        axis=0,
    )
    mixer_full = gather_rows(mixer_weight)
    expand_full = gather_rows(expand_weight)
    reduce_full = gather_rows(reduce_weight)

    joint_out = product(normed_clip, joint_full, PLAIN)
    bias_part = lax.dynamic_slice_in_dim(joint_bias, part_at * part_width, part_width, 1)
    queries = (joint_out[:, :part_width] + bias_part[0]).astype(LOW)
    keys = joint_out[:, part_width : 2 * part_width].astype(LOW)
    values = (joint_out[:, 2 * part_width :] + bias_part[1]).astype(LOW)
    attended, log_total = attention_forward(queries, keys, values)

    attended_blocks = attended.reshape(4, rows_here, part_width)
    arrived = [attended_blocks[0]] + [swap(attended_blocks[d], "ctx", d) for d in (1, 2, 3)]

    def swapped_if(bit, pair):
        return [jnp.where(bit == 0, pair[0], pair[1]), jnp.where(bit == 0, pair[1], pair[0])]

    first_pair = swapped_if(part_at, arrived[:2])
    second_pair = swapped_if(part_at, arrived[2:])
    own_joined = jnp.concatenate(first_pair, axis=1)
    other_joined = jnp.concatenate(second_pair, axis=1)
    mixed_in = jnp.concatenate(swapped_if(clip_at, [own_joined, other_joined]), axis=0)

    flat_inputs = inputs.reshape(tokens_here, width)
    valid = jnp.broadcast_to(
        clip_mask.astype(FULL)[:, None, None], (clips_here, rows_here, 1)
    ).reshape(tokens_here, 1)
    mixer_out = sum_cores(product(mixed_in, mixer_full, ROW_BY_ROW)) + mixer_bias
    second_scaled, second_inverse = normalize(flat_inputs + mixer_out)
    second_normed = (second_scaled * second_gain + second_shift).astype(LOW)
    expanded = product(second_normed, expand_full, PLAIN) + expand_bias
    activated, gelu_back = jax.vjp(partial(jax.nn.gelu, approximate=False), expanded)
    activated_low = activated.astype(LOW)
    reduce_out = sum_cores(product(activated_low, reduce_full, ROW_BY_ROW)) + reduce_bias
    result = (flat_inputs + valid * (mixer_out + reduce_out)).astype(LOW)

    outer = cotangent.astype(FULL).reshape(tokens_here, width)
    branch_slope = outer * valid
    reduce_slope = branch_slope.astype(LOW)
    reduce_bias_grad = jnp.sum(reduce_slope.astype(FULL), axis=0)
    activated_slope = product(reduce_slope, reduce_full, PLAIN)
    expand_slope = gelu_back(activated_slope)[0].astype(LOW)
    expand_bias_grad = jnp.sum(expand_slope.astype(FULL), axis=0)
    second_slope = sum_cores(product(expand_slope, expand_full, ROW_BY_ROW))
    second_gain_grad = jnp.sum(second_slope * second_scaled, axis=0)
    second_shift_grad = jnp.sum(second_slope, axis=0)
    first_sum_back = norm_back(second_slope, second_gain, second_scaled, second_inverse)
    mixer_slope = (branch_slope + first_sum_back).astype(LOW)
    mixer_bias_grad = jnp.sum(mixer_slope.astype(FULL), axis=0)
    attended_slope = product(mixer_slope, mixer_full, PLAIN).astype(LOW)

    slope_clips = swapped_if(clip_at, [attended_slope[:rows_here], attended_slope[rows_here:]])
    leaving = []
    for piece in slope_clips:
        leaving += swapped_if(part_at, [piece[:, :part_width], piece[:, part_width:]])
    slope_clip = jnp.concatenate(
        [leaving[0]] + [swap(leaving[d], "ctx", d) for d in (1, 2, 3)], axis=0
    )

    reduce_grad = sum_blocks(sum_rows(reduce_slope, activated_low))
    expand_grad = sum_blocks(sum_rows(second_normed, expand_slope))
    mixer_grad = sum_blocks(sum_rows(mixer_slope, mixed_in))

    joint_slope = jnp.concatenate(
        attention_backward(queries, keys, values, slope_clip, attended, log_total), axis=1
    )
    slope_sums = jnp.sum(joint_slope.astype(FULL), axis=0)
    bias_sums = jnp.stack([slope_sums[:part_width], slope_sums[2 * part_width :]])
    joint_bias_grad = lax.dynamic_update_slice(
        jnp.zeros((2, features), FULL), bias_sums, (0, part_at * part_width)
    )

    first_part = product(joint_slope, joint_full, ROW_BY_ROW)
    first_half = first_part[:, :width_half].astype(LOW).astype(FULL) + swap(
        first_part[:, width_half:].astype(LOW), "tp", 1
    ).astype(FULL)
    pieces = first_half.astype(LOW).reshape(4, rows_here, width_half)
    own_half = pieces[0].astype(FULL) + swap(pieces[1], "ctx", 1).astype(FULL)
    other_half = swap(pieces[2], "ctx", 2).astype(FULL) + swap(pieces[3], "ctx", 3).astype(FULL)
    slope_half = jnp.concatenate(swapped_if(clip_at, [own_half, other_half]), axis=0).astype(LOW)
    slope_other = swap(slope_half, "tp", 1)
    first_slope = jnp.concatenate(swapped_if(core, [slope_half, slope_other]), axis=1).astype(FULL)

    flat_scaled = first_scaled.reshape(tokens_here, width)
    flat_inverse = first_inverse.reshape(tokens_here, 1)
    first_gain_grad = jnp.sum(first_slope * flat_scaled, axis=0)
    first_shift_grad = jnp.sum(first_slope, axis=0)
    tokens_grad = (
        outer + first_sum_back + norm_back(first_slope, first_gain, flat_scaled, flat_inverse)
    )

    normed_columns = jnp.concatenate(
        swapped_if(core, [normed_mine, normed_other]), axis=1
    )
    joint_sum = sum_rows(normed_columns, joint_slope).astype(LOW)
    joint_sum = (
        joint_sum.astype(FULL) + swap(joint_sum, "ctx", 2).astype(FULL)
    ).astype(LOW)
    joint_parts = swapped_if(part_at, [joint_sum, swap(joint_sum, "ctx", 1)])
    joint_grad = jnp.concatenate(
        [piece.reshape(-1, 3, part_width) for piece in joint_parts], axis=2
    ).astype(FULL)

    vectors = [
        first_gain_grad,
        first_shift_grad,
        joint_bias_grad[0],
        joint_bias_grad[1],
        mixer_bias_grad,
        second_gain_grad,
        second_shift_grad,
        expand_bias_grad,
        reduce_bias_grad,
    ]
    packed = sum_pairwise(jnp.concatenate(vectors).reshape(-1, 128), "ctx")
    if lax.axis_size("fsdp") == 4:
        packed = sum_pairwise(packed, "fsdp")
    else:
        packed = lax.psum(packed, "fsdp")
    packed = packed.reshape(-1)
    shares = []
    start = 0
    for vector in vectors:
        share = vector.shape[0] // lax.axis_size("fsdp")
        shares.append(lax.dynamic_slice_in_dim(packed, start + shard * share, share, 0))
        start += vector.shape[0]

    shape = (clips_here, rows_here, width)
    return (
        result.reshape(shape),
        tokens_grad.reshape(shape),
        shares[0],
        shares[1],
        joint_grad,
        jnp.stack([shares[2], shares[3]]),
        mixer_grad,
        shares[4],
        shares[5],
        shares[6],
        expand_grad,
        shares[7],
        reduce_grad,
        shares[8],
    )


def solution(mesh):
    return jax.shard_map(
        per_device,
        mesh=mesh,
        in_specs=(
            P("fsdp", "ctx", None),
            P("fsdp"),
            P("fsdp", "ctx", None),
            P(),
            P(),
            P("fsdp", None, "tp"),
            P(None, "tp"),
            P("fsdp", "tp"),
            P(),
            P(),
            P(),
            P("fsdp", "tp"),
            P("tp"),
            P("fsdp", "tp"),
            P(),
        ),
        out_specs=(
            P("fsdp", "ctx", None),
            P("fsdp", "ctx", None),
            P("fsdp"),
            P("fsdp"),
            P("fsdp", None, "tp"),
            P(None, ("tp", "fsdp")),
            P("fsdp", "tp"),
            P("fsdp"),
            P("fsdp"),
            P("fsdp"),
            P("fsdp", "tp"),
            P(("tp", "fsdp")),
            P("fsdp", "tp"),
            P("fsdp"),
        ),
        check_vma=False,
    )
```

time: 987 us -> 534 us (0.54)
  waiting for transfers between devices: 620 us -> 216 us
  matrix products: 185 us -> 64.5 us
  starting transfers between devices: 1.6 us -> 75.9 us
  Pallas kernels: 0 us -> 57.7 us
  blocking collectives: 29 us -> 0 us
  other arithmetic: 77.8 us -> 49.1 us
  between operations: 16.1 us -> 2.88 us
    ppermute x0 -> x80, waiting for transfers between devices: none -> 216 us  [swap(): return lax.ppermute(value, axis, [(i, i ^ distance) for i in range(size)])]
    all_gather x6 -> x0, waiting for transfers between devices: 210 us -> none  [the longest x1 58.9 us: per_device(): lax.all_gather(keys_local, 'ctx', axis=1, tiled=True)]
    reduce_scatter x4 -> x0, waiting for transfers between devices: 159 us -> none  [the longest x1 56 us: per_device(): lax.psum_scatter(reduce_grad.astype(jnp.bfloat16), 'fsdp', scatter_dimens...]
    psum x4 -> x0, waiting for transfers between devices: 146 us -> none  [the longest x1 80.2 us: per_device(): lax.psum(joint_rows.astype(jnp.bfloat16), 'ctx').astype(jnp.float32)]
    dot_general x18 -> x24, matrix products: 185 us -> 64.5 us  [product(): return lax.dot_general(left, right, dims, preferred_element_type=FULL)]
    unnamed x18 -> x0, waiting for transfers between devices: 106 us -> none
    ppermute x0 -> x80, starting transfers between devices: none -> 75.9 us  [swap(): return lax.ppermute(value, axis, [(i, i ^ distance) for i in range(size)])]
    pallas_call x0 -> x2, Pallas kernels: none -> 57.7 us  [the longest x1 37.7 us: attention_backward(): pl.pallas_call(attention_backward_kernel, grid=(count // chunk,), in_spec...]
  transfers between devices with their start and end apart: 16 -> 80, of which waited for: 16 -> 35; matrix products, arithmetic and copies ran while one was open for 19% -> 21% of each run, Pallas kernels for 0% -> 11%
where the time goes in v1:
time: 534 us; the launch traced here: 526 us
  waiting for transfers between devices  216 us (40%)
  starting transfers between devices  75.9 us (14%)
  matrix products  64.5 us (12%)
  local copies, waits for them, and re-layouts  60.1 us (11%)
  Pallas kernels  57.7 us (11%)
  other arithmetic  49.1 us (9%)
    ppermute x80, waiting for transfers between devices, swap(): return lax.ppermute(value, axis, [(i, i ^ distance) for i in range(size)])  216 us
    ppermute x80, starting transfers between devices, swap(): return lax.ppermute(value, axis, [(i, i ^ distance) for i in range(size)])  75.9 us
    dot_general x24, matrix products, product(): return lax.dot_general(left, right, dims, preferred_element_type=FULL)  64.5 us
    pallas_call x1, Pallas kernels, attention_backward(): pl.pallas_call(attention_backward_kernel, grid=(count // chunk,), in_spec...  37.7 us
    pallas_call x1, Pallas kernels, attention_forward(): pl.pallas_call(attention_forward_kernel, grid=(steps,), in_specs=[part, w...  20 us
    unnamed x157, local copies, waits for them, and re-layouts  13.5 us
  transfers between devices with their start and end apart: 80, of which 35 were waited for; matrix products, arithmetic and copies ran while one was open for 21% of the time, Pallas kernels for 11%

profile of v1, /device:TPU:0, one launch (start us, length us, event | category | flops | bytes accessed | tf_op | source)
XLA Modules:
  0.0 526.4 jit_solution(10859293169441302918)
XLA Ops:
  12.1 4.0 collective-permute-start.2
  42.8 10.0 %collective-permute-done.1 = bf16[392,512]{1,0:T(8,128)(2,1)S(1)} collective-permute-done((bf16[392,512]{1,0:T(8,128)(2,1)}, bf16[392,512]{1,0:T(8,128)(2,1)S(1)}, u32[]{:S(2)}, u32[]{:S(2)}) %collective-permute-start.1) | collective-permute-done | bytes 401440 | tf_op jit(solution)/shard_map/ppermute | solution.py:173
  62.4 3.7 fusion.14
  66.6 20.0 %attention_forward.1 = (bf16[1568,256]{1,0:T(8,128)(2,1)S(1)}, f32[7,8,224]{2,1,0:T(8,128)S(1)}) custom-call(bf16[1568,256]{1,0:T(8,128)(2,1)S(1)} %get-tuple-element.52.q_ref, bf16[1568,256]{1,0:T(8,128)(2,1)S(1)} %slice.416.k_ref, bf16[1568,256]{1,0:T(8,128)(2,1)S(1)} %get-tuple-element.51.v_ref), custom_call_target="tpu_custom_call" | custom-call | tf_op jit(solution)/shard_map/attention_forward/pallas_call | solution.py:76
  86.8 3.1 broadcast_select_fusion
  96.7 7.0 %collective-permute-done.23 = bf16[256,2048]{1,0:T(8,128)(2,1)S(1)} collective-permute-done((bf16[256,2048]{1,0:T(8,128)(2,1)}, bf16[256,2048]{1,0:T(8,128)(2,1)S(1)}, u32[]{:S(2)}, u32[]{:S(2)}) %collective-permute-start.23) | collective-permute-done | bytes 1048608 | tf_op jit(solution)/shard_map/ppermute | solution.py:173
  119.5 8.5 %collective-permute-done.24 = bf16[128,2048]{1,0:T(8,128)(2,1)S(1)} collective-permute-done((bf16[128,2048]{1,0:T(8,128)(2,1)S(1)}, bf16[128,2048]{1,0:T(8,128)(2,1)S(1)}, u32[]{:S(2)}, u32[]{:S(2)}) %collective-permute-start.24) | collective-permute-done | bytes 524320 | tf_op jit(solution)/shard_map/ppermute | solution.py:173
  135.4 5.4 %fusion.130 = f32[784,2048]{1,0:T(8,128)S(1)} fusion(bf16[784,1024]{1,0:T(8,128)(2,1)S(1)} %add_convert_fusion.3, bf16[1024,2048]{1,0:T(8,128)(2,1)} %constant_dynamic-update-slice_fusion.6), kind=kOutput, calls=%fused_computation.320 | convolution fusion | flops 3288334336 | bytes 12222464 | tf_op jit(solution)/shard_map/dot_general | solution.py:21
  140.9 20.7 %convert_reduce_fusion = (f32[2048]{0:T(1024)S(1)}, bf16[784,2048]{1,0:T(8,128)(2,1)}, f32[784,2048]{1,0:T(8,128)S(1)}) fusion(f32[784,2048]{1,0:T(8,128)S(1)} %fusion.130, f32[2048]{0:T(1024)S(1)} %copy-done.66, bf16[784,1024]{1,0:T(8,128)(2,1)S(1)} %copy-done.24, bf16[1024,2048]{1,0:T(8,128)(2,1)} %constant_dynamic-update-slice_fusion.1), kind=kOutput, calls=%fused_computation.2 | convolution fusion | flops 3408754688 | bytes 21872640 | tf_op jit(solution)/shard_map/dot_general | solution.py:21
  163.3 5.8 %convolution_convert_fusion.5 = bf16[784,1024]{1,0:T(8,128)(2,1)S(1)} fusion(bf16[784,2048]{1,0:T(8,128)(2,1)S(1)} %multiply_convert_fusion, bf16[1024,2048]{1,0:T(8,128)(2,1)} %constant_dynamic-update-slice_fusion.1), kind=kOutput, calls=%fused_computation.96 | convolution fusion | flops 3289137152 | bytes 9011200 | tf_op jit(solution)/shard_map/dot_general | solution.py:21
  171.0 5.8 %convolution_convert_fusion.4 = bf16[784,1024]{1,0:T(8,128)(2,1)S(1)} fusion(bf16[784,2048]{1,0:T(8,128)(2,1)S(1)} %copy-done.72, bf16[1024,2048]{1,0:T(8,128)(2,1)} %constant_dynamic-update-slice_fusion.6), kind=kOutput, calls=%fused_computation.95 | convolution fusion | flops 3289137152 | bytes 9011200 | tf_op jit(solution)/shard_map/dot_general | solution.py:21
  192.0 7.7 %collective-permute-done.71 = bf16[128,2048]{1,0:T(8,128)(2,1)S(1)} collective-permute-done((bf16[128,2048]{1,0:T(8,128)(2,1)S(1)}, bf16[128,2048]{1,0:T(8,128)(2,1)S(1)}, u32[]{:S(2)}, u32[]{:S(2)}) %collective-permute-start.71) | collective-permute-done | bytes 524320 | tf_op jit(solution)/shard_map/ppermute | solution.py:173
  201.5 9.4 %collective-permute-done.61 = bf16[128,2048]{1,0:T(8,128)(2,1)S(1)} collective-permute-done((bf16[128,2048]{1,0:T(8,128)(2,1)S(1)}, bf16[128,2048]{1,0:T(8,128)(2,1)S(1)}, u32[]{:S(2)}, u32[]{:S(2)}) %collective-permute-start.61) | collective-permute-done | bytes 524320 | tf_op jit(solution)/shard_map/ppermute | solution.py:173
  211.9 9.1 %collective-permute-done.75 = bf16[128,2048]{1,0:T(8,128)(2,1)S(1)} collective-permute-done((bf16[128,2048]{1,0:T(8,128)(2,1)S(1)}, bf16[128,2048]{1,0:T(8,128)(2,1)S(1)}, u32[]{:S(2)}, u32[]{:S(2)}) %collective-permute-start.75) | collective-permute-done | bytes 524320 | tf_op jit(solution)/shard_map/ppermute | solution.py:173
  222.8 9.4 %collective-permute-done.72 = bf16[128,2048]{1,0:T(8,128)(2,1)S(1)} collective-permute-done((bf16[128,2048]{1,0:T(8,128)(2,1)S(1)}, bf16[128,2048]{1,0:T(8,128)(2,1)S(1)}, u32[]{:S(2)}, u32[]{:S(2)}) %collective-permute-start.72) | collective-permute-done | bytes 524320 | tf_op jit(solution)/shard_map/ppermute | solution.py:173
  234.8 8.7 %collective-permute-done.65 = bf16[128,2048]{1,0:T(8,128)(2,1)S(1)} collective-permute-done((bf16[128,2048]{1,0:T(8,128)(2,1)S(1)}, bf16[128,2048]{1,0:T(8,128)(2,1)S(1)}, u32[]{:S(2)}, u32[]{:S(2)}) %collective-permute-start.65) | collective-permute-done | bytes 524320 | tf_op jit(solution)/shard_map/ppermute | solution.py:173
  244.7 8.4 %collective-permute-done.62 = bf16[128,2048]{1,0:T(8,128)(2,1)S(1)} collective-permute-done((bf16[128,2048]{1,0:T(8,128)(2,1)S(1)}, bf16[128,2048]{1,0:T(8,128)(2,1)S(1)}, u32[]{:S(2)}, u32[]{:S(2)}) %collective-permute-start.62) | collective-permute-done | bytes 524320 | tf_op jit(solution)/shard_map/ppermute | solution.py:173
  254.4 5.2 collective-permute-done.76
  260.5 14.1 %collective-permute-done.66 = bf16[128,2048]{1,0:T(8,128)(2,1)S(1)} collective-permute-done((bf16[128,2048]{1,0:T(8,128)(2,1)S(1)}, bf16[128,2048]{1,0:T(8,128)(2,1)S(1)}, u32[]{:S(2)}, u32[]{:S(2)}) %collective-permute-start.66) | collective-permute-done | bytes 524320 | tf_op jit(solution)/shard_map/ppermute | solution.py:173
  278.5 4.6 convert_reduce_fusion.4
  297.0 10.3 %collective-permute-done.29 = bf16[392,256]{1,0:T(8,128)(2,1)S(1)} collective-permute-done((bf16[392,256]{1,0:T(8,128)(2,1)S(1)}, bf16[392,256]{1,0:T(8,128)(2,1)S(1)}, u32[]{:S(2)}, u32[]{:S(2)}) %collective-permute-start.29) | collective-permute-done | bytes 200736 | tf_op jit(solution)/shard_map/ppermute | solution.py:173
  310.0 37.7 %attention_backward.1 = (bf16[1568,256]{1,0:T(8,128)(2,1)}, bf16[1568,256]{1,0:T(8,128)(2,1)}, bf16[1568,256]{1,0:T(8,128)(2,1)}) custom-call(bf16[1568,256]{1,0:T(8,128)(2,1)} %copy-done.2, bf16[1568,256]{1,0:T(8,128)(2,1)} %copy-done, bf16[1568,256]{1,0:T(8,128)(2,1)} %copy-done.1, bf16[1568,256]{1,0:T(8,128)(2,1)} %pad_maximum_fusion.8.da_ref, ...), custom_call_target="tpu_custom_call" | custom-call | tf_op jit(solution)/shard_map/attention_backward/pallas_call | solution.py:154
  355.4 4.1 convolution_convert_fusion
  382.4 13.5 %collective-permute-done.78 = bf16[64,2048]{1,0:T(8,128)(2,1)S(1)} collective-permute-done((bf16[64,2048]{1,0:T(8,128)(2,1)S(1)}, bf16[64,2048]{1,0:T(8,128)(2,1)S(1)}, u32[]{:S(2)}, u32[]{:S(2)}) %collective-permute-start.78) | collective-permute-done | bytes 262176 | tf_op jit(solution)/shard_map/ppermute | solution.py:173
  409.3 27.7 %collective-permute-done.68 = bf16[64,2048]{1,0:T(8,128)(2,1)S(1)} collective-permute-done((bf16[64,2048]{1,0:T(8,128)(2,1)S(1)}, bf16[64,2048]{1,0:T(8,128)(2,1)S(1)}, u32[]{:S(2)}, u32[]{:S(2)}) %collective-permute-start.68) | collective-permute-done | bytes 262176 | tf_op jit(solution)/shard_map/ppermute | solution.py:173
  440.0 5.5 %collective-permute-done.48 = bf16[256,768]{1,0:T(8,128)(2,1)S(1)} collective-permute-done((bf16[256,768]{1,0:T(8,128)(2,1)S(1)}, bf16[256,768]{1,0:T(8,128)(2,1)S(1)}, u32[]{:S(2)}, u32[]{:S(2)}) %collective-permute-start.48) | collective-permute-done | bytes 393248 | tf_op jit(solution)/shard_map/ppermute | solution.py:173
  445.6 8.4 %collective-permute-done.33 = bf16[392,512]{1,0:T(8,128)(2,1)S(1)} collective-permute-done((bf16[392,512]{1,0:T(8,128)(2,1)S(1)}, bf16[392,512]{1,0:T(8,128)(2,1)S(1)}, u32[]{:S(2)}, u32[]{:S(2)}) %collective-permute-start.33) | collective-permute-done | bytes 401440 | tf_op jit(solution)/shard_map/ppermute | solution.py:173
  454.0 7.8 %collective-permute-done.32 = bf16[392,512]{1,0:T(8,128)(2,1)S(1)} collective-permute-done((bf16[392,512]{1,0:T(8,128)(2,1)S(1)}, bf16[392,512]{1,0:T(8,128)(2,1)S(1)}, u32[]{:S(2)}, u32[]{:S(2)}) %collective-permute-start.32) | collective-permute-done | bytes 401440 | tf_op jit(solution)/shard_map/ppermute | solution.py:173
  463.8 9.3 %collective-permute-done.79 = bf16[128,2048]{1,0:T(8,128)(2,1)S(1)} collective-permute-done((bf16[128,2048]{1,0:T(8,128)(2,1)S(1)}, bf16[128,2048]{1,0:T(8,128)(2,1)S(1)}, u32[]{:S(2)}, u32[]{:S(2)}) %collective-permute-start.79) | collective-permute-done | bytes 524320 | tf_op jit(solution)/shard_map/ppermute | solution.py:173
  474.7 9.7 %collective-permute-done.69 = bf16[128,2048]{1,0:T(8,128)(2,1)S(1)} collective-permute-done((bf16[128,2048]{1,0:T(8,128)(2,1)S(1)}, bf16[128,2048]{1,0:T(8,128)(2,1)S(1)}, u32[]{:S(2)}, u32[]{:S(2)}) %collective-permute-start.69) | collective-permute-done | bytes 524320 | tf_op jit(solution)/shard_map/ppermute | solution.py:173
  485.9 6.8 %collective-permute-done.49 = bf16[256,768]{1,0:T(8,128)(2,1)S(1)} collective-permute-done((bf16[256,768]{1,0:T(8,128)(2,1)S(1)}, bf16[256,768]{1,0:T(8,128)(2,1)S(1)}, u32[]{:S(2)}, u32[]{:S(2)}) %collective-permute-start.49) | collective-permute-done | bytes 393248 | tf_op jit(solution)/shard_map/ppermute | solution.py:173
  517.8 6.1 %fusion.10 = f32[784,1024]{1,0:T(8,128)} fusion(f32[2,392,1024]{2,1,0:T(8,128)} %get-tuple-element.61, bf16[2,392,1024]{2,1,0:T(8,128)(2,1)} %param.17, f32[784]{0:T(1024)S(1)} %div.34, f32[784]{0:T(1024)S(1)} %broadcast_multiply_fusion, f32[1024]{0:T(1024)S(1)} %copy-done.53, f32[784]{0:T(1024)S(1)} %copy-done.63, bf16[784,512]{1,0:T(8,128)(2,1)} %copy-done.17, ...), kind=kLoop, calls=%fused_computation.36 | loop fusion | flops 17661952 | bytes 16086464 | tf_op jit(solution)/shard_map/add | solution.py:409
  (454 shorter events, 206.2 us)
Async XLA Ops:
  0.7 28.3 %collective-permute-start.14 = (bf16[256,512]{1,0:T(8,128)(2,1)}, bf16[256,512]{1,0:T(8,128)(2,1)S(1)}, u32[]{:S(2)}, u32[]{:S(2)}) collective-permute-start(bf16[256,512]{1,0:T(8,128)(2,1)} %param.22), channel_id=1, source_target_pairs={{0,16},{8,24},{16,0},{24,8},{1,17},{9,25},{17,1},{25,9},{2,18},{10... | collective-permute-start | bytes 786440 | tf_op jit(solution)/shard_map/ppermute | solution.py:173
  3.7 26.9 %collective-permute-start.13 = (bf16[256,512]{1,0:T(8,128)(2,1)}, bf16[256,512]{1,0:T(8,128)(2,1)}, u32[]{:S(2)}, u32[]{:S(2)}) collective-permute-start(bf16[256,512]{1,0:T(8,128)(2,1)} %param.22), channel_id=1, source_target_pairs={{0,8},{8,0},{16,24},{24,16},{1,9},{9,1},{17,25},{25,17},{2,10},{10... | collective-permute-start | bytes 786440 | tf_op jit(solution)/shard_map/ppermute | solution.py:173
  8.4 28.2 %collective-permute-start.6 = (bf16[256,768]{1,0:T(8,128)(2,1)}, bf16[256,768]{1,0:T(8,128)(2,1)}, u32[]{:S(2)}, u32[]{:S(2)}) collective-permute-start(bf16[256,768]{1,0:T(8,128)(2,1)} %get-tuple-element.101), channel_id=1, source_target_pairs={{0,8},{8,0},{16,24},{24,16},{1,9},{9,1},{17,25},{25,17},{2,10},{10... | collective-permute-start | bytes 1179656 | tf_op jit(solution)/shard_map/ppermute | solution.py:173
  9.0 30.4 %collective-permute-start.7 = (bf16[256,768]{1,0:T(8,128)(2,1)}, bf16[256,768]{1,0:T(8,128)(2,1)}, u32[]{:S(2)}, u32[]{:S(2)}) collective-permute-start(bf16[256,768]{1,0:T(8,128)(2,1)} %get-tuple-element.101), channel_id=1, source_target_pairs={{0,16},{8,24},{16,0},{24,8},{1,17},{9,25},{17,1},{25,9},{2,18},{10... | collective-permute-start | bytes 1179656 | tf_op jit(solution)/shard_map/ppermute | solution.py:173
  12.1 30.7 %collective-permute-start.2 = (bf16[392,512]{1,0:T(8,128)(2,1)}, bf16[392,512]{1,0:T(8,128)(2,1)}, u32[]{:S(2)}, u32[]{:S(2)}) collective-permute-start(bf16[392,512]{1,0:T(8,128)(2,1)} %get-tuple-element.68), channel_id=1, source_target_pairs={{0,6},{2,4},{4,2},{6,0},{1,7},{3,5},{5,3},{7,1},{8,14},{10,12},{12... | collective-permute-start | bytes 1204232 | tf_op jit(solution)/shard_map/ppermute | solution.py:173
  55.4 38.1 %collective-permute-start.19 = (bf16[256,2048]{1,0:T(8,128)(2,1)}, bf16[256,2048]{1,0:T(8,128)(2,1)S(1)}, u32[]{:S(2)}, u32[]{:S(2)}) collective-permute-start(bf16[256,2048]{1,0:T(8,128)(2,1)} %param.26), channel_id=1, source_target_pairs={{0,16},{8,24},{16,0},{24,8},{1,17},{9,25},{17,1},{25,9},{2,18},{10... | collective-permute-start | bytes 3145736 | tf_op jit(solution)/shard_map/ppermute | solution.py:173
  57.5 37.5 %collective-permute-start.18 = (bf16[256,2048]{1,0:T(8,128)(2,1)}, bf16[256,2048]{1,0:T(8,128)(2,1)}, u32[]{:S(2)}, u32[]{:S(2)}) collective-permute-start(bf16[256,2048]{1,0:T(8,128)(2,1)} %param.26), channel_id=1, source_target_pairs={{0,8},{8,0},{16,24},{24,16},{1,9},{9,1},{17,25},{25,17},{2,10},{10... | collective-permute-start | bytes 3145736 | tf_op jit(solution)/shard_map/ppermute | solution.py:173
  60.4 43.3 %collective-permute-start.23 = (bf16[256,2048]{1,0:T(8,128)(2,1)}, bf16[256,2048]{1,0:T(8,128)(2,1)S(1)}, u32[]{:S(2)}, u32[]{:S(2)}) collective-permute-start(bf16[256,2048]{1,0:T(8,128)(2,1)} %param.28), channel_id=1, source_target_pairs={{0,16},{8,24},{16,0},{24,8},{1,17},{9,25},{17,1},{25,9},{2,18},{10... | collective-permute-start | bytes 3145736 | tf_op jit(solution)/shard_map/ppermute | solution.py:173
  60.9 45.4 %collective-permute-start.22 = (bf16[256,2048]{1,0:T(8,128)(2,1)}, bf16[256,2048]{1,0:T(8,128)(2,1)}, u32[]{:S(2)}, u32[]{:S(2)}) collective-permute-start(bf16[256,2048]{1,0:T(8,128)(2,1)} %param.28), channel_id=1, source_target_pairs={{0,8},{8,0},{16,24},{24,16},{1,9},{9,1},{17,25},{25,17},{2,10},{10... | collective-permute-start | bytes 3145736 | tf_op jit(solution)/shard_map/ppermute | solution.py:173
  188.1 23.6 %collective-permute-start.63 = (bf16[128,2048]{1,0:T(8,128)(2,1)S(1)}, bf16[128,2048]{1,0:T(8,128)(2,1)S(1)}, u32[]{:S(2)}, u32[]{:S(2)}) collective-permute-start(bf16[128,2048]{1,0:T(8,128)(2,1)S(1)} %get-tuple-element.74), channel_id=1, source_target_pairs={{0,16},{8,24},{16,0},{24,8},{1,17},{9,25},{17,1},{25,9},{2,18},{10... | collective-permute-start | bytes 1572872 | tf_op jit(solution)/shard_map/ppermute | solution.py:173
  190.5 30.5 %collective-permute-start.75 = (bf16[128,2048]{1,0:T(8,128)(2,1)S(1)}, bf16[128,2048]{1,0:T(8,128)(2,1)S(1)}, u32[]{:S(2)}, u32[]{:S(2)}) collective-permute-start(bf16[128,2048]{1,0:T(8,128)(2,1)S(1)} %slice.417), channel_id=1, source_target_pairs={{0,16},{8,24},{16,0},{24,8},{1,17},{9,25},{17,1},{25,9},{2,18},{10... | collective-permute-start | bytes 1572872 | tf_op jit(solution)/shard_map/ppermute | solution.py:173
  200.5 31.8 %collective-permute-start.72 = (bf16[128,2048]{1,0:T(8,128)(2,1)S(1)}, bf16[128,2048]{1,0:T(8,128)(2,1)S(1)}, u32[]{:S(2)}, u32[]{:S(2)}) collective-permute-start(bf16[128,2048]{1,0:T(8,128)(2,1)S(1)} %fusion.49), channel_id=1, source_target_pairs={{0,16},{8,24},{16,0},{24,8},{1,17},{9,25},{17,1},{25,9},{2,18},{10... | collective-permute-start | bytes 1572872 | tf_op jit(solution)/shard_map/ppermute | solution.py:173
  211.7 65.2 %collective-permute-start.26 = (bf16[784,1024]{1,0:T(8,128)(2,1)S(1)}, bf16[784,1024]{1,0:T(8,128)(2,1)S(1)}, u32[]{:S(2)}, u32[]{:S(2)}) collective-permute-start(bf16[784,1024]{1,0:T(8,128)(2,1)S(1)} %convolution_convert_fusion.5), channel_id=1, source_target_pairs={{0,1},{1,0},{2,3},{3,2},{4,5},{5,4},{6,7},{7,6},{8,9},{9,8},{10,11... | collective-permute-start | bytes 4816904 | tf_op jit(solution)/shard_map/ppermute | solution.py:173
  243.5 31.7 %collective-permute-start.27 = (bf16[784,1024]{1,0:T(8,128)(2,1)S(1)}, bf16[784,1024]{1,0:T(8,128)(2,1)S(1)}, u32[]{:S(2)}, u32[]{:S(2)}) collective-permute-start(bf16[784,1024]{1,0:T(8,128)(2,1)S(1)} %convolution_convert_fusion.4), channel_id=1, source_target_pairs={{0,1},{1,0},{2,3},{3,2},{4,5},{5,4},{6,7},{7,6},{8,9},{9,8},{10,11... | collective-permute-start | bytes 4816904 | tf_op jit(solution)/shard_map/ppermute | solution.py:173
  260.5 99.3 %collective-permute-start.77 = (bf16[64,2048]{1,0:T(8,128)(2,1)}, bf16[64,2048]{1,0:T(8,128)(2,1)}, u32[]{:S(2)}, u32[]{:S(2)}) collective-permute-start(bf16[64,2048]{1,0:T(8,128)(2,1)} %dynamic-slice_convert_fusion), channel_id=1, source_target_pairs={{0,4},{2,6},{4,0},{6,2},{1,5},{3,7},{5,1},{7,3},{8,12},{10,14},{12... | collective-permute-start | bytes 786440 | tf_op jit(solution)/shard_map/ppermute | solution.py:173
  275.1 93.5 %collective-permute-start.67 = (bf16[64,2048]{1,0:T(8,128)(2,1)S(1)}, bf16[64,2048]{1,0:T(8,128)(2,1)}, u32[]{:S(2)}, u32[]{:S(2)}) collective-permute-start(bf16[64,2048]{1,0:T(8,128)(2,1)S(1)} %dynamic-slice_convert_fusion.1), channel_id=1, source_target_pairs={{0,4},{2,6},{4,0},{6,2},{1,5},{3,7},{5,1},{7,3},{8,12},{10,14},{12... | collective-permute-start | bytes 786440 | tf_op jit(solution)/shard_map/ppermute | solution.py:173
  296.1 66.1 %collective-permute-start.55 = (bf16[128,512]{1,0:T(8,128)(2,1)}, bf16[128,512]{1,0:T(8,128)(2,1)S(1)}, u32[]{:S(2)}, u32[]{:S(2)}) collective-permute-start(bf16[128,512]{1,0:T(8,128)(2,1)} %slice.423), channel_id=1, source_target_pairs={{0,16},{8,24},{16,0},{24,8},{1,17},{9,25},{17,1},{25,9},{2,18},{10... | collective-permute-start | bytes 393224 | tf_op jit(solution)/shard_map/ppermute | solution.py:173
  307.3 56.1 %collective-permute-start.50 = (bf16[128,512]{1,0:T(8,128)(2,1)}, bf16[128,512]{1,0:T(8,128)(2,1)S(1)}, u32[]{:S(2)}, u32[]{:S(2)}) collective-permute-start(bf16[128,512]{1,0:T(8,128)(2,1)} %slice.424), channel_id=1, source_target_pairs={{0,8},{8,0},{16,24},{24,16},{1,9},{9,1},{17,25},{25,17},{2,10},{10... | collective-permute-start | bytes 393224 | tf_op jit(solution)/shard_map/ppermute | solution.py:173
  308.7 56.5 %collective-permute-start.52 = (bf16[128,512]{1,0:T(8,128)(2,1)}, bf16[128,512]{1,0:T(8,128)(2,1)}, u32[]{:S(2)}, u32[]{:S(2)}) collective-permute-start(bf16[128,512]{1,0:T(8,128)(2,1)} %fusion.95), channel_id=1, source_target_pairs={{0,16},{8,24},{16,0},{24,8},{1,17},{9,25},{17,1},{25,9},{2,18},{10... | collective-permute-start | bytes 393224 | tf_op jit(solution)/shard_map/ppermute | solution.py:173
  365.1 33.7 %collective-permute-start.47 = (bf16[128,768]{1,0:T(8,128)(2,1)S(1)}, bf16[128,768]{1,0:T(8,128)(2,1)S(1)}, u32[]{:S(2)}, u32[]{:S(2)}) collective-permute-start(bf16[128,768]{1,0:T(8,128)(2,1)S(1)} %slice.421), channel_id=1, source_target_pairs={{0,16},{8,24},{16,0},{24,8},{1,17},{9,25},{17,1},{25,9},{2,18},{10... | collective-permute-start | bytes 589832 | tf_op jit(solution)/shard_map/ppermute | solution.py:173
  366.1 32.7 %collective-permute-start.42 = (bf16[128,768]{1,0:T(8,128)(2,1)S(1)}, bf16[128,768]{1,0:T(8,128)(2,1)S(1)}, u32[]{:S(2)}, u32[]{:S(2)}) collective-permute-start(bf16[128,768]{1,0:T(8,128)(2,1)S(1)} %slice.422), channel_id=1, source_target_pairs={{0,8},{8,0},{16,24},{24,16},{1,9},{9,1},{17,25},{25,17},{2,10},{10... | collective-permute-start | bytes 589832 | tf_op jit(solution)/shard_map/ppermute | solution.py:173
  373.7 29.8 %collective-permute-start.31 = (bf16[1568,512]{1,0:T(8,128)(2,1)S(1)}, bf16[1568,512]{1,0:T(8,128)(2,1)S(1)}, u32[]{:S(2)}, u32[]{:S(2)}) collective-permute-start(bf16[1568,512]{1,0:T(8,128)(2,1)S(1)} %slice.309), channel_id=1, source_target_pairs={{0,1},{1,0},{2,3},{3,2},{4,5},{5,4},{6,7},{7,6},{8,9},{9,8},{10,11... | collective-permute-start | bytes 4816904 | tf_op jit(solution)/shard_map/ppermute | solution.py:173
  398.8 38.1 %collective-permute-start.68 = (bf16[64,2048]{1,0:T(8,128)(2,1)S(1)}, bf16[64,2048]{1,0:T(8,128)(2,1)S(1)}, u32[]{:S(2)}, u32[]{:S(2)}) collective-permute-start(bf16[64,2048]{1,0:T(8,128)(2,1)S(1)} %add_convert_fusion.7), channel_id=1, source_target_pairs={{0,4},{2,6},{4,0},{6,2},{1,5},{3,7},{5,1},{7,3},{8,12},{10,14},{12... | collective-permute-start | bytes 786440 | tf_op jit(solution)/shard_map/ppermute | solution.py:173
  398.9 38.2 %collective-permute-start.59 = (bf16[128,512]{1,0:T(8,128)(2,1)S(1)}, bf16[128,512]{1,0:T(8,128)(2,1)S(1)}, u32[]{:S(2)}, u32[]{:S(2)}) collective-permute-start(bf16[128,512]{1,0:T(8,128)(2,1)S(1)} %maximum_select_fusion.5), channel_id=1, source_target_pairs={{0,2},{2,0},{4,6},{6,4},{1,3},{3,1},{5,7},{7,5},{8,10},{10,8},{12,... | collective-permute-start | bytes 393224 | tf_op jit(solution)/shard_map/ppermute | solution.py:173
  403.5 42.0 %collective-permute-start.48 = (bf16[256,768]{1,0:T(8,128)(2,1)S(1)}, bf16[256,768]{1,0:T(8,128)(2,1)S(1)}, u32[]{:S(2)}, u32[]{:S(2)}) collective-permute-start(bf16[256,768]{1,0:T(8,128)(2,1)S(1)} %pad_maximum_fusion.13), channel_id=1, source_target_pairs={{0,4},{2,6},{4,0},{6,2},{1,5},{3,7},{5,1},{7,3},{8,12},{10,14},{12... | collective-permute-start | bytes 1179656 | tf_op jit(solution)/shard_map/ppermute | solution.py:173
  404.3 49.7 %collective-permute-start.33 = (bf16[392,512]{1,0:T(8,128)(2,1)S(1)}, bf16[392,512]{1,0:T(8,128)(2,1)S(1)}, u32[]{:S(2)}, u32[]{:S(2)}) collective-permute-start(bf16[392,512]{1,0:T(8,128)(2,1)S(1)} %get-tuple-element.64), channel_id=1, source_target_pairs={{0,4},{2,6},{4,0},{6,2},{1,5},{3,7},{5,1},{7,3},{8,12},{10,14},{12... | collective-permute-start | bytes 1204232 | tf_op jit(solution)/shard_map/ppermute | solution.py:173
  407.3 46.8 %collective-permute-start.34 = (bf16[392,512]{1,0:T(8,128)(2,1)S(1)}, bf16[392,512]{1,0:T(8,128)(2,1)S(1)}, u32[]{:S(2)}, u32[]{:S(2)}) collective-permute-start(bf16[392,512]{1,0:T(8,128)(2,1)S(1)} %get-tuple-element.65), channel_id=1, source_target_pairs={{0,6},{2,4},{4,2},{6,0},{1,7},{3,5},{5,3},{7,1},{8,14},{10,12},{12... | collective-permute-start | bytes 1204232 | tf_op jit(solution)/shard_map/ppermute | solution.py:173
  436.9 24.9 %collective-permute-start.32 = (bf16[392,512]{1,0:T(8,128)(2,1)S(1)}, bf16[392,512]{1,0:T(8,128)(2,1)S(1)}, u32[]{:S(2)}, u32[]{:S(2)}) collective-permute-start(bf16[392,512]{1,0:T(8,128)(2,1)S(1)} %get-tuple-element.66), channel_id=1, source_target_pairs={{0,2},{2,0},{4,6},{6,4},{1,3},{3,1},{5,7},{7,5},{8,10},{10,8},{12,... | collective-permute-start | bytes 1204232 | tf_op jit(solution)/shard_map/ppermute | solution.py:173
  437.1 36.0 %collective-permute-start.79 = (bf16[128,2048]{1,0:T(8,128)(2,1)S(1)}, bf16[128,2048]{1,0:T(8,128)(2,1)S(1)}, u32[]{:S(2)}, u32[]{:S(2)}) collective-permute-start(bf16[128,2048]{1,0:T(8,128)(2,1)S(1)} %maximum_select_fusion.3), channel_id=1, source_target_pairs={{0,2},{2,0},{4,6},{6,4},{1,3},{3,1},{5,7},{7,5},{8,10},{10,8},{12,... | collective-permute-start | bytes 1572872 | tf_op jit(solution)/shard_map/ppermute | solution.py:173
  445.5 38.9 %collective-permute-start.69 = (bf16[128,2048]{1,0:T(8,128)(2,1)S(1)}, bf16[128,2048]{1,0:T(8,128)(2,1)S(1)}, u32[]{:S(2)}, u32[]{:S(2)}) collective-permute-start(bf16[128,2048]{1,0:T(8,128)(2,1)S(1)} %maximum_select_fusion.2), channel_id=1, source_target_pairs={{0,2},{2,0},{4,6},{6,4},{1,3},{3,1},{5,7},{7,5},{8,10},{10,8},{12,... | collective-permute-start | bytes 1572872 | tf_op jit(solution)/shard_map/ppermute | solution.py:173
  454.0 38.6 %collective-permute-start.49 = (bf16[256,768]{1,0:T(8,128)(2,1)S(1)}, bf16[256,768]{1,0:T(8,128)(2,1)S(1)}, u32[]{:S(2)}, u32[]{:S(2)}) collective-permute-start(bf16[256,768]{1,0:T(8,128)(2,1)S(1)} %add_convert_fusion.5), channel_id=1, source_target_pairs={{0,2},{2,0},{4,6},{6,4},{1,3},{3,1},{5,7},{7,5},{8,10},{10,8},{12,... | collective-permute-start | bytes 1179656 | tf_op jit(solution)/shard_map/ppermute | solution.py:173
  463.8 39.1 %collective-permute-start.35 = (bf16[784,512]{1,0:T(8,128)(2,1)}, bf16[784,512]{1,0:T(8,128)(2,1)}, u32[]{:S(2)}, u32[]{:S(2)}) collective-permute-start(bf16[784,512]{1,0:T(8,128)(2,1)} %pad_maximum_fusion.9), channel_id=1, source_target_pairs={{0,1},{1,0},{2,3},{3,2},{4,5},{5,4},{6,7},{7,6},{8,9},{9,8},{10,11... | collective-permute-start | bytes 2408456 | tf_op jit(solution)/shard_map/ppermute | solution.py:173
  (121 other events, 1323.3 us)

commit v2 on v1

v2 whole, which is shorter than its diff:
```python
import jax
import jax.numpy as jnp
from jax import lax
from jax.experimental import pallas as pl
from jax.experimental.pallas import tpu as pltpu
from jax.sharding import PartitionSpec as P

HEAD_DIM = 64
EPSILON = 1e-06
LOW = jnp.bfloat16
FULL = jnp.float32

ROW_BY_ROW = (((1,), (1,)), ((), ()))
PLAIN = (((1,), (0,)), ((), ()))
COLUMN_BY_COLUMN = (((0,), (0,)), ((), ()))


def product(left, right, dims):
    return lax.dot_general(left, right, dims, preferred_element_type=FULL)


def normalize(value_rows):
    center = value_rows - jnp.mean(value_rows, axis=-1, keepdims=True)
    inverse = lax.rsqrt(jnp.mean(center * center, axis=-1, keepdims=True) + EPSILON)
    return (center * inverse, inverse)


def norm_back(upstream, gain, scaled, inverse):
    weighted = upstream * gain
    return inverse * (
        weighted
        - jnp.mean(weighted, axis=-1, keepdims=True)
        - scaled * jnp.mean(weighted * scaled, axis=-1, keepdims=True)
    )


def attention_forward_kernel(q_ref, k_ref, v_ref, o_ref, lse_ref):
    rows, width = q_ref.shape
    lane = lax.broadcasted_iota(jnp.int32, (rows, width), 1)
    lse = jnp.zeros((rows, width), FULL)
    q = q_ref[...] * jnp.asarray(HEAD_DIM ** (-0.5), LOW)
    k = k_ref[...]
    v = v_ref[...]
    out = None
    for head in range(width // HEAD_DIM):
        mask = (lane // HEAD_DIM) == head
        scores = product(jnp.where(mask, q, jnp.zeros_like(q)), k, ROW_BY_ROW)
        top = jnp.max(scores, axis=-1, keepdims=True)
        weights = jnp.exp(scores - top)
        total = jnp.sum(weights, axis=-1, keepdims=True)
        part = product(weights.astype(LOW), v, PLAIN) / total
        out = part if out is None else jnp.where(mask, part, out)
        lse = jnp.where(lane == head, top + jnp.log(total), lse)
    o_ref[...] = out.astype(LOW)
    lse_ref[0] = lse.T[: lse_ref.shape[1]]


def row_chunk(count):
    for chunk in range(256, 0, -16):
        if count % chunk == 0:
            return chunk
    raise ValueError("rows")


def attention_forward(joint, pair):
    count, columns = joint.shape
    width = 2 * HEAD_DIM
    chunk = row_chunk(count)
    steps = count // chunk
    kind = columns // (3 * width)
    whole_k = pl.BlockSpec((count, width), lambda i: (0, kind + pair))
    whole_v = pl.BlockSpec((count, width), lambda i: (0, 2 * kind + pair))
    out, lse = pl.pallas_call(
        attention_forward_kernel,
        grid=(steps,),
        in_specs=[pl.BlockSpec((chunk, width), lambda i: (i, pair)), whole_k, whole_v],
        out_specs=[
            pl.BlockSpec((chunk, width), lambda i: (i, 0)),
            pl.BlockSpec((1, 8, chunk), lambda i: (i, 0, 0)),
        ],
        out_shape=[
            jax.ShapeDtypeStruct((count, width), LOW),
            jax.ShapeDtypeStruct((steps, 8, chunk), FULL),
        ],
        compiler_params=pltpu.CompilerParams(vmem_limit_bytes=40 << 20),
        cost_estimate=pl.CostEstimate(
            flops=16 * count * count * width,
            transcendentals=2 * count * count,
            bytes_accessed=8 * count * width,
        ),
        name="attention_forward",
    )(joint, joint, joint)
    return out, lse.transpose(1, 0, 2).reshape(8, count)


def attention_backward_kernel(
    q_ref, k_ref, v_ref, da_ref, o_ref, lse_ref, dq_ref, dk_ref, dv_ref,
    q_heads, da_heads, delta_ref, dq_total,
):
    count, width = q_ref.shape
    chunk = k_ref.shape[0]
    step = pl.program_id(0)
    heads = width // HEAD_DIM
    scale = jnp.asarray(HEAD_DIM ** (-0.5), LOW)

    @pl.when(step == 0)
    def _():
        lane = lax.broadcasted_iota(jnp.int32, (count, width), 1)
        delta = jnp.zeros((count, width), FULL)
        q = q_ref[...] * scale
        da = da_ref[...]
        both = da.astype(FULL) * o_ref[...].astype(FULL)
        for head in range(heads):
            mask = (lane // HEAD_DIM) == head
            q_heads[head] = jnp.where(mask, q, jnp.zeros_like(q))
            da_heads[head] = jnp.where(mask, da, jnp.zeros_like(da))
            row = jnp.sum(jnp.where(mask, both, 0.0), axis=-1, keepdims=True)
            delta = jnp.where(lane == head, row, delta)
        delta_ref[...] = delta.T[:8]
        dq_total[...] = jnp.zeros_like(dq_total)

    lane = lax.broadcasted_iota(jnp.int32, (chunk, width), 1)
    k = k_ref[...]
    v = v_ref[...]
    scaled_k = k * scale
    dk = dv = None
    for head in range(heads):
        q = q_heads[head]
        da = da_heads[head]
        probs = jnp.exp(product(k, q, ROW_BY_ROW) - lse_ref[head : head + 1, :])
        slope = probs * (product(v, da, ROW_BY_ROW) - delta_ref[head : head + 1, :])
        slope = slope.astype(LOW)
        dv_part = product(probs.astype(LOW), da, PLAIN)
        dk_part = product(slope, q, PLAIN)
        dv = dv_part if dv is None else dv + dv_part
        dk = dk_part if dk is None else dk + dk_part
        one_k = jnp.where((lane // HEAD_DIM) == head, scaled_k, jnp.zeros_like(k))
        dq_total[...] += product(slope, one_k, COLUMN_BY_COLUMN)
    dk_ref[...] = dk.astype(LOW)
    dv_ref[...] = dv.astype(LOW)

    @pl.when(step == pl.num_programs(0) - 1)
    def _():
        dq_ref[...] = dq_total[...].astype(LOW)


def attention_backward(joint, da, out, lse, pair):
    count, columns = joint.shape
    width = 2 * HEAD_DIM
    chunk = row_chunk(count)
    kind = columns // (3 * width)
    part_k = pl.BlockSpec((chunk, width), lambda i: (i, kind + pair))
    part_v = pl.BlockSpec((chunk, width), lambda i: (i, 2 * kind + pair))
    whole = pl.BlockSpec((count, width), lambda i: (0, pair))
    alone = pl.BlockSpec((count, width), lambda i: (0, 0))
    part_out = pl.BlockSpec((chunk, width), lambda i: (i, 0))
    grad = jax.ShapeDtypeStruct((count, width), LOW)
    return pl.pallas_call(
        attention_backward_kernel,
        grid=(count // chunk,),
        in_specs=[whole, part_k, part_v, alone, alone, pl.BlockSpec((8, count), lambda i: (0, 0))],
        out_specs=[alone, part_out, part_out],
        out_shape=[grad, grad, grad],
        scratch_shapes=[
            pltpu.VMEM((2, count, width), LOW),
            pltpu.VMEM((2, count, width), LOW),
            pltpu.VMEM((8, count), FULL),
            pltpu.VMEM((count, width), FULL),
        ],
        compiler_params=pltpu.CompilerParams(vmem_limit_bytes=40 << 20),
        cost_estimate=pl.CostEstimate(
            flops=40 * count * count * width,
            transcendentals=2 * count * count,
            bytes_accessed=16 * count * width,
        ),
        name="attention_backward",
    )(joint, joint, joint, da, out, lse)


def feed_forward_kernel(
    normed_ref, slope_ref, expand_ref, bias_ref, reduce_ref,
    active_ref, expand_slope_ref, back_ref, bias_grad_ref, total,
):
    step = pl.program_id(0)
    count = normed_ref.shape[0]
    half = count // 2
    bias_grad = None
    for rows in (slice(0, half), slice(half, count)):
        hidden = product(normed_ref[rows], expand_ref[...], PLAIN) + bias_ref[...]
        upstream = product(slope_ref[rows], reduce_ref[...], PLAIN)
        share = 0.5 * (1.0 + lax.erf(hidden * (0.5**0.5)))
        active_ref[rows] = (hidden * share).astype(LOW)
        density = jnp.exp(-0.5 * hidden * hidden) * 0.3989422804014327
        slope = (upstream * (share + hidden * density)).astype(LOW)
        expand_slope_ref[rows] = slope
        part = jnp.sum(slope.astype(FULL), axis=0, keepdims=True)
        bias_grad = part if bias_grad is None else bias_grad + part
        back = product(slope, expand_ref[...], ROW_BY_ROW)

        @pl.when(step == 0)
        def _():
            total[rows] = back

        @pl.when(step > 0)
        def _():
            total[rows] += back

    bias_grad_ref[...] = bias_grad

    @pl.when(step == pl.num_programs(0) - 1)
    def _():
        back_ref[...] = total[...].astype(LOW)


def feed_forward(normed, slope, expand, bias, reduce):
    count, width = normed.shape
    hidden = expand.shape[1]
    block = 512 if hidden % 512 == 0 else hidden
    whole = pl.BlockSpec((count, width), lambda i: (0, 0))
    columns = pl.BlockSpec((width, block), lambda i: (0, i))
    out = pl.BlockSpec((count, block), lambda i: (0, i))
    row = pl.BlockSpec((1, block), lambda i: (0, i))
    return pl.pallas_call(
        feed_forward_kernel,
        grid=(hidden // block,),
        in_specs=[whole, whole, columns, row, columns],
        out_specs=[out, out, whole, row],
        out_shape=[
            jax.ShapeDtypeStruct((count, hidden), LOW),
            jax.ShapeDtypeStruct((count, hidden), LOW),
            jax.ShapeDtypeStruct((count, width), LOW),
            jax.ShapeDtypeStruct((1, hidden), FULL),
        ],
        scratch_shapes=[pltpu.VMEM((count, width), FULL)],
        compiler_params=pltpu.CompilerParams(vmem_limit_bytes=48 << 20),
        cost_estimate=pl.CostEstimate(
            flops=6 * count * width * hidden,
            transcendentals=2 * count * hidden,
            bytes_accessed=4 * (count * hidden + width * hidden) + 6 * count * width,
        ),
        name="feed_forward",
    )(normed, slope, expand, bias, reduce)


def swap(value, axis, distance):
    size = lax.axis_size(axis)
    return lax.ppermute(value, axis, [(i, i ^ distance) for i in range(size)])


def fence(*values):
    return lax.optimization_barrier(values)


def gather_near(rows_here):
    if lax.axis_size("fsdp") != 4:
        return (lax.all_gather(rows_here, "fsdp", axis=0, tiled=True),)
    return (rows_here, swap(rows_here, "fsdp", 1), swap(rows_here, "fsdp", 2))


def gather_far(held):
    if len(held) == 1:
        return held
    rows_here, near, side = held
    half = rows_here.shape[0] // 2
    return held + (swap(side[:half], "fsdp", 1), swap(near[half:], "fsdp", 2))


def place_near(held):
    if len(held) == 1:
        return held[0]
    rows_here, near, side = held[:3]
    me = lax.axis_index("fsdp")
    count, width = rows_here.shape
    out = jnp.zeros((4 * count, width), rows_here.dtype)
    out = lax.dynamic_update_slice(out, rows_here, (me * count, 0))
    out = lax.dynamic_update_slice(out, near, ((me ^ 1) * count, 0))
    return lax.dynamic_update_slice(out, side, ((me ^ 2) * count, 0))


def place_far(out, held):
    if len(held) == 1:
        return out
    far_top, far_low = held[3:]
    half = far_top.shape[0]
    start = (lax.axis_index("fsdp") ^ 3) * 2 * half
    out = lax.dynamic_update_slice(out, far_top, (start, 0))
    return lax.dynamic_update_slice(out, far_low, (start + half, 0))


def grad_block(left, right, distance):
    count = left.shape[1] // 4
    start = (lax.axis_index("fsdp") ^ distance) * count
    piece = lax.dynamic_slice_in_dim(left, start, count, 1)
    return product(piece, right, COLUMN_BY_COLUMN)


def sum_far(left, right):
    if lax.axis_size("fsdp") != 4:
        return ()
    far = grad_block(left, right, 3).astype(LOW)
    half = far.shape[0] // 2
    return (swap(far[:half], "fsdp", 1), swap(far[half:], "fsdp", 2))


def sum_near(left, right, far):
    if not far:
        whole = product(left, right, COLUMN_BY_COLUMN).astype(LOW)
        return (lax.psum_scatter(whole, "fsdp", scatter_dimension=0, tiled=True),)
    far_top, far_low = far
    half = far_top.shape[0]
    near = grad_block(left, right, 1)
    side = grad_block(left, right, 2)
    near = jnp.concatenate([near[:half], near[half:] + far_low.astype(FULL)], axis=0)
    side = jnp.concatenate([side[:half] + far_top.astype(FULL), side[half:]], axis=0)
    return (swap(near.astype(LOW), "fsdp", 1), swap(side.astype(LOW), "fsdp", 2))


def sum_own(left, right, near):
    if len(near) == 1:
        return near[0].astype(FULL)
    return grad_block(left, right, 0) + (near[0].astype(FULL) + near[1].astype(FULL))


def split_rows(value, bit, distance):
    half = value.shape[0] // 2
    keep = lax.dynamic_slice_in_dim(value, bit * half, half, 0)
    send = lax.dynamic_slice_in_dim(value, (1 - bit) * half, half, 0)
    return keep, swap(send.astype(LOW), "ctx", distance)


def both(pair):
    return pair[0].astype(FULL) + pair[1].astype(FULL)


def join_rows(value, bit, distance):
    other = swap(value, "ctx", distance)
    return jnp.where(
        bit == 0,
        jnp.concatenate([value, other], axis=0),
        jnp.concatenate([other, value], axis=0),
    )


def sum_pairwise(value, axis):
    near = value + swap(value, axis, 1)
    far = swap(value, axis, 2) + swap(value, axis, 3)
    return near + far


def swapped_if(bit, pair):
    return [jnp.where(bit == 0, pair[0], pair[1]), jnp.where(bit == 0, pair[1], pair[0])]


def per_device(
    tokens,
    clip_mask,
    cotangent,
    first_gain,
    first_shift,
    joint_weight,
    joint_bias,
    mixer_weight,
    mixer_bias,
    second_gain,
    second_shift,
    expand_weight,
    expand_bias,
    reduce_weight,
    reduce_bias,
):
    clips_here, rows_here, width = tokens.shape
    if lax.axis_size("ctx") != 4 or lax.axis_size("tp") != 2 or clips_here != 2:
        raise ValueError("mesh")
    shard = lax.axis_index("fsdp")
    block = lax.axis_index("ctx")
    core = lax.axis_index("tp")
    clip_at = block >> 1
    part_at = block & 1
    width_half = width // 2
    quarter = width_half // 2
    features = joint_weight.shape[2]
    part_width = features // 2
    pair_width = 2 * HEAD_DIM
    tokens_here = clips_here * rows_here

    expand_full = lax.all_gather(expand_weight, "fsdp", axis=0, tiled=True)
    inputs = tokens.astype(FULL)
    first_scaled, first_inverse = normalize(inputs)
    first_normed = (first_scaled * first_gain + first_shift).astype(LOW)
    mine = lax.dynamic_slice_in_dim(first_normed, core * width_half, width_half, 2)
    other_side = lax.dynamic_slice_in_dim(first_normed, (1 - core) * width_half, width_half, 2)
    own_clip = lax.dynamic_index_in_dim(mine, clip_at, 0, False)
    own_other = lax.dynamic_index_in_dim(other_side, clip_at, 0, False)
    other_clip = lax.dynamic_index_in_dim(mine, 1 - clip_at, 0, False)
    joint_part = lax.dynamic_slice_in_dim(joint_weight, part_at * part_width, part_width, 2)
    joint_part = jnp.concatenate([joint_part[:, kind] for kind in range(3)], axis=1)

    own_clip, left, right, joint_part = fence(
        own_clip, other_clip[:, :quarter], other_clip[:, quarter:], joint_part
    )
    near_rows = swap(own_clip, "ctx", 1)
    across_left = swap(left, "ctx", 2)
    far_right = swap(right, "ctx", 3)
    joint_held = gather_near(joint_part)

    near_rows, across_left, far_right, joint_held = fence(
        near_rows, across_left, far_right, joint_held
    )
    far_left = swap(across_left, "ctx", 1)
    across_right = swap(far_right, "ctx", 1)
    near_other = swap(near_rows, "tp", 1)
    joint_held = gather_far(joint_held)

    far_left, across_right, near_other, joint_held, mixer_weight = fence(
        far_left, across_right, near_other, joint_held, mixer_weight
    )
    cross_rows = jnp.concatenate(
        [
            jnp.concatenate([across_left, across_right], axis=1),
            jnp.concatenate([far_left, far_right], axis=1),
        ],
        axis=0,
    )
    cross_other = swap(cross_rows, "tp", 1)
    mixer_held = gather_near(mixer_weight)
    joint_rows = place_far(place_near(joint_held), joint_held)
    joint_full = jnp.concatenate(
        [
            lax.dynamic_slice_in_dim(joint_rows, core * width_half, width_half, 0),
            lax.dynamic_slice_in_dim(joint_rows, (1 - core) * width_half, width_half, 0),
        ],
        axis=0,
    )

    cross_other, mixer_held, joint_full, reduce_weight = fence(
        cross_other, mixer_held, joint_full, reduce_weight
    )
    mixer_held = gather_far(mixer_held)
    reduce_held = gather_near(reduce_weight)
    normed_mine = jnp.concatenate([own_clip, near_rows, cross_rows], axis=0)
    normed_other = jnp.concatenate([own_other, near_other, cross_other], axis=0)
    normed_clip = jnp.concatenate([normed_mine, normed_other], axis=1)
    bias_part = lax.dynamic_slice_in_dim(joint_bias, part_at * part_width, part_width, 1)
    bias_row = jnp.concatenate([bias_part[0], jnp.zeros_like(bias_part[0]), bias_part[1]])
    joint_out = (product(normed_clip, joint_full, PLAIN) + bias_row).astype(LOW)
    out_first, log_first = attention_forward(joint_out, 0)

    out_first, joint_out, mixer_held = fence(out_first, joint_out, mixer_held)
    first_blocks = out_first.reshape(4, rows_here, pair_width)
    arrived_first = [swap(first_blocks[d], "ctx", d) for d in (1, 2, 3)]
    out_second, log_second = attention_forward(joint_out, 1)

    out_second, arrived_first, reduce_held, expand_full = fence(
        out_second, arrived_first, reduce_held, expand_full
    )
    second_blocks = out_second.reshape(4, rows_here, pair_width)
    arrived_second = [swap(second_blocks[d], "ctx", d) for d in (1, 2, 3)]
    reduce_near = place_near(reduce_held)
    reduce_held = gather_far(reduce_held)
    mixer_full = place_far(place_near(mixer_held), mixer_held)

    arrived_second, reduce_held, reduce_near, mixer_full = fence(
        arrived_second, reduce_held, reduce_near, mixer_full
    )
    reduce_full = place_far(reduce_near, reduce_held)
    arrived = [jnp.concatenate([first_blocks[0], second_blocks[0]], axis=1)] + [
        jnp.concatenate([one, two], axis=1) for one, two in zip(arrived_first, arrived_second)
    ]
    own_joined = jnp.concatenate(swapped_if(part_at, arrived[:2]), axis=1)
    other_joined = jnp.concatenate(swapped_if(part_at, arrived[2:]), axis=1)
    mixed_in = jnp.concatenate(swapped_if(clip_at, [own_joined, other_joined]), axis=0)
    flat_inputs = inputs.reshape(tokens_here, width)
    valid = jnp.broadcast_to(
        clip_mask.astype(FULL)[:, None, None], (clips_here, rows_here, 1)
    ).reshape(tokens_here, 1)
    mixer_part = product(mixed_in, mixer_full, ROW_BY_ROW).astype(LOW)
    mixer_out = both((mixer_part, swap(mixer_part, "tp", 1))) + mixer_bias
    second_scaled, second_inverse = normalize(flat_inputs + mixer_out)
    second_normed = (second_scaled * second_gain + second_shift).astype(LOW)
    outer = cotangent.astype(FULL).reshape(tokens_here, width)
    branch_slope = outer * valid
    reduce_slope = branch_slope.astype(LOW)
    reduce_bias_grad = jnp.sum(reduce_slope.astype(FULL), axis=0)

    second_normed, reduce_slope, reduce_full = fence(second_normed, reduce_slope, reduce_full)
    activated, expand_slope, second_part, expand_bias_grad = feed_forward(
        second_normed, reduce_slope, expand_full, expand_bias[None], reduce_full
    )
    expand_bias_grad = expand_bias_grad[0]

    second_swapped = swap(second_part, "tp", 1)
    reduce_far = sum_far(reduce_slope, activated)
    second_slope = both((second_part, second_swapped))
    second_gain_grad = jnp.sum(second_slope * second_scaled, axis=0)
    second_shift_grad = jnp.sum(second_slope, axis=0)
    first_sum_back = norm_back(second_slope, second_gain, second_scaled, second_inverse)
    mixer_slope = (branch_slope + first_sum_back).astype(LOW)
    mixer_bias_grad = jnp.sum(mixer_slope.astype(FULL), axis=0)
    attended_slope = product(mixer_slope, mixer_full, PLAIN).astype(LOW)

    attended_slope, reduce_far, mixer_slope, expand_slope, mixed_in, activated = fence(
        attended_slope, reduce_far, mixer_slope, expand_slope, mixed_in, activated
    )
    leaving = []
    for piece in swapped_if(clip_at, [attended_slope[:rows_here], attended_slope[rows_here:]]):
        leaving += swapped_if(part_at, [piece[:, :part_width], piece[:, part_width:]])
    slope_first = [leaving[0][:, :pair_width]] + [
        swap(leaving[d][:, :pair_width], "ctx", d) for d in (1, 2, 3)
    ]
    reduce_near = sum_near(reduce_slope, activated, reduce_far)
    early_whole = jnp.concatenate(
        [
            product(second_normed, expand_slope, COLUMN_BY_COLUMN).astype(LOW),
            product(mixer_slope, mixed_in, COLUMN_BY_COLUMN).astype(LOW),
        ],
        axis=1,
    )

    slope_first, early_whole, leaving = fence(slope_first, early_whole, leaving)
    early_rows = lax.psum_scatter(early_whole, "fsdp", scatter_dimension=0, tiled=True)
    slope_second = [leaving[0][:, pair_width:]] + [
        swap(leaving[d][:, pair_width:], "ctx", d) for d in (1, 2, 3)
    ]
    grad_first = attention_backward(
        joint_out, jnp.concatenate(slope_first, axis=0), out_first, log_first, 0
    )

    grad_first, slope_second, reduce_near = fence(grad_first, slope_second, reduce_near)
    reduce_rows = split_rows(sum_own(reduce_slope, activated, reduce_near), part_at, 1)
    grad_second = attention_backward(
        joint_out, jnp.concatenate(slope_second, axis=0), out_second, log_second, 1
    )

    grad_second, reduce_rows = fence(grad_second, reduce_rows)
    reduce_rows = split_rows(both(reduce_rows), clip_at, 2)
    joint_slope = jnp.concatenate(
        [grad[kind] for kind in range(3) for grad in (grad_first, grad_second)], axis=1
    )
    first_there = product(joint_slope, joint_full[width_half:], ROW_BY_ROW).astype(LOW)
    first_here = product(joint_slope, joint_full[:width_half], ROW_BY_ROW).astype(LOW)
    first_half = both((first_here, swap(first_there, "tp", 1))).astype(LOW)

    first_half, reduce_rows, joint_slope, early_rows = fence(
        first_half, reduce_rows, joint_slope, early_rows
    )
    early_rows = lax.psum(early_rows, "ctx")
    pieces = first_half.reshape(4, rows_here, width_half)
    to_left = (pieces[2][:, :quarter], swap(pieces[3][:, :quarter], "ctx", 1))
    to_right = (pieces[3][:, quarter:], swap(pieces[2][:, quarter:], "ctx", 1))
    own_half = (pieces[0], swap(pieces[1], "ctx", 1))
    reduce_rows = both(reduce_rows).astype(LOW)
    normed_columns = jnp.concatenate(swapped_if(core, [normed_mine, normed_other]), axis=1)
    joint_far = sum_far(normed_columns, joint_slope)
    slope_sums = jnp.sum(joint_slope.astype(FULL), axis=0)
    bias_sums = jnp.stack([slope_sums[:part_width], slope_sums[2 * part_width :]])
    joint_bias_grad = lax.dynamic_update_slice(
        jnp.zeros((2, features), FULL), bias_sums, (0, part_at * part_width)
    )

    to_left, to_right, own_half, joint_far, activated = fence(
        to_left, to_right, own_half, joint_far, activated
    )
    other_half = jnp.concatenate(
        [
            swap(both(to_left).astype(LOW), "ctx", 2),
            swap(both(to_right).astype(LOW), "ctx", 3),
        ],
        axis=1,
    )
    joint_near = sum_near(normed_columns, joint_slope, joint_far)
    reduce_part = product(activated, reduce_full, ROW_BY_ROW).astype(LOW)
    reduce_swapped = swap(reduce_part, "tp", 1)

    other_half, joint_near, reduce_rows, reduce_part, reduce_swapped = fence(
        other_half, joint_near, reduce_rows, reduce_part, reduce_swapped
    )
    reduce_out = both((reduce_part, reduce_swapped)) + reduce_bias
    result = (flat_inputs + valid * (mixer_out + reduce_out)).astype(LOW)
    slope_half = jnp.concatenate(
        swapped_if(clip_at, [both(own_half).astype(LOW), other_half]), axis=0
    )
    slope_other = swap(slope_half, "tp", 1)
    first_slope = jnp.concatenate(swapped_if(core, [slope_half, slope_other]), axis=1)
    first_slope, early_rows = fence(first_slope, early_rows)
    first_slope = first_slope.astype(FULL)
    early_rows = early_rows.astype(FULL)
    expand_grad = early_rows[:, : expand_full.shape[1]]
    mixer_grad = early_rows[:, expand_full.shape[1] :]
    joint_sum = sum_own(normed_columns, joint_slope, joint_near).astype(LOW)
    joint_sum = both((joint_sum, swap(joint_sum, "ctx", 2))).astype(LOW)
    joint_parts = swapped_if(part_at, [joint_sum, swap(joint_sum, "ctx", 1)])
    joint_grad = jnp.concatenate(
        [piece.reshape(-1, 3, part_width) for piece in joint_parts], axis=2
    ).astype(FULL)
    reduce_grad = join_rows(join_rows(reduce_rows, clip_at, 2), part_at, 1).astype(FULL)

    flat_scaled = first_scaled.reshape(tokens_here, width)
    flat_inverse = first_inverse.reshape(tokens_here, 1)
    first_gain_grad = jnp.sum(first_slope * flat_scaled, axis=0)
    first_shift_grad = jnp.sum(first_slope, axis=0)
    tokens_grad = (
        outer + first_sum_back + norm_back(first_slope, first_gain, flat_scaled, flat_inverse)
    )

    vectors = [
        first_gain_grad,
        first_shift_grad,
        joint_bias_grad[0],
        joint_bias_grad[1],
        mixer_bias_grad,
        second_gain_grad,
        second_shift_grad,
        expand_bias_grad,
        reduce_bias_grad,
    ]
    packed = sum_pairwise(jnp.concatenate(vectors).reshape(-1, 128), "ctx")
    if lax.axis_size("fsdp") == 4:
        packed = sum_pairwise(packed, "fsdp")
    else:
        packed = lax.psum(packed, "fsdp")
    packed = packed.reshape(-1)
    shares = []
    start = 0
    for vector in vectors:
        share = vector.shape[0] // lax.axis_size("fsdp")
        shares.append(lax.dynamic_slice_in_dim(packed, start + shard * share, share, 0))
        start += vector.shape[0]

    shape = (clips_here, rows_here, width)
    return (
        result.reshape(shape),
        tokens_grad.reshape(shape),
        shares[0],
        shares[1],
        joint_grad,
        jnp.stack([shares[2], shares[3]]),
        mixer_grad,
        shares[4],
        shares[5],
        shares[6],
        expand_grad,
        shares[7],
        reduce_grad,
        shares[8],
    )


def solution(mesh):
    return jax.shard_map(
        per_device,
        mesh=mesh,
        in_specs=(
            P("fsdp", "ctx", None),
            P("fsdp"),
            P("fsdp", "ctx", None),
            P(),
            P(),
            P("fsdp", None, "tp"),
            P(None, "tp"),
            P("fsdp", "tp"),
            P(),
            P(),
            P(),
            P("fsdp", "tp"),
            P("tp"),
            P("fsdp", "tp"),
            P(),
        ),
        out_specs=(
            P("fsdp", "ctx", None),
            P("fsdp", "ctx", None),
            P("fsdp"),
            P("fsdp"),
            P("fsdp", None, "tp"),
            P(None, ("tp", "fsdp")),
            P("fsdp", "tp"),
            P("fsdp"),
            P("fsdp"),
            P("fsdp"),
            P("fsdp", "tp"),
            P(("tp", "fsdp")),
            P("fsdp", "tp"),
            P("fsdp"),
        ),
        check_vma=False,
    )
```

time: 534 us -> 493 us (0.923)
  waiting for transfers between devices: 216 us -> 177 us
  local copies, waits for them, and re-layouts: 60.1 us -> 35.4 us
  Pallas kernels: 57.7 us -> 73.8 us
  between operations: 2.88 us -> 16.3 us
  other arithmetic: 49.1 us -> 62.3 us
  matrix products: 64.5 us -> 54.7 us
  starting transfers between devices: 75.9 us -> 68.6 us
    ppermute x80 -> x61, waiting for transfers between devices: 216 us -> 177 us  [swap(): return lax.ppermute(value, axis, [(i, i ^ distance) for i in range(size)])]
    pallas_call x1 -> x3, Pallas kernels: 20 us -> 38.6 us  [the longest x2 22.6 us: attention_forward(): pl.pallas_call(attention_forward_kernel, grid=(steps,), in_specs=[pl.Bloc...]
    dynamic_update_slice x19 -> x15, local copies, waits for them, and re-layouts: 21.1 us -> 3.4 us  [the longest x3 1.38 us: place_near(): out = lax.dynamic_update_slice(out, near, ((me ^ 1) * count, 0))]
    dot_general x24 -> x16, matrix products: 64.5 us -> 54.7 us  [product(): return lax.dot_general(left, right, dims, preferred_element_type=FULL)]
    ppermute x80 -> x61, starting transfers between devices: 75.9 us -> 68.4 us  [swap(): return lax.ppermute(value, axis, [(i, i ^ distance) for i in range(size)])]
    slice x25 -> x28, local copies, waits for them, and re-layouts: 7.54 us -> 13.3 us  [the longest x1 2.22 us: per_device(): to_right = (pieces[3][:, quarter:], swap(pieces[2][:, quarter:], 'ctx', 1))]
    pallas_call x1 -> x2, Pallas kernels: 37.7 us -> 35.2 us  [attention_backward(): pl.pallas_call(attention_backward_kernel, grid=(count // chunk,), in_spec...]
    unnamed x157 -> x243, local copies, waits for them, and re-layouts: 13.5 us -> 11.2 us
  transfers between devices with their start and end apart: 80 -> 64, of which waited for: 35 -> 22; matrix products, arithmetic and copies ran while one was open for 21% -> 24% of each run, Pallas kernels for 11% -> 12%
where the time goes in v2:
time: 493 us; the launch traced here: 488 us
  waiting for transfers between devices  177 us (36%)
  Pallas kernels  73.8 us (15%)
  starting transfers between devices  68.6 us (14%)
  other arithmetic  62.3 us (13%)
  matrix products  54.7 us (11%)
  local copies, waits for them, and re-layouts  35.4 us (7%)
  between operations  16.3 us (3%)
    ppermute x61, waiting for transfers between devices, swap(): return lax.ppermute(value, axis, [(i, i ^ distance) for i in range(size)])  177 us
    ppermute x61, starting transfers between devices, swap(): return lax.ppermute(value, axis, [(i, i ^ distance) for i in range(size)])  68.4 us
    dot_general x16, matrix products, product(): return lax.dot_general(left, right, dims, preferred_element_type=FULL)  54.7 us
    pallas_call x2, Pallas kernels, attention_backward(): pl.pallas_call(attention_backward_kernel, grid=(count // chunk,), in_spec...  35.2 us
    pallas_call x2, Pallas kernels, attention_forward(): pl.pallas_call(attention_forward_kernel, grid=(steps,), in_specs=[pl.Bloc...  22.6 us
    pallas_call x1, Pallas kernels, feed_forward(): pl.pallas_call(feed_forward_kernel, grid=(hidden // block,), in_specs=[wh...  16 us
    unnamed x243, local copies, waits for them, and re-layouts  11.2 us
  transfers between devices with their start and end apart: 64, of which 22 were waited for; matrix products, arithmetic and copies ran while one was open for 24% of the time, Pallas kernels for 12%

profile of v2, /device:TPU:0, one launch (start us, length us, event | category | flops | bytes accessed | tf_op | source)
XLA Modules:
  0.0 488.2 jit_solution(1122465618150239502)
XLA Ops:
  14.5 3.1 collective-permute-start
  23.5 14.6 %collective-permute-done.1 = bf16[392,256]{1,0:T(8,128)(2,1)S(1)} collective-permute-done((bf16[392,256]{1,0:T(8,128)(2,1)S(1)}, bf16[392,256]{1,0:T(8,128)(2,1)S(1)}, u32[]{:S(2)}, u32[]{:S(2)}) %collective-permute-start.1) | collective-permute-done | bytes 200736 | tf_op jit(solution)/shard_map/ppermute | solution.py:247
  44.3 5.4 %collective-permute-done.8 = bf16[128,768]{1,0:T(8,128)(2,1)S(1)} collective-permute-done((bf16[128,768]{1,0:T(8,128)(2,1)S(1)}, bf16[128,768]{1,0:T(8,128)(2,1)S(1)}, u32[]{:S(2)}, u32[]{:S(2)}) %collective-permute-start.8) | collective-permute-done | bytes 196640 | tf_op jit(solution)/shard_map/ppermute | solution.py:247
  54.8 11.0 %collective-permute-done.11 = bf16[256,512]{1,0:T(8,128)(2,1)S(1)} collective-permute-done((bf16[256,512]{1,0:T(8,128)(2,1)S(1)}, bf16[256,512]{1,0:T(8,128)(2,1)S(1)}, u32[]{:S(2)}, u32[]{:S(2)}) %collective-permute-start.11) | collective-permute-done | bytes 262176 | tf_op jit(solution)/shard_map/ppermute | solution.py:247
  70.8 22.6 %add_convert_fusion.q_ref.k_ref.v_ref = bf16[1568,768]{1,0:T(8,128)(2,1)S(1)} fusion(bf16[1024,768]{1,0:T(8,128)(2,1)S(1)} %pad_maximum_fusion.4, bf16[784,512]{1,0:T(8,128)(2,1)S(1)} %collective-permute-done.10, bf16[392,512]{1,0:T(8,128)(2,1)S(1)} %copy-done.83, bf16[392,512]{1,0:T(8,128)(2,1)S(1)} %get-tuple-element.284, ...), kind=kOutput, calls=%fused_computation.5 | convolution fusion | flops 2491138048 | bytes 7195648 | tf_op jit(solution)/shard_map/dot_general | solution.py:19
  93.5 11.2 %attention_forward.2 = (bf16[1568,128]{1,0:T(8,128)(2,1)S(1)}, f32[7,8,224]{2,1,0:T(8,128)S(1)}) custom-call(bf16[1568,768]{1,0:T(8,128)(2,1)S(1)} %add_convert_fusion.q_ref.k_ref.v_ref, bf16[1568,768]{1,0:T(8,128)(2,1)S(1)} %add_convert_fusion.q_ref.k_ref.v_ref, bf16[1568,768]{1,0:T(8,128)(2,1)S(1)} %add_convert_fusion.q_ref.k_ref.v_ref), custom_call_target="tpu_custom_call" | custom-call | flops 5035261952 | bytes 1605632 | tf_op jit(solution)/shard_map/attention_forward/pallas_call | solution.py:73
  109.5 11.4 %attention_forward.3 = (bf16[1568,128]{1,0:T(8,128)(2,1)S(1)}, f32[7,8,224]{2,1,0:T(8,128)S(1)}) custom-call(bf16[1568,768]{1,0:T(8,128)(2,1)S(1)} %add_convert_fusion.q_ref.k_ref.v_ref, bf16[1568,768]{1,0:T(8,128)(2,1)S(1)} %add_convert_fusion.q_ref.k_ref.v_ref, bf16[1568,768]{1,0:T(8,128)(2,1)S(1)} %add_convert_fusion.q_ref.k_ref.v_ref), custom_call_target="tpu_custom_call" | custom-call | flops 5035261952 | bytes 1605632 | tf_op jit(solution)/shard_map/attention_forward/pallas_call | solution.py:73
  132.4 3.7 collective-permute-done.23
  146.3 4.7 fusion.25
  156.7 16.0 %feed_forward.1 = (bf16[784,2048]{1,0:T(8,128)(2,1)}, bf16[784,2048]{1,0:T(8,128)(2,1)}, bf16[784,1024]{1,0:T(8,128)(2,1)S(1)}, f32[1,2048]{1,0:T(1,128)S(1)}) custom-call(bf16[784,1024]{1,0:T(8,128)(2,1)S(1)} %add_convert_fusion.3.normed_ref, bf16[784,1024]{1,0:T(8,128)(2,1)S(1)} %fusion.22.slope_ref, ...), custom_call_target="tpu_custom_call" | custom-call | flops 9865003008 | bytes 19628032 | tf_op jit(solution)/shard_map/feed_forward/pallas_call | solution.py:223
  173.2 3.2 convolution_convert_fusion.3
  184.0 6.5 %collective-permute-done.27 = bf16[128,2048]{1,0:T(8,128)(2,1)S(1)} collective-permute-done((bf16[128,2048]{1,0:T(8,128)(2,1)S(1)}, bf16[128,2048]{1,0:T(8,128)(2,1)S(1)}, u32[]{:S(2)}, u32[]{:S(2)}) %collective-permute-start.27) | collective-permute-done | bytes 524320 | tf_op jit(solution)/shard_map/ppermute | solution.py:247
  192.3 3.2 collective-permute-start.30
  197.3 4.8 convolution_convert_fusion
  207.8 3.3 fusion.48
  221.3 17.7 %attention_backward.2 = (bf16[1568,128]{1,0:T(8,128)(2,1)S(1)}, bf16[1568,128]{1,0:T(8,128)(2,1)S(1)}, bf16[1568,128]{1,0:T(8,128)(2,1)S(1)}) custom-call(bf16[1568,768]{1,0:T(8,128)(2,1)S(1)} %copy-done.6, bf16[1568,768]{1,0:T(8,128)(2,1)S(1)} %copy-done.6, bf16[1568,768]{1,0:T(8,128)(2,1)S(1)} %copy-done.6, ...), custom_call_target="tpu_custom_call" | custom-call | flops 12588154880 | bytes 3211264 | tf_op jit(solution)/shard_map/attention_backward/pallas_call | solution.py:158
  239.1 18.1 %collective-permute-done.35 = bf16[256,2048]{1,0:T(8,128)(2,1)S(1)} collective-permute-done((bf16[256,2048]{1,0:T(8,128)(2,1)S(1)}, bf16[256,2048]{1,0:T(8,128)(2,1)S(1)}, u32[]{:S(2)}, u32[]{:S(2)}) %collective-permute-start.35) | collective-permute-done | bytes 1048608 | tf_op jit(solution)/shard_map/ppermute | solution.py:247
  257.1 5.1 %collective-permute-done.36 = bf16[256,2048]{1,0:T(8,128)(2,1)S(1)} collective-permute-done((bf16[256,2048]{1,0:T(8,128)(2,1)S(1)}, bf16[256,2048]{1,0:T(8,128)(2,1)S(1)}, u32[]{:S(2)}, u32[]{:S(2)}) %collective-permute-start.36) | collective-permute-done | bytes 1048608 | tf_op jit(solution)/shard_map/ppermute | solution.py:247
  263.7 17.5 %attention_backward.3 = (bf16[1568,128]{1,0:T(8,128)(2,1)S(1)}, bf16[1568,128]{1,0:T(8,128)(2,1)S(1)}, bf16[1568,128]{1,0:T(8,128)(2,1)S(1)}) custom-call(bf16[1568,768]{1,0:T(8,128)(2,1)S(1)} %copy-done.6, bf16[1568,768]{1,0:T(8,128)(2,1)S(1)} %copy-done.6, bf16[1568,768]{1,0:T(8,128)(2,1)S(1)} %copy-done.6, ...), custom_call_target="tpu_custom_call" | custom-call | flops 12588154880 | bytes 3211264 | tf_op jit(solution)/shard_map/attention_backward/pallas_call | solution.py:158
  287.9 3.0 collective-permute-start.39
  294.4 8.5 %collective-permute-done.39 = bf16[64,2048]{1,0:T(8,128)(2,1)} collective-permute-done((bf16[64,2048]{1,0:T(8,128)(2,1)S(1)}, bf16[64,2048]{1,0:T(8,128)(2,1)}, u32[]{:S(2)}, u32[]{:S(2)}) %collective-permute-start.39) | collective-permute-done | bytes 262176 | tf_op jit(solution)/shard_map/ppermute | solution.py:247
  323.2 24.9 %collective-permute-done.42 = bf16[392,512]{1,0:T(8,128)(2,1)} collective-permute-done((bf16[392,512]{1,0:T(8,128)(2,1)}, bf16[392,512]{1,0:T(8,128)(2,1)}, u32[]{:S(2)}, u32[]{:S(2)}) %collective-permute-start.42) | collective-permute-done | bytes 401440 | tf_op jit(solution)/shard_map/ppermute | solution.py:247
  348.1 5.9 %convolution_convert_fusion.5 = bf16[784,1024]{1,0:T(8,128)(2,1)S(1)} fusion(bf16[784,2048]{1,0:T(8,128)(2,1)S(1)} %copy-done.24, bf16[1024,2048]{1,0:T(8,128)(2,1)} %constant_dynamic-update-slice_fusion.18.reduce_ref), kind=kOutput, calls=%fused_computation.68 | convolution fusion | flops 3289137152 | bytes 9011200 | tf_op jit(solution)/shard_map/dot_general | solution.py:19
  362.2 6.1 %collective-permute-done.46 = bf16[392,256]{1,0:T(8,128)(2,1)S(1)} collective-permute-done((bf16[392,256]{1,0:T(8,128)(2,1)S(1)}, bf16[392,256]{1,0:T(8,128)(2,1)S(1)}, u32[]{:S(2)}, u32[]{:S(2)}) %collective-permute-start.46) | collective-permute-done | bytes 200736 | tf_op jit(solution)/shard_map/ppermute | solution.py:247
  368.3 20.1 %collective-permute-done.45 = bf16[392,256]{1,0:T(8,128)(2,1)S(1)} collective-permute-done((bf16[392,256]{1,0:T(8,128)(2,1)S(1)}, bf16[392,256]{1,0:T(8,128)(2,1)S(1)}, u32[]{:S(2)}, u32[]{:S(2)}) %collective-permute-start.45) | collective-permute-done | bytes 200736 | tf_op jit(solution)/shard_map/ppermute | solution.py:247
  389.6 2.9 collective-permute-start.59
  395.4 27.8 %collective-permute-done.59 = bf16[64,2048]{1,0:T(8,128)(2,1)S(1)} collective-permute-done((bf16[64,2048]{1,0:T(8,128)(2,1)S(1)}, bf16[64,2048]{1,0:T(8,128)(2,1)S(1)}, u32[]{:S(2)}, u32[]{:S(2)}) %collective-permute-start.59) | collective-permute-done | bytes 262176 | tf_op jit(solution)/shard_map/ppermute | solution.py:247
  426.3 5.5 %add_convert_fusion.1 = bf16[784,1024]{1,0:T(8,128)(2,1)} fusion(bf16[784,1024]{1,0:T(8,128)(2,1)S(1)} %collective-permute-done.49, bf16[784,1024]{1,0:T(8,128)(2,1)S(1)} %convolution_convert_fusion.5, bf16[784,1024]{1,0:T(8,128)(2,1)} %collective-permute-done.25, bf16[784,1024]{1,0:T(8,128)(2,1)} %convolution_convert_fusion.4, f32[1024]{0:T(1024)S(1)} %copy-done.104, ...), kind=kLoop, calls=%fused_computation.46 | loop fusion | flops 10436608 | bytes 9645120 | tf_op jit(solution)/shard_map/convert_element_type | solution.py:578
  431.7 14.6 %collective-permute-done.58 = bf16[256,768]{1,0:T(8,128)(2,1)S(1)} collective-permute-done((bf16[256,768]{1,0:T(8,128)(2,1)S(1)}, bf16[256,768]{1,0:T(8,128)(2,1)S(1)}, u32[]{:S(2)}, u32[]{:S(2)}) %collective-permute-start.58) | collective-permute-done | bytes 393248 | tf_op jit(solution)/shard_map/ppermute | solution.py:247
  451.1 3.3 fusion.32
  457.3 4.6 convert_reduce_fusion.1
  472.3 4.7 fusion.5
  (503 shorter events, 157.1 us)
Async XLA Ops:
  7.2 114.8 %all-gather.2.cloned.1.call-start = ((), (), s32[]{:S(2)}) async-start(), calls=%async_computation.1 | async-start | bytes 5242880 | tf_op jit(solution)/shard_map/all_gather | solution.py:386
  7.9 294.9 %reduce-scatter.2.cloned.1.call-start = ((), (), s32[]{:S(2)}) async-start(), calls=%async_computation.2 | async-start | bytes 6553600 | tf_op jit(solution)/shard_map/reduce_scatter | solution.py:520
  14.5 24.2 %collective-permute-start = (bf16[392,512]{1,0:T(8,128)(2,1)S(1)}, bf16[392,512]{1,0:T(8,128)(2,1)S(1)}, u32[]{:S(2)}, u32[]{:S(2)}) collective-permute-start(bf16[392,512]{1,0:T(8,128)(2,1)S(1)} %get-tuple-element.130), channel_id=1, source_target_pairs={{0,2},{2,0},{4,6},{6,4},{1,3},{3,1},{5,7},{7,5},{8,10},{10,8},{12,... | collective-permute-start | bytes 1204232 | tf_op jit(solution)/shard_map/ppermute | solution.py:247
  17.6 20.4 %collective-permute-start.3 = (bf16[256,768]{1,0:T(8,128)(2,1)S(1)}, bf16[256,768]{1,0:T(8,128)(2,1)S(1)}, u32[]{:S(2)}, u32[]{:S(2)}) collective-permute-start(bf16[256,768]{1,0:T(8,128)(2,1)S(1)} %pad_maximum_fusion.15), channel_id=1, source_target_pairs={{0,8},{8,0},{16,24},{24,16},{1,9},{9,1},{17,25},{25,17},{2,10},{10... | collective-permute-start | bytes 1179656 | tf_op jit(solution)/shard_map/ppermute | solution.py:247
  19.1 19.0 %collective-permute-start.4 = (bf16[256,768]{1,0:T(8,128)(2,1)S(1)}, bf16[256,768]{1,0:T(8,128)(2,1)S(1)}, u32[]{:S(2)}, u32[]{:S(2)}) collective-permute-start(bf16[256,768]{1,0:T(8,128)(2,1)S(1)} %pad_maximum_fusion.15), channel_id=1, source_target_pairs={{0,16},{8,24},{16,0},{24,8},{1,17},{9,25},{17,1},{25,9},{2,18},{10... | collective-permute-start | bytes 1179656 | tf_op jit(solution)/shard_map/ppermute | solution.py:247
  20.6 17.4 %collective-permute-start.1 = (bf16[392,256]{1,0:T(8,128)(2,1)S(1)}, bf16[392,256]{1,0:T(8,128)(2,1)S(1)}, u32[]{:S(2)}, u32[]{:S(2)}) collective-permute-start(bf16[392,256]{1,0:T(8,128)(2,1)S(1)} %get-tuple-element.131), channel_id=1, source_target_pairs={{0,4},{2,6},{4,0},{6,2},{1,5},{3,7},{5,1},{7,3},{8,12},{10,14},{12... | collective-permute-start | bytes 602120 | tf_op jit(solution)/shard_map/ppermute | solution.py:247
  23.2 14.8 %collective-permute-start.2 = (bf16[392,256]{1,0:T(8,128)(2,1)S(1)}, bf16[392,256]{1,0:T(8,128)(2,1)S(1)}, u32[]{:S(2)}, u32[]{:S(2)}) collective-permute-start(bf16[392,256]{1,0:T(8,128)(2,1)S(1)} %get-tuple-element.132), channel_id=1, source_target_pairs={{0,6},{2,4},{4,2},{6,0},{1,7},{3,5},{5,3},{7,1},{8,14},{10,12},{12... | collective-permute-start | bytes 602120 | tf_op jit(solution)/shard_map/ppermute | solution.py:247
  66.5 54.5 %collective-permute-start.18 = (bf16[256,2048]{1,0:T(8,128)(2,1)S(1)}, bf16[256,2048]{1,0:T(8,128)(2,1)}, u32[]{:S(2)}, u32[]{:S(2)}) collective-permute-start(bf16[256,2048]{1,0:T(8,128)(2,1)S(1)} %copy-done.51), channel_id=1, source_target_pairs={{0,8},{8,0},{16,24},{24,16},{1,9},{9,1},{17,25},{25,17},{2,10},{10... | collective-permute-start | bytes 3145736 | tf_op jit(solution)/shard_map/ppermute | solution.py:247
  67.8 54.2 %collective-permute-start.19 = (bf16[256,2048]{1,0:T(8,128)(2,1)S(1)}, bf16[256,2048]{1,0:T(8,128)(2,1)S(1)}, u32[]{:S(2)}, u32[]{:S(2)}) collective-permute-start(bf16[256,2048]{1,0:T(8,128)(2,1)S(1)} %copy-done.51), channel_id=1, source_target_pairs={{0,16},{8,24},{16,0},{24,8},{1,17},{9,25},{17,1},{25,9},{2,18},{10... | collective-permute-start | bytes 3145736 | tf_op jit(solution)/shard_map/ppermute | solution.py:247
  69.1 35.6 %collective-permute-start.13 = (bf16[128,512]{1,0:T(8,128)(2,1)S(1)}, bf16[128,512]{1,0:T(8,128)(2,1)S(1)}, u32[]{:S(2)}, u32[]{:S(2)}) collective-permute-start(bf16[128,512]{1,0:T(8,128)(2,1)S(1)} %slice.216), channel_id=1, source_target_pairs={{0,8},{8,0},{16,24},{24,16},{1,9},{9,1},{17,25},{25,17},{2,10},{10... | collective-permute-start | bytes 393224 | tf_op jit(solution)/shard_map/ppermute | solution.py:247
  69.5 35.2 %collective-permute-start.14 = (bf16[128,512]{1,0:T(8,128)(2,1)S(1)}, bf16[128,512]{1,0:T(8,128)(2,1)S(1)}, u32[]{:S(2)}, u32[]{:S(2)}) collective-permute-start(bf16[128,512]{1,0:T(8,128)(2,1)S(1)} %slice.217), channel_id=1, source_target_pairs={{0,16},{8,24},{16,0},{24,8},{1,17},{9,25},{17,1},{25,9},{2,18},{10... | collective-permute-start | bytes 393224 | tf_op jit(solution)/shard_map/ppermute | solution.py:247
  104.7 16.2 %collective-permute-start.15 = (bf16[392,128]{1,0:T(8,128)(2,1)S(1)}, bf16[392,128]{1,0:T(8,128)(2,1)S(1)}, u32[]{:S(2)}, u32[]{:S(2)}) collective-permute-start(bf16[392,128]{1,0:T(8,128)(2,1)S(1)} %get-tuple-element.311), channel_id=1, source_target_pairs={{0,2},{2,0},{4,6},{6,4},{1,3},{3,1},{5,7},{7,5},{8,10},{10,8},{12,... | collective-permute-start | bytes 301064 | tf_op jit(solution)/shard_map/ppermute | solution.py:247
  191.5 15.3 %collective-permute-start.29 = (bf16[392,128]{1,0:T(8,128)(2,1)}, bf16[392,128]{1,0:T(8,128)(2,1)}, u32[]{:S(2)}, u32[]{:S(2)}) collective-permute-start(bf16[392,128]{1,0:T(8,128)(2,1)} %slice.275), channel_id=1, source_target_pairs={{0,2},{2,0},{4,6},{6,4},{1,3},{3,1},{5,7},{7,5},{8,10},{10,8},{12,... | collective-permute-start | bytes 301064 | tf_op jit(solution)/shard_map/ppermute | solution.py:247
  192.3 14.5 %collective-permute-start.30 = (bf16[392,128]{1,0:T(8,128)(2,1)}, bf16[392,128]{1,0:T(8,128)(2,1)}, u32[]{:S(2)}, u32[]{:S(2)}) collective-permute-start(bf16[392,128]{1,0:T(8,128)(2,1)} %slice.278), channel_id=1, source_target_pairs={{0,4},{2,6},{4,0},{6,2},{1,5},{3,7},{5,1},{7,3},{8,12},{10,14},{12... | collective-permute-start | bytes 301064 | tf_op jit(solution)/shard_map/ppermute | solution.py:247
  206.9 250.4 %all-reduce.2.cloned.1.call-start = ((), (), s32[]{:S(2)}) async-start(), calls=%async_computation.3 | async-start | bytes 2621440 | tf_op jit(solution)/shard_map/psum | solution.py:546
  211.4 45.8 %collective-permute-start.35 = (bf16[256,2048]{1,0:T(8,128)(2,1)S(1)}, bf16[256,2048]{1,0:T(8,128)(2,1)S(1)}, u32[]{:S(2)}, u32[]{:S(2)}) collective-permute-start(bf16[256,2048]{1,0:T(8,128)(2,1)S(1)} %pad_maximum_fusion.5), channel_id=1, source_target_pairs={{0,8},{8,0},{16,24},{24,16},{1,9},{9,1},{17,25},{25,17},{2,10},{10... | collective-permute-start | bytes 3145736 | tf_op jit(solution)/shard_map/ppermute | solution.py:247
  214.8 47.4 %collective-permute-start.36 = (bf16[256,2048]{1,0:T(8,128)(2,1)S(1)}, bf16[256,2048]{1,0:T(8,128)(2,1)S(1)}, u32[]{:S(2)}, u32[]{:S(2)}) collective-permute-start(bf16[256,2048]{1,0:T(8,128)(2,1)S(1)} %pad_maximum_fusion.6), channel_id=1, source_target_pairs={{0,16},{8,24},{16,0},{24,8},{1,17},{9,25},{17,1},{25,9},{2,18},{10... | collective-permute-start | bytes 3145736 | tf_op jit(solution)/shard_map/ppermute | solution.py:247
  215.7 23.4 %collective-permute-start.32 = (bf16[392,128]{1,0:T(8,128)(2,1)S(1)}, bf16[392,128]{1,0:T(8,128)(2,1)S(1)}, u32[]{:S(2)}, u32[]{:S(2)}) collective-permute-start(bf16[392,128]{1,0:T(8,128)(2,1)S(1)} %slice.241), channel_id=1, source_target_pairs={{0,2},{2,0},{4,6},{6,4},{1,3},{3,1},{5,7},{7,5},{8,10},{10,8},{12,... | collective-permute-start | bytes 301064 | tf_op jit(solution)/shard_map/ppermute | solution.py:247
  215.8 23.3 %collective-permute-start.33 = (bf16[392,128]{1,0:T(8,128)(2,1)S(1)}, bf16[392,128]{1,0:T(8,128)(2,1)S(1)}, u32[]{:S(2)}, u32[]{:S(2)}) collective-permute-start(bf16[392,128]{1,0:T(8,128)(2,1)S(1)} %slice.242), channel_id=1, source_target_pairs={{0,4},{2,6},{4,0},{6,2},{1,5},{3,7},{5,1},{7,3},{8,12},{10,14},{12... | collective-permute-start | bytes 301064 | tf_op jit(solution)/shard_map/ppermute | solution.py:247
  218.6 20.5 %collective-permute-start.34 = (bf16[392,128]{1,0:T(8,128)(2,1)S(1)}, bf16[392,128]{1,0:T(8,128)(2,1)S(1)}, u32[]{:S(2)}, u32[]{:S(2)}) collective-permute-start(bf16[392,128]{1,0:T(8,128)(2,1)S(1)} %slice.243), channel_id=1, source_target_pairs={{0,6},{2,4},{4,2},{6,0},{1,7},{3,5},{5,3},{7,1},{8,14},{10,12},{12... | collective-permute-start | bytes 301064 | tf_op jit(solution)/shard_map/ppermute | solution.py:247
  263.6 17.8 %collective-permute-start.37 = (bf16[128,2048]{1,0:T(8,128)(2,1)S(1)}, bf16[128,2048]{1,0:T(8,128)(2,1)S(1)}, u32[]{:S(2)}, u32[]{:S(2)}) collective-permute-start(bf16[128,2048]{1,0:T(8,128)(2,1)S(1)} %dynamic-slice_convert_fusion), channel_id=1, source_target_pairs={{0,2},{2,0},{4,6},{6,4},{1,3},{3,1},{5,7},{7,5},{8,10},{10,8},{12,... | collective-permute-start | bytes 1572872 | tf_op jit(solution)/shard_map/ppermute | solution.py:247
  287.9 15.0 %collective-permute-start.39 = (bf16[64,2048]{1,0:T(8,128)(2,1)S(1)}, bf16[64,2048]{1,0:T(8,128)(2,1)}, u32[]{:S(2)}, u32[]{:S(2)}) collective-permute-start(bf16[64,2048]{1,0:T(8,128)(2,1)S(1)} %dynamic-slice_convert_fusion.1), channel_id=1, source_target_pairs={{0,4},{2,6},{4,0},{6,2},{1,5},{3,7},{5,1},{7,3},{8,12},{10,14},{12... | collective-permute-start | bytes 786440 | tf_op jit(solution)/shard_map/ppermute | solution.py:247
  312.7 35.4 %collective-permute-start.42 = (bf16[392,512]{1,0:T(8,128)(2,1)}, bf16[392,512]{1,0:T(8,128)(2,1)}, u32[]{:S(2)}, u32[]{:S(2)}) collective-permute-start(bf16[392,512]{1,0:T(8,128)(2,1)} %get-tuple-element.278), channel_id=1, source_target_pairs={{0,2},{2,0},{4,6},{6,4},{1,3},{3,1},{5,7},{7,5},{8,10},{10,8},{12,... | collective-permute-start | bytes 1204232 | tf_op jit(solution)/shard_map/ppermute | solution.py:247
  354.0 34.4 %collective-permute-start.49 = (bf16[784,1024]{1,0:T(8,128)(2,1)S(1)}, bf16[784,1024]{1,0:T(8,128)(2,1)S(1)}, u32[]{:S(2)}, u32[]{:S(2)}) collective-permute-start(bf16[784,1024]{1,0:T(8,128)(2,1)S(1)} %convolution_convert_fusion.5), channel_id=1, source_target_pairs={{0,1},{1,0},{2,3},{3,2},{4,5},{5,4},{6,7},{7,6},{8,9},{9,8},{10,11... | collective-permute-start | bytes 4816904 | tf_op jit(solution)/shard_map/ppermute | solution.py:247
  357.6 30.9 %collective-permute-start.47 = (bf16[256,768]{1,0:T(8,128)(2,1)S(1)}, bf16[256,768]{1,0:T(8,128)(2,1)S(1)}, u32[]{:S(2)}, u32[]{:S(2)}) collective-permute-start(bf16[256,768]{1,0:T(8,128)(2,1)S(1)} %pad_maximum_fusion.16), channel_id=1, source_target_pairs={{0,8},{8,0},{16,24},{24,16},{1,9},{9,1},{17,25},{25,17},{2,10},{10... | collective-permute-start | bytes 1179656 | tf_op jit(solution)/shard_map/ppermute | solution.py:247
  360.1 28.4 %collective-permute-start.48 = (bf16[256,768]{1,0:T(8,128)(2,1)S(1)}, bf16[256,768]{1,0:T(8,128)(2,1)S(1)}, u32[]{:S(2)}, u32[]{:S(2)}) collective-permute-start(bf16[256,768]{1,0:T(8,128)(2,1)S(1)} %pad_maximum_fusion.17), channel_id=1, source_target_pairs={{0,16},{8,24},{16,0},{24,8},{1,17},{9,25},{17,1},{25,9},{2,18},{10... | collective-permute-start | bytes 1179656 | tf_op jit(solution)/shard_map/ppermute | solution.py:247
  362.1 26.3 %collective-permute-start.45 = (bf16[392,256]{1,0:T(8,128)(2,1)S(1)}, bf16[392,256]{1,0:T(8,128)(2,1)S(1)}, u32[]{:S(2)}, u32[]{:S(2)}) collective-permute-start(bf16[392,256]{1,0:T(8,128)(2,1)S(1)} %add_convert_fusion.9), channel_id=1, source_target_pairs={{0,4},{2,6},{4,0},{6,2},{1,5},{3,7},{5,1},{7,3},{8,12},{10,14},{12... | collective-permute-start | bytes 602120 | tf_op jit(solution)/shard_map/ppermute | solution.py:247
  389.5 34.6 %collective-permute-start.57 = (bf16[256,768]{1,0:T(8,128)(2,1)S(1)}, bf16[256,768]{1,0:T(8,128)(2,1)S(1)}, u32[]{:S(2)}, u32[]{:S(2)}) collective-permute-start(bf16[256,768]{1,0:T(8,128)(2,1)S(1)} %fusion.29), channel_id=1, source_target_pairs={{0,4},{2,6},{4,0},{6,2},{1,5},{3,7},{5,1},{7,3},{8,12},{10,14},{12... | collective-permute-start | bytes 1179656 | tf_op jit(solution)/shard_map/ppermute | solution.py:247
  389.6 33.6 %collective-permute-start.59 = (bf16[64,2048]{1,0:T(8,128)(2,1)S(1)}, bf16[64,2048]{1,0:T(8,128)(2,1)S(1)}, u32[]{:S(2)}, u32[]{:S(2)}) collective-permute-start(bf16[64,2048]{1,0:T(8,128)(2,1)S(1)} %add_convert_fusion.7), channel_id=1, source_target_pairs={{0,4},{2,6},{4,0},{6,2},{1,5},{3,7},{5,1},{7,3},{8,12},{10,14},{12... | collective-permute-start | bytes 786440 | tf_op jit(solution)/shard_map/ppermute | solution.py:247
  395.4 59.0 %collective-permute-start.50 = (bf16[784,512]{1,0:T(8,128)(2,1)}, bf16[784,512]{1,0:T(8,128)(2,1)}, u32[]{:S(2)}, u32[]{:S(2)}) collective-permute-start(bf16[784,512]{1,0:T(8,128)(2,1)} %pad_maximum_fusion.9), channel_id=1, source_target_pairs={{0,1},{1,0},{2,3},{3,2},{4,5},{5,4},{6,7},{7,6},{8,9},{9,8},{10,11... | collective-permute-start | bytes 2408456 | tf_op jit(solution)/shard_map/ppermute | solution.py:247
  424.1 27.1 %collective-permute-start.60 = (bf16[128,2048]{1,0:T(8,128)(2,1)}, bf16[128,2048]{1,0:T(8,128)(2,1)}, u32[]{:S(2)}, u32[]{:S(2)}) collective-permute-start(bf16[128,2048]{1,0:T(8,128)(2,1)} %maximum_select_fusion.1), channel_id=1, source_target_pairs={{0,2},{2,0},{4,6},{6,4},{1,3},{3,1},{5,7},{7,5},{8,10},{10,8},{12,... | collective-permute-start | bytes 1572872 | tf_op jit(solution)/shard_map/ppermute | solution.py:247
  424.2 22.2 %collective-permute-start.58 = (bf16[256,768]{1,0:T(8,128)(2,1)S(1)}, bf16[256,768]{1,0:T(8,128)(2,1)S(1)}, u32[]{:S(2)}, u32[]{:S(2)}) collective-permute-start(bf16[256,768]{1,0:T(8,128)(2,1)S(1)} %add_convert_fusion.6), channel_id=1, source_target_pairs={{0,2},{2,0},{4,6},{6,4},{1,3},{3,1},{5,7},{7,5},{8,10},{10,8},{12,... | collective-permute-start | bytes 1179656 | tf_op jit(solution)/shard_map/ppermute | solution.py:247
  (144 other events, 1365.1 us)
Sparse Core Ops, SparseCore 0:
  9.9 74.7 all-gather.1
  207.0 82.8 reduce-scatter.1
  318.0 94.9 all-reduce.1

commit v3 on v2

v3 whole, which is shorter than its diff:
```python
import jax
import jax.numpy as jnp
from jax import lax
from jax.experimental import pallas as pl
from jax.experimental.pallas import tpu as pltpu
from jax.sharding import PartitionSpec as P

HEAD_DIM = 64
EPSILON = 1e-06
LOW = jnp.bfloat16
FULL = jnp.float32

ROW_BY_ROW = (((1,), (1,)), ((), ()))
PLAIN = (((1,), (0,)), ((), ()))
COLUMN_BY_COLUMN = (((0,), (0,)), ((), ()))


def product(left, right, dims):
    return lax.dot_general(left, right, dims, preferred_element_type=FULL)


def normalize(value_rows):
    center = value_rows - jnp.mean(value_rows, axis=-1, keepdims=True)
    inverse = lax.rsqrt(jnp.mean(center * center, axis=-1, keepdims=True) + EPSILON)
    return (center * inverse, inverse)


def norm_back(upstream, gain, scaled, inverse):
    weighted = upstream * gain
    return inverse * (
        weighted
        - jnp.mean(weighted, axis=-1, keepdims=True)
        - scaled * jnp.mean(weighted * scaled, axis=-1, keepdims=True)
    )


def row_chunk(count, most):
    for chunk in range(most, 0, -16):
        if count % chunk == 0:
            return chunk
    raise ValueError("rows")


def first_norm_kernel(tokens_ref, gain_ref, shift_ref, out_ref):
    scaled, _ = normalize(tokens_ref[...].astype(FULL))
    out_ref[...] = (scaled * gain_ref[...] + shift_ref[...]).astype(LOW)


def second_norm_kernel(tokens_ref, one_ref, two_ref, bias_ref, gain_ref, shift_ref, out_ref):
    mixed = one_ref[...].astype(FULL) + two_ref[...].astype(FULL) + bias_ref[...]
    scaled, _ = normalize(tokens_ref[...].astype(FULL) + mixed)
    out_ref[...] = (scaled * gain_ref[...] + shift_ref[...]).astype(LOW)


def add_sums(ref, rows):
    sums = jnp.concatenate([jnp.sum(row, axis=0, keepdims=True) for row in rows], axis=0)

    @pl.when(pl.program_id(0) == 0)
    def _():
        ref[: len(rows)] = sums

    @pl.when(pl.program_id(0) > 0)
    def _():
        ref[: len(rows)] += sums


def second_norm_back_kernel(
    tokens_ref, one_ref, two_ref, bias_ref, gain_ref, left_ref, right_ref, outer_ref,
    slope_ref, back_ref, sums_ref,
):
    mixed = one_ref[...].astype(FULL) + two_ref[...].astype(FULL) + bias_ref[...]
    scaled, inverse = normalize(tokens_ref[...].astype(FULL) + mixed)
    upstream = left_ref[...].astype(FULL) + right_ref[...].astype(FULL)
    back = norm_back(upstream, gain_ref[...], scaled, inverse)
    slope = (outer_ref[...].astype(FULL) + back).astype(LOW)
    slope_ref[...] = slope
    back_ref[...] = back
    add_sums(sums_ref, [upstream * scaled, upstream, slope.astype(FULL)])


def first_norm_back_kernel(
    tokens_ref, upstream_ref, gain_ref, outer_ref, back_ref, out_ref, sums_ref
):
    scaled, inverse = normalize(tokens_ref[...].astype(FULL))
    upstream = upstream_ref[...].astype(FULL)
    back = norm_back(upstream, gain_ref[...], scaled, inverse)
    out_ref[...] = outer_ref[...].astype(FULL) + back_ref[...] + back
    add_sums(sums_ref, [upstream * scaled, upstream])


def by_rows(kernel, name, out_types, sums, *values):
    count, width = values[0].shape
    chunk = row_chunk(count, 112)
    part = pl.BlockSpec((chunk, width), lambda i: (i, 0))
    in_specs = [
        part if value.shape[0] == count else pl.BlockSpec((1, width), lambda i: (0, 0))
        for value in values
    ]
    out_specs = [part for _ in out_types]
    out_shape = [jax.ShapeDtypeStruct((count, width), kind) for kind in out_types]
    if sums:
        out_specs.append(pl.BlockSpec((8, width), lambda i: (0, 0)))
        out_shape.append(jax.ShapeDtypeStruct((8, width), FULL))
    return pl.pallas_call(
        kernel,
        grid=(count // chunk,),
        in_specs=in_specs,
        out_specs=out_specs,
        out_shape=out_shape,
        compiler_params=pltpu.CompilerParams(vmem_limit_bytes=32 << 20),
        name=name,
    )(*values)


def joint_kernel(mine_ref, other_ref, weight_ref, bias_ref, out_ref):
    half = mine_ref.shape[1]
    out = product(mine_ref[...], weight_ref[:half], PLAIN)
    out += product(other_ref[...], weight_ref[half:], PLAIN)
    out_ref[...] = (out + bias_ref[...]).astype(LOW)


def joint_projection(mine, other, weight, bias):
    count, half = mine.shape
    columns = weight.shape[1]
    chunk = row_chunk(count, 784)
    part = pl.BlockSpec((chunk, half), lambda i: (i, 0))
    return pl.pallas_call(
        joint_kernel,
        grid=(count // chunk,),
        in_specs=[
            part,
            part,
            pl.BlockSpec(weight.shape, lambda i: (0, 0)),
            pl.BlockSpec((1, columns), lambda i: (0, 0)),
        ],
        out_specs=pl.BlockSpec((chunk, columns), lambda i: (i, 0)),
        out_shape=jax.ShapeDtypeStruct((count, columns), LOW),
        compiler_params=pltpu.CompilerParams(vmem_limit_bytes=40 << 20),
        name="joint_projection",
    )(mine, other, weight, bias)


def rows_kernel(left_ref, right_ref, out_ref):
    out_ref[...] = product(left_ref[...], right_ref[...], ROW_BY_ROW).astype(LOW)


def rows_product(left, right, name):
    count, depth = left.shape
    columns = right.shape[0]
    chunk = row_chunk(count, 400)
    return pl.pallas_call(
        rows_kernel,
        grid=(count // chunk,),
        in_specs=[
            pl.BlockSpec((chunk, depth), lambda i: (i, 0)),
            pl.BlockSpec((columns, depth), lambda i: (0, 0)),
        ],
        out_specs=pl.BlockSpec((chunk, columns), lambda i: (i, 0)),
        out_shape=jax.ShapeDtypeStruct((count, columns), LOW),
        compiler_params=pltpu.CompilerParams(vmem_limit_bytes=48 << 20),
        name=name,
    )(left, right)


def grad_kernel(distances, place_ref, *refs):
    lefts, (right_ref, out_ref, turned) = refs[:-3], refs[-3:]

    @pl.when(pl.program_id(1) == 0)
    def _():
        left = lefts[0][...]
        if len(lefts) == 2:
            slot = place_ref[0] ^ distance_at(distances, pl.program_id(0))
            left = jnp.where((slot >> 1) == 0, left, lefts[1][...])
        turned[...] = left.T

    out_ref[0] = product(turned[...], right_ref[...], PLAIN).astype(LOW)


def distance_at(distances, step):
    if len(distances) == 1:
        return distances[0]
    return distances[0] + step * (distances[1] - distances[0])


def grad_products(lefts, right, place, distances, name):
    tokens_here, columns = right.shape
    quarter = sum(left.shape[1] for left in lefts) // 4
    blocks = lefts[0].shape[1] // quarter
    width = 512 if columns % 512 == 0 else columns // 2 if columns % 256 == 0 else columns

    def left_at(i, j, place):
        return (0, (place[0] ^ distance_at(distances, i)) & (blocks - 1))

    return pl.pallas_call(
        lambda *refs: grad_kernel(distances, *refs),
        grid_spec=pltpu.PrefetchScalarGridSpec(
            num_scalar_prefetch=1,
            grid=(len(distances), columns // width),
            in_specs=[pl.BlockSpec((tokens_here, quarter), left_at) for _ in lefts]
            + [pl.BlockSpec((tokens_here, width), lambda i, j, place: (0, j))],
            out_specs=pl.BlockSpec((1, quarter, width), lambda i, j, place: (i, 0, j)),
            scratch_shapes=[pltpu.VMEM((quarter, tokens_here), LOW)],
        ),
        out_shape=jax.ShapeDtypeStruct((len(distances), quarter, columns), LOW),
        compiler_params=pltpu.CompilerParams(vmem_limit_bytes=48 << 20),
        name=name,
    )(place.astype(jnp.int32).reshape(1), *lefts, right)


def attention_forward_kernel(q_ref, k_ref, v_ref, o_ref, lse_ref):
    rows, width = q_ref.shape
    lane = lax.broadcasted_iota(jnp.int32, (rows, width), 1)
    lse = jnp.zeros((rows, width), FULL)
    q = q_ref[...] * jnp.asarray(HEAD_DIM ** (-0.5), LOW)
    k = k_ref[...]
    v = v_ref[...]
    out = None
    for head in range(width // HEAD_DIM):
        mask = (lane // HEAD_DIM) == head
        scores = product(jnp.where(mask, q, jnp.zeros_like(q)), k, ROW_BY_ROW)
        top = jnp.max(scores, axis=-1, keepdims=True)
        weights = jnp.exp(scores - top)
        total = jnp.sum(weights, axis=-1, keepdims=True)
        part = product(weights.astype(LOW), v, PLAIN) / total
        out = part if out is None else jnp.where(mask, part, out)
        lse = jnp.where(lane == head, top + jnp.log(total), lse)
    o_ref[...] = out.astype(LOW)
    lse_ref[0] = lse.T[: lse_ref.shape[1]]


def attention_forward(joint, pair):
    count, columns = joint.shape
    width = 2 * HEAD_DIM
    chunk = row_chunk(count, 256)
    steps = count // chunk
    kind = columns // (3 * width)
    whole_k = pl.BlockSpec((count, width), lambda i: (0, kind + pair))
    whole_v = pl.BlockSpec((count, width), lambda i: (0, 2 * kind + pair))
    out, lse = pl.pallas_call(
        attention_forward_kernel,
        grid=(steps,),
        in_specs=[pl.BlockSpec((chunk, width), lambda i: (i, pair)), whole_k, whole_v],
        out_specs=[
            pl.BlockSpec((chunk, width), lambda i: (i, 0)),
            pl.BlockSpec((1, 8, chunk), lambda i: (i, 0, 0)),
        ],
        out_shape=[
            jax.ShapeDtypeStruct((count, width), LOW),
            jax.ShapeDtypeStruct((steps, 8, chunk), FULL),
        ],
        compiler_params=pltpu.CompilerParams(vmem_limit_bytes=40 << 20),
        name="attention_forward",
    )(joint, joint, joint)
    return out, lse.transpose(1, 0, 2).reshape(8, count)


def attention_backward_kernel(
    q_ref, k_ref, v_ref, da_ref, o_ref, lse_ref, dq_ref, dk_ref, dv_ref,
    q_heads, da_heads, delta_ref, dq_total,
):
    count, width = q_ref.shape
    chunk = k_ref.shape[0]
    step = pl.program_id(0)
    heads = width // HEAD_DIM
    scale = jnp.asarray(HEAD_DIM ** (-0.5), LOW)

    @pl.when(step == 0)
    def _():
        lane = lax.broadcasted_iota(jnp.int32, (count, width), 1)
        delta = jnp.zeros((count, width), FULL)
        q = q_ref[...] * scale
        da = da_ref[...]
        both = da.astype(FULL) * o_ref[...].astype(FULL)
        for head in range(heads):
            mask = (lane // HEAD_DIM) == head
            q_heads[head] = jnp.where(mask, q, jnp.zeros_like(q))
            da_heads[head] = jnp.where(mask, da, jnp.zeros_like(da))
            row = jnp.sum(jnp.where(mask, both, 0.0), axis=-1, keepdims=True)
            delta = jnp.where(lane == head, row, delta)
        delta_ref[...] = delta.T[:8]
        dq_total[...] = jnp.zeros_like(dq_total)

    lane = lax.broadcasted_iota(jnp.int32, (chunk, width), 1)
    k = k_ref[...]
    v = v_ref[...]
    scaled_k = k * scale
    dk = dv = None
    for head in range(heads):
        q = q_heads[head]
        da = da_heads[head]
        probs = jnp.exp(product(k, q, ROW_BY_ROW) - lse_ref[head : head + 1, :])
        slope = probs * (product(v, da, ROW_BY_ROW) - delta_ref[head : head + 1, :])
        slope = slope.astype(LOW)
        dv_part = product(probs.astype(LOW), da, PLAIN)
        dk_part = product(slope, q, PLAIN)
        dv = dv_part if dv is None else dv + dv_part
        dk = dk_part if dk is None else dk + dk_part
        one_k = jnp.where((lane // HEAD_DIM) == head, scaled_k, jnp.zeros_like(k))
        dq_total[...] += product(slope, one_k, COLUMN_BY_COLUMN)
    dk_ref[...] = dk.astype(LOW)
    dv_ref[...] = dv.astype(LOW)

    @pl.when(step == pl.num_programs(0) - 1)
    def _():
        dq_ref[...] = dq_total[...].astype(LOW)


def attention_backward(joint, da, out, lse, pair):
    count, columns = joint.shape
    width = 2 * HEAD_DIM
    chunk = row_chunk(count, 256)
    kind = columns // (3 * width)
    part_k = pl.BlockSpec((chunk, width), lambda i: (i, kind + pair))
    part_v = pl.BlockSpec((chunk, width), lambda i: (i, 2 * kind + pair))
    whole = pl.BlockSpec((count, width), lambda i: (0, pair))
    alone = pl.BlockSpec((count, width), lambda i: (0, 0))
    part_out = pl.BlockSpec((chunk, width), lambda i: (i, 0))
    grad = jax.ShapeDtypeStruct((count, width), LOW)
    return pl.pallas_call(
        attention_backward_kernel,
        grid=(count // chunk,),
        in_specs=[whole, part_k, part_v, alone, alone, pl.BlockSpec((8, count), lambda i: (0, 0))],
        out_specs=[alone, part_out, part_out],
        out_shape=[grad, grad, grad],
        scratch_shapes=[
            pltpu.VMEM((2, count, width), LOW),
            pltpu.VMEM((2, count, width), LOW),
            pltpu.VMEM((8, count), FULL),
            pltpu.VMEM((count, width), FULL),
        ],
        compiler_params=pltpu.CompilerParams(vmem_limit_bytes=40 << 20),
        name="attention_backward",
    )(joint, joint, joint, da, out, lse)


def reduce_columns(place_ref, piece, rows):
    return pl.ds(pl.multiple_of(place_ref[piece], rows), rows)


def feed_forward_kernel(pieces, place_ref, normed_ref, slope_ref, expand_ref, bias_ref, *refs):
    reduce_refs = refs[:pieces]
    active_ref, expand_slope_ref, back_ref, bias_grad_ref, total = refs[pieces:]
    step = pl.program_id(0)
    count = normed_ref.shape[0]
    half = count // 2
    bias_grad = None
    for rows in (slice(0, half), slice(half, count)):
        hidden = product(normed_ref[rows], expand_ref[...], PLAIN) + bias_ref[...]
        upstream = None
        for piece, reduce_ref in enumerate(reduce_refs):
            columns = reduce_columns(place_ref, piece, reduce_ref.shape[0])
            part = product(slope_ref[rows, columns], reduce_ref[...], PLAIN)
            upstream = part if upstream is None else upstream + part
        share = 0.5 * (1.0 + lax.erf(hidden * (0.5**0.5)))
        active_ref[rows] = (hidden * share).astype(LOW)
        density = jnp.exp(-0.5 * hidden * hidden) * 0.3989422804014327
        slope = (upstream * (share + hidden * density)).astype(LOW)
        expand_slope_ref[rows] = slope
        part = jnp.sum(slope.astype(FULL), axis=0, keepdims=True)
        bias_grad = part if bias_grad is None else bias_grad + part
        back = product(slope, expand_ref[...], ROW_BY_ROW)

        @pl.when(step == 0)
        def _():
            total[rows] = back

        @pl.when(step > 0)
        def _():
            total[rows] += back

    bias_grad_ref[...] = bias_grad

    @pl.when(step == pl.num_programs(0) - 1)
    def _():
        back_ref[...] = total[...].astype(LOW)


def feed_forward(normed, slope, expand, bias, reduce, place):
    count, width = normed.shape
    hidden = expand.shape[1]
    block = 512 if hidden % 512 == 0 else hidden
    whole = pl.BlockSpec((count, width), lambda i, place: (0, 0))
    columns = pl.BlockSpec((width, block), lambda i, place: (0, i))
    out = pl.BlockSpec((count, block), lambda i, place: (0, i))
    row = pl.BlockSpec((1, block), lambda i, place: (0, i))
    return pl.pallas_call(
        lambda *refs: feed_forward_kernel(len(reduce), *refs),
        grid_spec=pltpu.PrefetchScalarGridSpec(
            num_scalar_prefetch=1,
            grid=(hidden // block,),
            in_specs=[whole, whole, columns, row]
            + [pl.BlockSpec((piece.shape[0], block), lambda i, place: (0, i)) for piece in reduce],
            out_specs=[out, out, whole, row],
            scratch_shapes=[pltpu.VMEM((count, width), FULL)],
        ),
        out_shape=[
            jax.ShapeDtypeStruct((count, hidden), LOW),
            jax.ShapeDtypeStruct((count, hidden), LOW),
            jax.ShapeDtypeStruct((count, width), LOW),
            jax.ShapeDtypeStruct((1, hidden), FULL),
        ],
        compiler_params=pltpu.CompilerParams(vmem_limit_bytes=48 << 20),
        name="feed_forward",
    )(place, normed, slope, expand, bias, *reduce)


def reduce_kernel(place_ref, active_ref, *refs):
    out_ref = refs[-1]
    for piece, reduce_ref in enumerate(refs[:-1]):
        columns = reduce_columns(place_ref, piece, reduce_ref.shape[0])
        out_ref[:, columns] = product(active_ref[...], reduce_ref[...], ROW_BY_ROW).astype(LOW)


def reduce_output(active, reduce, place):
    count, hidden = active.shape
    width = sum(piece.shape[0] for piece in reduce)
    chunk = row_chunk(count, 400)
    return pl.pallas_call(
        reduce_kernel,
        grid_spec=pltpu.PrefetchScalarGridSpec(
            num_scalar_prefetch=1,
            grid=(count // chunk,),
            in_specs=[pl.BlockSpec((chunk, hidden), lambda i, place: (i, 0))]
            + [pl.BlockSpec(piece.shape, lambda i, place: (0, 0)) for piece in reduce],
            out_specs=pl.BlockSpec((chunk, width), lambda i, place: (i, 0)),
        ),
        out_shape=jax.ShapeDtypeStruct((count, width), LOW),
        compiler_params=pltpu.CompilerParams(vmem_limit_bytes=48 << 20),
        name="reduce_output",
    )(place, active, *reduce)


def swap(value, axis, distance):
    size = lax.axis_size(axis)
    return lax.ppermute(value, axis, [(i, i ^ distance) for i in range(size)])


def fence(*values):
    return lax.optimization_barrier(values)


def gather_near(rows_here):
    if lax.axis_size("fsdp") != 4:
        return (lax.all_gather(rows_here, "fsdp", axis=0, tiled=True),)
    return (rows_here, swap(rows_here, "fsdp", 1), swap(rows_here, "fsdp", 2))


def gather_far(held):
    if len(held) == 1:
        return held
    rows_here, near, side = held
    half = rows_here.shape[0] // 2
    return held + (swap(side[:half], "fsdp", 1), swap(near[half:], "fsdp", 2))


def place_near(held):
    if len(held) == 1:
        return held[0]
    rows_here, near, side = held[:3]
    me = lax.axis_index("fsdp")
    count, width = rows_here.shape
    out = jnp.zeros((4 * count, width), rows_here.dtype)
    out = lax.dynamic_update_slice(out, rows_here, (me * count, 0))
    out = lax.dynamic_update_slice(out, near, ((me ^ 1) * count, 0))
    return lax.dynamic_update_slice(out, side, ((me ^ 2) * count, 0))


def place_far(out, held):
    if len(held) == 1:
        return out
    far_top, far_low = held[3:]
    half = far_top.shape[0]
    start = (lax.axis_index("fsdp") ^ 3) * 2 * half
    out = lax.dynamic_update_slice(out, far_top, (start, 0))
    return lax.dynamic_update_slice(out, far_low, (start + half, 0))


def far_halves(far):
    half = far.shape[0] // 2
    return (swap(far[:half], "fsdp", 1), swap(far[half:], "fsdp", 2))


def add_far(near, side, far):
    half = near.shape[0] // 2
    near = jnp.concatenate([near[:half], both((near[half:], far[1])).astype(LOW)], axis=0)
    side = jnp.concatenate([both((side[:half], far[0])).astype(LOW), side[half:]], axis=0)
    return (near, side)


def near_rows_out(pair):
    return (swap(pair[0], "fsdp", 1), swap(pair[1], "fsdp", 2))


def split_rows(value, bit, distance):
    half = value.shape[0] // 2
    keep = lax.dynamic_slice_in_dim(value, bit * half, half, 0)
    send = lax.dynamic_slice_in_dim(value, (1 - bit) * half, half, 0)
    return keep, swap(send.astype(LOW), "ctx", distance)


def both(pair):
    return pair[0].astype(FULL) + pair[1].astype(FULL)


def join_rows(value, bit, distance):
    other = swap(value, "ctx", distance)
    return jnp.where(
        bit == 0,
        jnp.concatenate([value, other], axis=0),
        jnp.concatenate([other, value], axis=0),
    )


def pairwise(pieces):
    return (pieces[0] + pieces[1]) + (pieces[2] + pieces[3])


def swapped_if(bit, pair):
    return [jnp.where(bit == 0, pair[0], pair[1]), jnp.where(bit == 0, pair[1], pair[0])]


def per_device(
    tokens,
    clip_mask,
    cotangent,
    first_gain,
    first_shift,
    joint_weight,
    joint_bias,
    mixer_weight,
    mixer_bias,
    second_gain,
    second_shift,
    expand_weight,
    expand_bias,
    reduce_weight,
    reduce_bias,
):
    clips_here, rows_here, width = tokens.shape
    if lax.axis_size("ctx") != 4 or lax.axis_size("tp") != 2 or clips_here != 2:
        raise ValueError("mesh")
    shard = lax.axis_index("fsdp")
    block = lax.axis_index("ctx")
    core = lax.axis_index("tp")
    clip_at = block >> 1
    part_at = block & 1
    width_half = width // 2
    quarter = width_half // 2
    features = joint_weight.shape[2]
    part_width = features // 2
    pair_width = 2 * HEAD_DIM
    tokens_here = clips_here * rows_here

    expand_full = lax.all_gather(expand_weight, "fsdp", axis=0, tiled=True)
    flat_tokens = tokens.reshape(tokens_here, width)
    (first_normed,) = by_rows(
        first_norm_kernel, "first_norm", [LOW], False,
        flat_tokens, first_gain[None], first_shift[None],
    )
    first_normed = first_normed.reshape(clips_here, rows_here, width)
    mine = lax.dynamic_slice_in_dim(first_normed, core * width_half, width_half, 2)
    other_side = lax.dynamic_slice_in_dim(first_normed, (1 - core) * width_half, width_half, 2)
    own_clip = lax.dynamic_index_in_dim(mine, clip_at, 0, False)
    own_other = lax.dynamic_index_in_dim(other_side, clip_at, 0, False)
    other_clip = lax.dynamic_index_in_dim(mine, 1 - clip_at, 0, False)
    joint_part = lax.dynamic_slice_in_dim(joint_weight, part_at * part_width, part_width, 2)
    both_parts = jnp.concatenate([joint_part[:, kind] for kind in range(3)] + [mixer_weight], axis=1)

    own_clip, left, right, both_parts = fence(
        own_clip, other_clip[:, :quarter], other_clip[:, quarter:], both_parts
    )
    near_rows = swap(own_clip, "ctx", 1)
    across_left = swap(left, "ctx", 2)
    far_right = swap(right, "ctx", 3)
    held = gather_near(both_parts)

    near_rows, across_left, far_right, held = fence(near_rows, across_left, far_right, held)
    passed = swap(jnp.concatenate([across_left, far_right], axis=1), "ctx", 1)
    near_other = swap(near_rows, "tp", 1)
    held = gather_far(held)

    passed, near_other, held = fence(passed, near_other, held)
    cross_rows = jnp.concatenate(
        [
            jnp.concatenate([across_left, passed[:, quarter:]], axis=1),
            jnp.concatenate([passed[:, :quarter], far_right], axis=1),
        ],
        axis=0,
    )
    cross_other = swap(cross_rows, "tp", 1)
    both_full = place_far(place_near(held), held)
    joint_columns = 3 * part_width
    joint_full = jnp.concatenate(
        [
            lax.dynamic_slice(both_full, (start * width_half, 0), (width_half, joint_columns))
            for start in (core, 1 - core)
        ],
        axis=0,
    )

    cross_other, joint_full, both_full, reduce_weight = fence(
        cross_other, joint_full, both_full, reduce_weight
    )
    mixer_full = both_full[:, joint_columns:]
    reduce_held = gather_near(reduce_weight)
    normed_mine = jnp.concatenate([own_clip, near_rows, cross_rows], axis=0)
    normed_other = jnp.concatenate([own_other, near_other, cross_other], axis=0)
    bias_part = lax.dynamic_slice_in_dim(joint_bias, part_at * part_width, part_width, 1)
    bias_row = jnp.concatenate([bias_part[0], jnp.zeros_like(bias_part[0]), bias_part[1]])
    joint_out = joint_projection(normed_mine, normed_other, joint_full, bias_row[None])
    out_first, log_first = attention_forward(joint_out, 0)

    out_first, joint_out, mixer_full = fence(out_first, joint_out, mixer_full)
    first_blocks = out_first.reshape(4, rows_here, pair_width)
    arrived_first = [swap(first_blocks[d], "ctx", d) for d in (1, 2, 3)]
    out_second, log_second = attention_forward(joint_out, 1)

    out_second, arrived_first, reduce_held, expand_full = fence(
        out_second, arrived_first, reduce_held, expand_full
    )
    second_blocks = out_second.reshape(4, rows_here, pair_width)
    arrived_second = [swap(second_blocks[d], "ctx", d) for d in (1, 2, 3)]
    reduce_held = gather_far(reduce_held)

    (arrived_second,) = fence(arrived_second)
    arrived = [jnp.concatenate([first_blocks[0], second_blocks[0]], axis=1)] + [
        jnp.concatenate([one, two], axis=1) for one, two in zip(arrived_first, arrived_second)
    ]
    own_joined = jnp.concatenate(swapped_if(part_at, arrived[:2]), axis=1)
    other_joined = jnp.concatenate(swapped_if(part_at, arrived[2:]), axis=1)
    mixed_in = jnp.concatenate(swapped_if(clip_at, [own_joined, other_joined]), axis=0)
    mixer_part = product(mixed_in, mixer_full, ROW_BY_ROW).astype(LOW)
    mixer_swapped = swap(mixer_part, "tp", 1)
    mixer_row = mixer_bias[None]
    (second_normed,) = by_rows(
        second_norm_kernel, "second_norm", [LOW], False,
        flat_tokens, mixer_part, mixer_swapped, mixer_row, second_gain[None], second_shift[None],
    )
    valid = clip_mask.astype(FULL)[:, None, None]
    reduce_slope = (cotangent.astype(FULL) * valid).astype(LOW).reshape(tokens_here, width)
    reduce_bias_grad = jnp.sum(reduce_slope.astype(FULL), axis=0)

    second_normed, reduce_slope, reduce_held = fence(second_normed, reduce_slope, reduce_held)
    four = lax.axis_size("fsdp") == 4
    start = jnp.zeros((), jnp.int32)
    if four:
        rows = width // 4
        reduce_at = jnp.stack([shard, shard ^ 1, shard ^ 2, shard ^ 3, shard ^ 3]) * rows
        reduce_at = (reduce_at + jnp.array([0, 0, 0, 0, rows // 2], jnp.int32)).astype(jnp.int32)
    else:
        reduce_at = start.reshape(1)
    activated, expand_slope, second_part, expand_bias_grad = feed_forward(
        second_normed, reduce_slope, expand_full, expand_bias[None], reduce_held, reduce_at
    )
    expand_bias_grad = expand_bias_grad[0]

    second_swapped = swap(second_part, "tp", 1)
    expand_whole = grad_products(
        [second_normed], expand_slope, start, (0, 1, 2, 3), "expand_grad"
    ).reshape(width, -1)
    expand_rows = lax.psum_scatter(expand_whole, "fsdp", scatter_dimension=0, tiled=True)
    mixer_slope, first_sum_back, second_sums = by_rows(
        second_norm_back_kernel, "second_norm_back", [LOW, FULL], True,
        flat_tokens, mixer_part, mixer_swapped, mixer_row, second_gain[None],
        second_part, second_swapped, reduce_slope,
    )
    attended_slope = product(mixer_slope, mixer_full, PLAIN).astype(LOW)

    attended_slope, mixer_slope, mixed_in, activated = fence(
        attended_slope, mixer_slope, mixed_in, activated
    )
    leaving = []
    for piece in swapped_if(clip_at, [attended_slope[:rows_here], attended_slope[rows_here:]]):
        leaving += swapped_if(part_at, [piece[:, :part_width], piece[:, part_width:]])
    slope_first = [leaving[0][:, :pair_width]] + [
        swap(leaving[d][:, :pair_width], "ctx", d) for d in (1, 2, 3)
    ]
    place, order = (shard, (3, 2, 1, 0)) if four else (start, (0, 1, 2, 3))
    reduce_parts = grad_products([reduce_slope], activated, place, order, "reduce_grad")
    mixer_parts = grad_products([mixer_slope], mixed_in, place, order, "mixer_grad")
    wide = jnp.concatenate([reduce_parts, mixer_parts], axis=2)

    slope_first, leaving, wide = fence(slope_first, leaving, wide)
    half = width // 8
    wide_far = far_halves(wide[0]) if four else ()
    slope_second = [leaving[0][:, pair_width:]] + [
        swap(leaving[d][:, pair_width:], "ctx", d) for d in (1, 2, 3)
    ]
    grad_first = attention_backward(
        joint_out, jnp.concatenate(slope_first, axis=0), out_first, log_first, 0
    )

    grad_first, slope_second, expand_rows, wide_far = fence(
        grad_first, slope_second, expand_rows, wide_far
    )
    wide_early, wide_late = (), ()
    if four:
        wide_late = (
            both((wide[2][half:], wide_far[1])).astype(LOW),
            both((wide[1][:half], wide_far[0])).astype(LOW),
        )
        wide_early = (wide[2][:half], wide[1][half:])
    expand_rows, slope_second, wide_early, wide_late = fence(
        expand_rows, slope_second, wide_early, wide_late
    )
    if four:
        wide_early = near_rows_out(wide_early)
    expand_rows = split_rows(expand_rows, part_at, 1)
    grad_second = attention_backward(
        joint_out, jnp.concatenate(slope_second, axis=0), out_second, log_second, 1
    )

    grad_second, expand_rows, wide_early, wide_late = fence(
        grad_second, expand_rows, wide_early, wide_late
    )
    expand_rows = split_rows(both(expand_rows), clip_at, 2)
    if four:
        wide_late = near_rows_out(wide_late)
    joint_slope = jnp.concatenate(
        [grad[kind] for kind in range(3) for grad in (grad_first, grad_second)], axis=1
    )
    first_there = product(joint_slope, joint_full[width_half:], ROW_BY_ROW).astype(LOW)
    first_here = rows_product(joint_slope, joint_full[:width_half], "first_slope")
    first_half = both((first_here, swap(first_there, "tp", 1))).astype(LOW)

    first_half, joint_slope, expand_rows, wide_late = fence(
        first_half, joint_slope, expand_rows, wide_late
    )
    expand_rows = both(expand_rows).astype(LOW)
    pieces = first_half.reshape(4, rows_here, width_half)
    passing = jnp.concatenate([pieces[1], pieces[3][:, :quarter], pieces[2][:, quarter:]], axis=1)
    passing = swap(passing, "ctx", 1)
    place = (shard if four else start) ^ (2 * core)
    joint_parts = grad_products([normed_mine, normed_other], joint_slope, place, order, "joint_grad")
    slope_sums = jnp.sum(joint_slope.astype(FULL), axis=0)
    bias_sums = jnp.stack([slope_sums[:part_width], slope_sums[2 * part_width :]])
    joint_bias_grad = lax.dynamic_update_slice(
        jnp.zeros((2, features), FULL), bias_sums, (0, part_at * part_width)
    )

    expand_rows = join_rows(expand_rows, clip_at, 2)

    passing, joint_parts, wide, expand_rows, activated = fence(
        passing, joint_parts, wide, expand_rows, activated
    )
    if four:
        wide_sum = jnp.concatenate(
            [both((wide_early[0], wide_late[1])), both((wide_late[0], wide_early[1]))], axis=0
        )
        wide_sum = wide[3].astype(FULL) + wide_sum
    else:
        wide_sum = lax.psum_scatter(
            wide.reshape(width, -1), "fsdp", scatter_dimension=0, tiled=True
        ).astype(FULL)
    wide_rows = split_rows(wide_sum, part_at, 1)
    joint_far = far_halves(joint_parts[0]) if four else ()
    own_half = both((pieces[0], passing[:, :width_half])).astype(LOW)
    to_left = both((pieces[2][:, :quarter], passing[:, width_half : width_half + quarter]))
    to_right = both((pieces[3][:, quarter:], passing[:, width_half + quarter :]))
    other_half = jnp.concatenate(
        [swap(to_left.astype(LOW), "ctx", 2), swap(to_right.astype(LOW), "ctx", 3)], axis=1
    )
    reduce_part = reduce_output(activated, reduce_held, reduce_at)

    other_half, joint_far, reduce_part, wide_rows = fence(
        other_half, joint_far, reduce_part, wide_rows
    )
    wide_rows = split_rows(both(wide_rows), clip_at, 2)
    slope_half = jnp.concatenate(
        swapped_if(clip_at, [own_half, other_half]), axis=0
    )
    slope_other = swap(slope_half, "tp", 1)
    first_slope = jnp.concatenate(swapped_if(core, [slope_half, slope_other]), axis=1)
    tokens_grad, first_sums = by_rows(
        first_norm_back_kernel, "first_norm_back", [FULL], True,
        flat_tokens, first_slope, first_gain[None],
        cotangent.reshape(tokens_here, width), first_sum_back,
    )
    reduce_swapped = swap(reduce_part, "tp", 1)
    if four:
        joint_near = near_rows_out(add_far(joint_parts[2], joint_parts[1], joint_far))
    else:
        joint_near = lax.psum_scatter(
            joint_parts.reshape(width, -1), "fsdp", scatter_dimension=0, tiled=True
        )

    first_sums, tokens_grad, joint_near, wide_rows, reduce_swapped = fence(
        first_sums, tokens_grad, joint_near, wide_rows, reduce_swapped
    )
    vectors = [
        first_sums[0],
        first_sums[1],
        joint_bias_grad[0],
        joint_bias_grad[1],
        second_sums[2],
        second_sums[0],
        second_sums[1],
        expand_bias_grad,
        reduce_bias_grad,
    ]
    packed = jnp.concatenate(vectors).reshape(-1, 128)
    packed_pieces = [packed] + [swap(packed, "ctx", d) for d in (1, 2, 3)]
    joint_sum = joint_parts[3].astype(FULL) + both(joint_near) if four else joint_near
    joint_sum = joint_sum.astype(LOW)
    joint_sum = (joint_sum, swap(joint_sum, "ctx", 2))
    wide_rows = join_rows(both(wide_rows).astype(LOW), clip_at, 2)
    reduce_out = both((reduce_part, reduce_swapped)) + reduce_bias
    mixer_out = both((mixer_part, mixer_swapped)) + mixer_bias
    branches = (mixer_out + reduce_out).reshape(clips_here, rows_here, width)
    result = (tokens.astype(FULL) + valid * branches).astype(LOW)

    packed_pieces, joint_sum, wide_rows, result = fence(
        packed_pieces, joint_sum, wide_rows, result
    )
    packed = pairwise(packed_pieces)
    if four:
        packed = pairwise([packed] + [swap(packed, "fsdp", d) for d in (1, 2, 3)])
    else:
        packed = lax.psum(packed, "fsdp")
    joint_sum = both(joint_sum).astype(LOW)
    joint_parts = swapped_if(part_at, [joint_sum, swap(joint_sum, "ctx", 1)])
    joint_grad = jnp.concatenate(
        [piece.reshape(-1, 3, part_width) for piece in joint_parts], axis=2
    ).astype(FULL)
    wide_rows = join_rows(wide_rows, part_at, 1).astype(FULL)
    reduce_grad = wide_rows[:, : activated.shape[1]]
    mixer_grad = wide_rows[:, activated.shape[1] :]
    expand_grad = join_rows(expand_rows, part_at, 1).astype(FULL)
    packed = packed.reshape(-1)
    shares = []
    start = 0
    for vector in vectors:
        share = vector.shape[0] // lax.axis_size("fsdp")
        shares.append(lax.dynamic_slice_in_dim(packed, start + shard * share, share, 0))
        start += vector.shape[0]

    shape = (clips_here, rows_here, width)
    return (
        result,
        tokens_grad.reshape(shape),
        shares[0],
        shares[1],
        joint_grad,
        jnp.stack([shares[2], shares[3]]),
        mixer_grad,
        shares[4],
        shares[5],
        shares[6],
        expand_grad,
        shares[7],
        reduce_grad,
        shares[8],
    )


def solution(mesh):
    return jax.shard_map(
        per_device,
        mesh=mesh,
        in_specs=(
            P("fsdp", "ctx", None),
            P("fsdp"),
            P("fsdp", "ctx", None),
            P(),
            P(),
            P("fsdp", None, "tp"),
            P(None, "tp"),
            P("fsdp", "tp"),
            P(),
            P(),
            P(),
            P("fsdp", "tp"),
            P("tp"),
            P("fsdp", "tp"),
            P(),
        ),
        out_specs=(
            P("fsdp", "ctx", None),
            P("fsdp", "ctx", None),
            P("fsdp"),
            P("fsdp"),
            P("fsdp", None, "tp"),
            P(None, ("tp", "fsdp")),
            P("fsdp", "tp"),
            P("fsdp"),
            P("fsdp"),
            P("fsdp"),
            P("fsdp", "tp"),
            P(("tp", "fsdp")),
            P("fsdp", "tp"),
            P("fsdp"),
        ),
        check_vma=False,
    )
```

time: 493 us -> 475 us (0.963); the launches traced: 488 us -> 465 us
  Pallas kernels: 73.8 us -> 147 us
  matrix products: 54.7 us -> 5.78 us
  waiting for transfers between devices: 177 us -> 134 us
  other arithmetic: 62.3 us -> 30.4 us
  local copies, waits for them, and re-layouts: 35.4 us -> 61.9 us
    pallas_call x1 -> x12, Pallas kernels: 16 us -> 89.7 us  [the longest x4 34.5 us: grad_products(): pl.pallas_call(lambda *refs: grad_kernel(distances, *refs), grid_spec=plt...]
    dot_general x16 -> x3, matrix products: 54.7 us -> 5.78 us  [product(): return lax.dot_general(left, right, dims, preferred_element_type=FULL)]
    ppermute x61 -> x60, waiting for transfers between devices: 177 us -> 133 us  [swap(): return lax.ppermute(value, axis, [(i, i ^ distance) for i in range(size)])]
    unnamed x243 -> x164, local copies, waits for them, and re-layouts: 11.2 us -> 32.2 us
    reduce_sum x7 -> x0, other arithmetic: 16.5 us -> none  [the longest x1 4.58 us: per_device(): first_shift_grad = jnp.sum(first_slope, axis=0)]
    convert_element_type x9 -> x12, other arithmetic: 14.7 us -> 11.8 us  [the longest x1 3.14 us: per_device(): both((wide[1][:half], wide_far[0])).astype(LOW)]
    ppermute x61 -> x60, starting transfers between devices: 68.4 us -> 69.7 us  [swap(): return lax.ppermute(value, axis, [(i, i ^ distance) for i in range(size)])]
  transfers between devices with their start and end apart: 64 -> 62, of which waited for: 22 -> 24; matrix products, arithmetic and copies ran while one was open for 24% -> 12% of each run, Pallas kernels for 12% -> 25%
where the time goes in v3:
time: 475 us; the launch traced here: 465 us
  Pallas kernels  147 us (31%)
  waiting for transfers between devices  134 us (28%)
  starting transfers between devices  69.8 us (15%)
  local copies, waits for them, and re-layouts  61.9 us (13%)
  other arithmetic  30.4 us (6%)
  between operations  16 us (3%)
  matrix products  5.78 us (1%)
    ppermute x60, waiting for transfers between devices, swap(): return lax.ppermute(value, axis, [(i, i ^ distance) for i in range(size)])  133 us
    ppermute x60, starting transfers between devices, swap(): return lax.ppermute(value, axis, [(i, i ^ distance) for i in range(size)])  69.7 us
    pallas_call x2, Pallas kernels, attention_backward(): pl.pallas_call(attention_backward_kernel, grid=(count // chunk,), in_spec...  35.1 us
    pallas_call x4, Pallas kernels, grad_products(): pl.pallas_call(lambda *refs: grad_kernel(distances, *refs), grid_spec=plt...  34.5 us
    unnamed x164, local copies, waits for them, and re-layouts  32.2 us
    pallas_call x2, Pallas kernels, attention_forward(): pl.pallas_call(attention_forward_kernel, grid=(steps,), in_specs=[pl.Bloc...  22.4 us
    pallas_call x1, Pallas kernels, feed_forward(): pl.pallas_call(lambda *refs: feed_forward_kernel(len(reduce), *refs), gri...  18.6 us
    pallas_call x4, Pallas kernels, by_rows(): pl.pallas_call(kernel, grid=(count // chunk,), in_specs=in_specs, out_spe...  18.4 us
  transfers between devices with their start and end apart: 62, of which 24 were waited for; matrix products, arithmetic and copies ran while one was open for 12% of the time, Pallas kernels for 25%

profile of v3, /device:TPU:0, one launch (start us, length us, event | category | flops | bytes accessed | tf_op | source)
XLA Modules:
  0.0 465.2 jit_solution(6042835749073654537)
XLA Ops:
  13.6 3.0 collective-permute-start.3
  22.6 11.3 %collective-permute-done.1 = bf16[392,256]{1,0:T(8,128)(2,1)S(1)} collective-permute-done((bf16[392,256]{1,0:T(8,128)(2,1)S(1)}, bf16[392,256]{1,0:T(8,128)(2,1)S(1)}, u32[]{:S(2)}, u32[]{:S(2)}) %collective-permute-start.1) | collective-permute-done | bytes 200736 | tf_op jit(solution)/shard_map/ppermute | solution.py:435
  33.8 5.5 %collective-permute-done.2 = bf16[392,256]{1,0:T(8,128)(2,1)S(1)} collective-permute-done((bf16[392,256]{1,0:T(8,128)(2,1)S(1)}, bf16[392,256]{1,0:T(8,128)(2,1)S(1)}, u32[]{:S(2)}, u32[]{:S(2)}) %collective-permute-start.2) | collective-permute-done | bytes 200736 | tf_op jit(solution)/shard_map/ppermute | solution.py:435
  49.5 12.9 %collective-permute-done.7 = bf16[128,1280]{1,0:T(8,128)(2,1)} collective-permute-done((bf16[128,1280]{1,0:T(8,128)(2,1)}, bf16[128,1280]{1,0:T(8,128)(2,1)}, u32[]{:S(2)}, u32[]{:S(2)}) %collective-permute-start.7) | collective-permute-done | bytes 327712 | tf_op jit(solution)/shard_map/ppermute | solution.py:435
  75.3 2.9 joint_projection.1.q_ref.k_ref.v_ref
  79.4 11.2 %attention_forward.2 = (bf16[1568,128]{1,0:T(8,128)(2,1)S(1)}, f32[7,8,224]{2,1,0:T(8,128)S(1)}) custom-call(bf16[1568,768]{1,0:T(8,128)(2,1)S(1)} %joint_projection.1.q_ref.k_ref.v_ref, bf16[1568,768]{1,0:T(8,128)(2,1)S(1)} %joint_projection.1.q_ref.k_ref.v_ref, bf16[1568,768]{1,0:T(8,128)(2,1)S(1)} %joint_projection.1.q_ref.k_ref.v_ref), custom_call_target="tpu_custom_call" | custom-call | tf_op jit(solution)/shard_map/attention_forward/pallas_call | solution.py:239
  96.8 11.2 %attention_forward.3 = (bf16[1568,128]{1,0:T(8,128)(2,1)S(1)}, f32[7,8,224]{2,1,0:T(8,128)S(1)}) custom-call(bf16[1568,768]{1,0:T(8,128)(2,1)S(1)} %joint_projection.1.q_ref.k_ref.v_ref, bf16[1568,768]{1,0:T(8,128)(2,1)S(1)} %joint_projection.1.q_ref.k_ref.v_ref, bf16[1568,768]{1,0:T(8,128)(2,1)S(1)} %joint_projection.1.q_ref.k_ref.v_ref), custom_call_target="tpu_custom_call" | custom-call | tf_op jit(solution)/shard_map/attention_forward/pallas_call | solution.py:239
  116.9 4.1 collective-permute-done.16
  128.9 5.4 %second_norm.1.refs_1_ = bf16[784,1024]{1,0:T(8,128)(2,1)S(1)} custom-call(bf16[784,1024]{1,0:T(8,128)(2,1)S(1)} %bitcast.92, bf16[784,1024]{1,0:T(8,128)(2,1)} %convolution_convert_fusion.1.one_ref, bf16[784,1024]{1,0:T(8,128)(2,1)} %collective-permute-done.18.two_ref, f32[1,1024]{1,0:T(1,128)S(1)} %bitcast.102, f32[1,1024]{1,0:T(1,128)S(1)} %bitcast.106, ...), custom_call_target="tpu_custom_call" | custom-call | tf_op jit(solution)/shard_map/second_norm/pallas_call | solution.py:104
  135.5 4.7 %collective-permute-done.19.refs_8_.refs_3_ = bf16[128,2048]{1,0:T(8,128)(2,1)S(1)} collective-permute-done((bf16[128,2048]{1,0:T(8,128)(2,1)S(1)}, bf16[128,2048]{1,0:T(8,128)(2,1)S(1)}, u32[]{:S(2)}, u32[]{:S(2)}) %collective-permute-start.19) | collective-permute-done | bytes 524320 | tf_op jit(solution)/shard_map/ppermute | solution.py:435
  140.4 18.6 %feed_forward.1 = (bf16[784,2048]{1,0:T(8,128)(2,1)}, bf16[784,2048]{1,0:T(8,128)(2,1)}, bf16[784,1024]{1,0:T(8,128)(2,1)S(1)}, f32[1,2048]{1,0:T(1,128)S(1)}) custom-call(s32[5]{0:T(128)S(1)} %multiply_add_fusion.refs_0_.place_ref, bf16[784,1024]{1,0:T(8,128)(2,1)} %copy-done.7, bf16[784,1024]{1,0:T(8,128)(2,1)} %bitcast.95, ...), custom_call_target="tpu_custom_call" | custom-call | tf_op jit(solution)/shard_map/feed_forward/pallas_call | solution.py:386
  162.0 11.2 %expand_grad.1 = bf16[4,256,2048]{2,1,0:T(8,128)(2,1)} custom-call(s32[1]{0:T(128)} %constant.111.clone.1.refs_0_, bf16[784,1024]{1,0:T(8,128)(2,1)S(1)} %copy-done.8, bf16[784,2048]{1,0:T(8,128)(2,1)S(1)} %copy-done.20), custom_call_target="tpu_custom_call" | custom-call | tf_op jit(solution)/shard_map/expand_grad/pallas_call | solution.py:194
  180.1 6.4 %second_norm_back.1 = (bf16[784,1024]{1,0:T(8,128)(2,1)S(1)}, f32[784,1024]{1,0:T(8,128)S(1)}, f32[8,1024]{1,0:T(8,128)S(1)}) custom-call(bf16[784,1024]{1,0:T(8,128)(2,1)S(1)} %bitcast.93, bf16[784,1024]{1,0:T(8,128)(2,1)} %convolution_convert_fusion.1.one_ref, bf16[784,1024]{1,0:T(8,128)(2,1)} %collective-permute-done.18.two_ref, f32[1,1024]{1,0:T(1,128)S(1)} %bitcast.103, ...), custom_call_target="tpu_custom_call" | custom-call | tf_op jit(solution)/shard_map/second_norm_back/pallas_call | solution.py:104
  190.4 11.2 %reduce_grad.1 = bf16[4,256,2048]{2,1,0:T(8,128)(2,1)} custom-call(s32[1]{0:T(128)} %bitcast.14.refs_0_, bf16[784,1024]{1,0:T(8,128)(2,1)S(1)} %bitcast.97, bf16[784,2048]{1,0:T(8,128)(2,1)S(1)} %copy-done.13), custom_call_target="tpu_custom_call" | custom-call | tf_op jit(solution)/shard_map/reduce_grad/pallas_call | solution.py:194
  229.9 17.5 %attention_backward.2 = (bf16[1568,128]{1,0:T(8,128)(2,1)S(1)}, bf16[1568,128]{1,0:T(8,128)(2,1)S(1)}, bf16[1568,128]{1,0:T(8,128)(2,1)S(1)}) custom-call(bf16[1568,768]{1,0:T(8,128)(2,1)S(1)} %joint_projection.1.q_ref.k_ref.v_ref, bf16[1568,768]{1,0:T(8,128)(2,1)S(1)} %joint_projection.1.q_ref.k_ref.v_ref, ...), custom_call_target="tpu_custom_call" | custom-call | tf_op jit(solution)/shard_map/attention_backward/pallas_call | solution.py:319
  249.7 3.1 fusion.1
  259.7 17.7 %attention_backward.3 = (bf16[1568,128]{1,0:T(8,128)(2,1)S(1)}, bf16[1568,128]{1,0:T(8,128)(2,1)S(1)}, bf16[1568,128]{1,0:T(8,128)(2,1)S(1)}) custom-call(bf16[1568,768]{1,0:T(8,128)(2,1)S(1)} %joint_projection.1.q_ref.k_ref.v_ref, bf16[1568,768]{1,0:T(8,128)(2,1)S(1)} %joint_projection.1.q_ref.k_ref.v_ref, ...), custom_call_target="tpu_custom_call" | custom-call | tf_op jit(solution)/shard_map/attention_backward/pallas_call | solution.py:319
  285.8 3.1 collective-permute-start.34
  290.8 2.9 first_slope.1
  295.6 5.8 %collective-permute-done.34 = bf16[64,2048]{1,0:T(8,128)(2,1)S(1)} collective-permute-done((bf16[64,2048]{1,0:T(8,128)(2,1)S(1)}, bf16[64,2048]{1,0:T(8,128)(2,1)S(1)}, u32[]{:S(2)}, u32[]{:S(2)}) %collective-permute-start.34) | collective-permute-done | bytes 262176 | tf_op jit(solution)/shard_map/ppermute | solution.py:435
  301.4 4.3 collective-permute-done.35
  313.6 9.9 %joint_grad.1 = bf16[4,256,768]{2,1,0:T(8,128)(2,1)S(1)} custom-call(s32[1]{0:T(128)} %bitcast.30.refs_0_, bf16[1568,512]{1,0:T(8,128)(2,1)S(1)} %copy-done.10, bf16[1568,512]{1,0:T(8,128)(2,1)S(1)} %copy-done.12, bf16[1568,768]{1,0:T(8,128)(2,1)} %copy-done.6), custom_call_target="tpu_custom_call" | custom-call | tf_op jit(solution)/shard_map/joint_grad/pallas_call | solution.py:194
  323.7 8.7 %collective-permute-done.37 = bf16[392,1024]{1,0:T(8,128)(2,1)S(1)} collective-permute-done((bf16[392,1024]{1,0:T(8,128)(2,1)S(1)}, bf16[392,1024]{1,0:T(8,128)(2,1)S(1)}, u32[]{:S(2)}, u32[]{:S(2)}) %collective-permute-start.37) | collective-permute-done | bytes 802848 | tf_op jit(solution)/shard_map/ppermute | solution.py:435
  337.1 12.5 %reduce_output.1 = bf16[784,1024]{1,0:T(8,128)(2,1)S(1)} custom-call(s32[5]{0:T(128)S(1)} %multiply_add_fusion.refs_0_.place_ref, bf16[784,2048]{1,0:T(8,128)(2,1)} %get-tuple-element.249.refs_2_.active_ref, bf16[256,2048]{1,0:T(8,128)(2,1)} %refs_0_, bf16[256,2048]{1,0:T(8,128)(2,1)S(1)} %collective-permute-done.13.refs_6_.refs_1_, ...), custom_call_target="tpu_custom_call" | custom-call | tf_op jit(solution)/shard_map/reduce_output/pallas_call | solution.py:418
  354.0 9.8 %collective-permute-done.39 = bf16[392,256]{1,0:T(8,128)(2,1)S(1)} collective-permute-done((bf16[392,256]{1,0:T(8,128)(2,1)S(1)}, bf16[392,256]{1,0:T(8,128)(2,1)S(1)}, u32[]{:S(2)}, u32[]{:S(2)}) %collective-permute-start.39) | collective-permute-done | bytes 200736 | tf_op jit(solution)/shard_map/ppermute | solution.py:435
  364.2 3.9 collective-permute-done.40
  380.7 4.8 %first_norm_back.1 = (f32[784,1024]{1,0:T(8,128)}, f32[8,1024]{1,0:T(8,128)S(1)}) custom-call(bf16[784,1024]{1,0:T(8,128)(2,1)S(1)} %bitcast.94, bf16[784,1024]{1,0:T(8,128)(2,1)S(1)} %pad_maximum_fusion.2.upstream_ref, f32[1,1024]{1,0:T(1,128)S(1)} %bitcast.105, bf16[784,1024]{1,0:T(8,128)(2,1)S(1)} %bitcast.98, f32[784,1024]{1,0:T(8,128)S(1)} %copy-done.19), custom_call_target="tpu_custom_call" | custom-call | tf_op jit(solution)/shard_map/first_norm_back/pallas_call | solution.py:104
  390.5 2.9 collective-permute-start.52
  393.5 3.4 add_add_fusion
  398.6 17.5 %collective-permute-done.53 = bf16[64,2560]{1,0:T(8,128)(2,1)S(1)} collective-permute-done((bf16[64,2560]{1,0:T(8,128)(2,1)S(1)}, bf16[64,2560]{1,0:T(8,128)(2,1)S(1)}, u32[]{:S(2)}, u32[]{:S(2)}) %collective-permute-start.53) | collective-permute-done | bytes 327712 | tf_op jit(solution)/shard_map/ppermute | solution.py:435
  416.2 8.0 %collective-permute-done.52 = bf16[256,768]{1,0:T(8,128)(2,1)S(1)} collective-permute-done((bf16[256,768]{1,0:T(8,128)(2,1)S(1)}, bf16[256,768]{1,0:T(8,128)(2,1)S(1)}, u32[]{:S(2)}, u32[]{:S(2)}) %collective-permute-start.52) | collective-permute-done | bytes 393248 | tf_op jit(solution)/shard_map/ppermute | solution.py:435
  432.8 19.0 %collective-permute-done.57 = bf16[256,768]{1,0:T(8,128)(2,1)S(1)} collective-permute-done((bf16[256,768]{1,0:T(8,128)(2,1)S(1)}, bf16[256,768]{1,0:T(8,128)(2,1)S(1)}, u32[]{:S(2)}, u32[]{:S(2)}) %collective-permute-start.57) | collective-permute-done | bytes 393248 | tf_op jit(solution)/shard_map/ppermute | solution.py:435
  (394 shorter events, 175.0 us)
Async XLA Ops:
  7.2 102.3 %all-gather.2.cloned.1.call-start = ((), (), s32[]{:S(2)}) async-start(), calls=%async_computation.1 | async-start | bytes 5242880 | tf_op jit(solution)/shard_map/all_gather | solution.py:554
  7.9 241.8 %reduce-scatter.2.cloned.1.call-start = ((), (), s32[]{:S(2)}) async-start(), calls=%async_computation.2 | async-start | bytes 5242880 | tf_op jit(solution)/shard_map/reduce_scatter | solution.py:661
  13.6 27.7 %collective-permute-start.3 = (bf16[256,1280]{1,0:T(8,128)(2,1)S(1)}, bf16[256,1280]{1,0:T(8,128)(2,1)S(1)}, u32[]{:S(2)}, u32[]{:S(2)}) collective-permute-start(bf16[256,1280]{1,0:T(8,128)(2,1)S(1)} %pad_maximum_fusion.7), channel_id=1, source_target_pairs={{0,8},{8,0},{16,24},{24,16},{1,9},{9,1},{17,25},{25,17},{2,10},{10... | collective-permute-start | bytes 1966088 | tf_op jit(solution)/shard_map/ppermute | solution.py:435
  16.7 26.8 %collective-permute-start.4 = (bf16[256,1280]{1,0:T(8,128)(2,1)S(1)}, bf16[256,1280]{1,0:T(8,128)(2,1)S(1)}, u32[]{:S(2)}, u32[]{:S(2)}) collective-permute-start(bf16[256,1280]{1,0:T(8,128)(2,1)S(1)} %pad_maximum_fusion.7), channel_id=1, source_target_pairs={{0,16},{8,24},{16,0},{24,8},{1,17},{9,25},{17,1},{25,9},{2,18},{10... | collective-permute-start | bytes 1966088 | tf_op jit(solution)/shard_map/ppermute | solution.py:435
  18.2 21.2 %collective-permute-start = (bf16[392,512]{1,0:T(8,128)(2,1)S(1)}, bf16[392,512]{1,0:T(8,128)(2,1)S(1)}, u32[]{:S(2)}, u32[]{:S(2)}) collective-permute-start(bf16[392,512]{1,0:T(8,128)(2,1)S(1)} %get-tuple-element.148), channel_id=1, source_target_pairs={{0,2},{2,0},{4,6},{6,4},{1,3},{3,1},{5,7},{7,5},{8,10},{10,8},{12,... | collective-permute-start | bytes 1204232 | tf_op jit(solution)/shard_map/ppermute | solution.py:435
  22.3 17.0 %collective-permute-start.2 = (bf16[392,256]{1,0:T(8,128)(2,1)S(1)}, bf16[392,256]{1,0:T(8,128)(2,1)S(1)}, u32[]{:S(2)}, u32[]{:S(2)}) collective-permute-start(bf16[392,256]{1,0:T(8,128)(2,1)S(1)} %get-tuple-element.150), channel_id=1, source_target_pairs={{0,6},{2,4},{4,2},{6,0},{1,7},{3,5},{5,3},{7,1},{8,14},{10,12},{12... | collective-permute-start | bytes 602120 | tf_op jit(solution)/shard_map/ppermute | solution.py:435
  44.2 20.4 %collective-permute-start.5 = (bf16[392,512]{1,0:T(8,128)(2,1)}, bf16[392,512]{1,0:T(8,128)(2,1)}, u32[]{:S(2)}, u32[]{:S(2)}) collective-permute-start(bf16[392,512]{1,0:T(8,128)(2,1)} %pad_maximum_fusion.8), channel_id=1, source_target_pairs={{0,2},{2,0},{4,6},{6,4},{1,3},{3,1},{5,7},{7,5},{8,10},{10,8},{12,... | collective-permute-start | bytes 1204232 | tf_op jit(solution)/shard_map/ppermute | solution.py:435
  45.9 18.7 %collective-permute-start.6 = (bf16[392,512]{1,0:T(8,128)(2,1)S(1)}, bf16[392,512]{1,0:T(8,128)(2,1)S(1)}, u32[]{:S(2)}, u32[]{:S(2)}) collective-permute-start(bf16[392,512]{1,0:T(8,128)(2,1)S(1)} %collective-permute-done), channel_id=1, source_target_pairs={{0,1},{1,0},{2,3},{3,2},{4,5},{5,4},{6,7},{7,6},{8,9},{9,8},{10,11... | collective-permute-start | bytes 1204232 | tf_op jit(solution)/shard_map/ppermute | solution.py:435
  47.6 17.0 %collective-permute-start.8 = (bf16[128,1280]{1,0:T(8,128)(2,1)}, bf16[128,1280]{1,0:T(8,128)(2,1)}, u32[]{:S(2)}, u32[]{:S(2)}) collective-permute-start(bf16[128,1280]{1,0:T(8,128)(2,1)} %slice.290), channel_id=1, source_target_pairs={{0,16},{8,24},{16,0},{24,8},{1,17},{9,25},{17,1},{25,9},{2,18},{10... | collective-permute-start | bytes 983048 | tf_op jit(solution)/shard_map/ppermute | solution.py:435
  69.6 39.8 %collective-permute-start.13 = (bf16[256,2048]{1,0:T(8,128)(2,1)}, bf16[256,2048]{1,0:T(8,128)(2,1)S(1)}, u32[]{:S(2)}, u32[]{:S(2)}) collective-permute-start(bf16[256,2048]{1,0:T(8,128)(2,1)} %refs_0_), channel_id=1, source_target_pairs={{0,8},{8,0},{16,24},{24,16},{1,9},{9,1},{17,25},{25,17},{2,10},{10... | collective-permute-start | bytes 3145736 | tf_op jit(solution)/shard_map/ppermute | solution.py:435
  71.8 37.6 %collective-permute-start.14 = (bf16[256,2048]{1,0:T(8,128)(2,1)}, bf16[256,2048]{1,0:T(8,128)(2,1)}, u32[]{:S(2)}, u32[]{:S(2)}) collective-permute-start(bf16[256,2048]{1,0:T(8,128)(2,1)} %refs_0_), channel_id=1, source_target_pairs={{0,16},{8,24},{16,0},{24,8},{1,17},{9,25},{17,1},{25,9},{2,18},{10... | collective-permute-start | bytes 3145736 | tf_op jit(solution)/shard_map/ppermute | solution.py:435
  92.4 17.0 %collective-permute-start.10 = (bf16[392,128]{1,0:T(8,128)(2,1)}, bf16[392,128]{1,0:T(8,128)(2,1)}, u32[]{:S(2)}, u32[]{:S(2)}) collective-permute-start(bf16[392,128]{1,0:T(8,128)(2,1)} %get-tuple-element.343), channel_id=1, source_target_pairs={{0,2},{2,0},{4,6},{6,4},{1,3},{3,1},{5,7},{7,5},{8,10},{10,8},{12,... | collective-permute-start | bytes 301064 | tf_op jit(solution)/shard_map/ppermute | solution.py:435
  216.6 33.1 %collective-permute-start.28 = (bf16[128,2560]{1,0:T(8,128)(2,1)}, bf16[128,2560]{1,0:T(8,128)(2,1)}, u32[]{:S(2)}, u32[]{:S(2)}) collective-permute-start(bf16[128,2560]{1,0:T(8,128)(2,1)} %get-tuple-element.303), channel_id=1, source_target_pairs={{0,8},{8,0},{16,24},{24,16},{1,9},{9,1},{17,25},{25,17},{2,10},{10... | collective-permute-start | bytes 1966088 | tf_op jit(solution)/shard_map/ppermute | solution.py:435
  218.3 31.4 %collective-permute-start.29 = (bf16[128,2560]{1,0:T(8,128)(2,1)}, bf16[128,2560]{1,0:T(8,128)(2,1)}, u32[]{:S(2)}, u32[]{:S(2)}) collective-permute-start(bf16[128,2560]{1,0:T(8,128)(2,1)} %get-tuple-element.302), channel_id=1, source_target_pairs={{0,16},{8,24},{16,0},{24,8},{1,17},{9,25},{17,1},{25,9},{2,18},{10... | collective-permute-start | bytes 1966088 | tf_op jit(solution)/shard_map/ppermute | solution.py:435
  221.1 28.6 %collective-permute-start.25 = (bf16[392,128]{1,0:T(8,128)(2,1)S(1)}, bf16[392,128]{1,0:T(8,128)(2,1)}, u32[]{:S(2)}, u32[]{:S(2)}) collective-permute-start(bf16[392,128]{1,0:T(8,128)(2,1)S(1)} %slice.317), channel_id=1, source_target_pairs={{0,2},{2,0},{4,6},{6,4},{1,3},{3,1},{5,7},{7,5},{8,10},{10,8},{12,... | collective-permute-start | bytes 301064 | tf_op jit(solution)/shard_map/ppermute | solution.py:435
  222.5 27.2 %collective-permute-start.26 = (bf16[392,128]{1,0:T(8,128)(2,1)S(1)}, bf16[392,128]{1,0:T(8,128)(2,1)}, u32[]{:S(2)}, u32[]{:S(2)}) collective-permute-start(bf16[392,128]{1,0:T(8,128)(2,1)S(1)} %slice.318), channel_id=1, source_target_pairs={{0,4},{2,6},{4,0},{6,2},{1,5},{3,7},{5,1},{7,3},{8,12},{10,14},{12... | collective-permute-start | bytes 301064 | tf_op jit(solution)/shard_map/ppermute | solution.py:435
  225.8 23.8 %collective-permute-start.27 = (bf16[392,128]{1,0:T(8,128)(2,1)S(1)}, bf16[392,128]{1,0:T(8,128)(2,1)}, u32[]{:S(2)}, u32[]{:S(2)}) collective-permute-start(bf16[392,128]{1,0:T(8,128)(2,1)S(1)} %slice.319), channel_id=1, source_target_pairs={{0,6},{2,4},{4,2},{6,0},{1,7},{3,5},{5,3},{7,1},{8,14},{10,12},{12... | collective-permute-start | bytes 301064 | tf_op jit(solution)/shard_map/ppermute | solution.py:435
  252.9 24.6 %collective-permute-start.31 = (bf16[128,2560]{1,0:T(8,128)(2,1)}, bf16[128,2560]{1,0:T(8,128)(2,1)}, u32[]{:S(2)}, u32[]{:S(2)}) collective-permute-start(bf16[128,2560]{1,0:T(8,128)(2,1)} %get-tuple-element.230), channel_id=1, source_target_pairs={{0,8},{8,0},{16,24},{24,16},{1,9},{9,1},{17,25},{25,17},{2,10},{10... | collective-permute-start | bytes 1966088 | tf_op jit(solution)/shard_map/ppermute | solution.py:435
  253.6 23.8 %collective-permute-start.32 = (bf16[128,2560]{1,0:T(8,128)(2,1)}, bf16[128,2560]{1,0:T(8,128)(2,1)}, u32[]{:S(2)}, u32[]{:S(2)}) collective-permute-start(bf16[128,2560]{1,0:T(8,128)(2,1)} %get-tuple-element.231), channel_id=1, source_target_pairs={{0,16},{8,24},{16,0},{24,8},{1,17},{9,25},{17,1},{25,9},{2,18},{10... | collective-permute-start | bytes 1966088 | tf_op jit(solution)/shard_map/ppermute | solution.py:435
  256.0 21.4 %collective-permute-start.30 = (bf16[128,2048]{1,0:T(8,128)(2,1)}, bf16[128,2048]{1,0:T(8,128)(2,1)}, u32[]{:S(2)}, u32[]{:S(2)}) collective-permute-start(bf16[128,2048]{1,0:T(8,128)(2,1)} %get-tuple-element.323), channel_id=1, source_target_pairs={{0,2},{2,0},{4,6},{6,4},{1,3},{3,1},{5,7},{7,5},{8,10},{10,8},{12,... | collective-permute-start | bytes 1572872 | tf_op jit(solution)/shard_map/ppermute | solution.py:435
  307.8 24.6 %collective-permute-start.37 = (bf16[392,1024]{1,0:T(8,128)(2,1)S(1)}, bf16[392,1024]{1,0:T(8,128)(2,1)S(1)}, u32[]{:S(2)}, u32[]{:S(2)}) collective-permute-start(bf16[392,1024]{1,0:T(8,128)(2,1)S(1)} %pad_maximum_fusion.5), channel_id=1, source_target_pairs={{0,2},{2,0},{4,6},{6,4},{1,3},{3,1},{5,7},{7,5},{8,10},{10,8},{12,... | collective-permute-start | bytes 2408456 | tf_op jit(solution)/shard_map/ppermute | solution.py:435
  333.3 34.9 %collective-permute-start.59 = (bf16[128,2048]{1,0:T(8,128)(2,1)S(1)}, bf16[128,2048]{1,0:T(8,128)(2,1)}, u32[]{:S(2)}, u32[]{:S(2)}) collective-permute-start(bf16[128,2048]{1,0:T(8,128)(2,1)S(1)} %maximum_select_fusion.3), channel_id=1, source_target_pairs={{0,2},{2,0},{4,6},{6,4},{1,3},{3,1},{5,7},{7,5},{8,10},{10,8},{12,... | collective-permute-start | bytes 1572872 | tf_op jit(solution)/shard_map/ppermute | solution.py:435
  335.2 35.8 %collective-permute-start.43 = (bf16[128,2560]{1,0:T(8,128)(2,1)S(1)}, bf16[128,2560]{1,0:T(8,128)(2,1)S(1)}, u32[]{:S(2)}, u32[]{:S(2)}) collective-permute-start(bf16[128,2560]{1,0:T(8,128)(2,1)S(1)} %dynamic-slice_convert_fusion), channel_id=1, source_target_pairs={{0,2},{2,0},{4,6},{6,4},{1,3},{3,1},{5,7},{7,5},{8,10},{10,8},{12,... | collective-permute-start | bytes 1966088 | tf_op jit(solution)/shard_map/ppermute | solution.py:435
  351.1 17.0 %collective-permute-start.40 = (bf16[392,256]{1,0:T(8,128)(2,1)S(1)}, bf16[392,256]{1,0:T(8,128)(2,1)S(1)}, u32[]{:S(2)}, u32[]{:S(2)}) collective-permute-start(bf16[392,256]{1,0:T(8,128)(2,1)S(1)} %get-tuple-element.309), channel_id=1, source_target_pairs={{0,6},{2,4},{4,2},{6,0},{1,7},{3,5},{5,3},{7,1},{8,14},{10,12},{12... | collective-permute-start | bytes 602120 | tf_op jit(solution)/shard_map/ppermute | solution.py:435
  353.2 17.8 %collective-permute-start.41 = (bf16[128,768]{1,0:T(8,128)(2,1)S(1)}, bf16[128,768]{1,0:T(8,128)(2,1)S(1)}, u32[]{:S(2)}, u32[]{:S(2)}) collective-permute-start(bf16[128,768]{1,0:T(8,128)(2,1)S(1)} %get-tuple-element.322), channel_id=1, source_target_pairs={{0,8},{8,0},{16,24},{24,16},{1,9},{9,1},{17,25},{25,17},{2,10},{10... | collective-permute-start | bytes 589832 | tf_op jit(solution)/shard_map/ppermute | solution.py:435
  385.7 30.5 %collective-permute-start.49 = (f32[72,128]{1,0:T(8,128)S(1)}, f32[72,128]{1,0:T(8,128)S(1)}, u32[]{:S(2)}, u32[]{:S(2)}) collective-permute-start(f32[72,128]{1,0:T(8,128)S(1)} %bitcast.116), channel_id=1, source_target_pairs={{0,2},{2,0},{4,6},{6,4},{1,3},{3,1},{5,7},{7,5},{8,10},{10,8},{12,... | collective-permute-start | bytes 110600 | tf_op jit(solution)/shard_map/ppermute | solution.py:435
  386.5 29.7 %collective-permute-start.50 = (f32[72,128]{1,0:T(8,128)S(1)}, f32[72,128]{1,0:T(8,128)S(1)}, u32[]{:S(2)}, u32[]{:S(2)}) collective-permute-start(f32[72,128]{1,0:T(8,128)S(1)} %bitcast.117), channel_id=1, source_target_pairs={{0,4},{2,6},{4,0},{6,2},{1,5},{3,7},{5,1},{7,3},{8,12},{10,14},{12... | collective-permute-start | bytes 110600 | tf_op jit(solution)/shard_map/ppermute | solution.py:435
  388.0 28.3 %collective-permute-start.51 = (f32[72,128]{1,0:T(8,128)S(1)}, f32[72,128]{1,0:T(8,128)S(1)}, u32[]{:S(2)}, u32[]{:S(2)}) collective-permute-start(f32[72,128]{1,0:T(8,128)S(1)} %bitcast.118), channel_id=1, source_target_pairs={{0,6},{2,4},{4,2},{6,0},{1,7},{3,5},{5,3},{7,1},{8,14},{10,12},{12... | collective-permute-start | bytes 110600 | tf_op jit(solution)/shard_map/ppermute | solution.py:435
  390.3 25.8 %collective-permute-start.53 = (bf16[64,2560]{1,0:T(8,128)(2,1)S(1)}, bf16[64,2560]{1,0:T(8,128)(2,1)S(1)}, u32[]{:S(2)}, u32[]{:S(2)}) collective-permute-start(bf16[64,2560]{1,0:T(8,128)(2,1)S(1)} %add_convert_fusion.4), channel_id=1, source_target_pairs={{0,4},{2,6},{4,0},{6,2},{1,5},{3,7},{5,1},{7,3},{8,12},{10,14},{12... | collective-permute-start | bytes 983048 | tf_op jit(solution)/shard_map/ppermute | solution.py:435
  390.5 33.7 %collective-permute-start.52 = (bf16[256,768]{1,0:T(8,128)(2,1)S(1)}, bf16[256,768]{1,0:T(8,128)(2,1)S(1)}, u32[]{:S(2)}, u32[]{:S(2)}) collective-permute-start(bf16[256,768]{1,0:T(8,128)(2,1)S(1)} %fusion.4), channel_id=1, source_target_pairs={{0,4},{2,6},{4,0},{6,2},{1,5},{3,7},{5,1},{7,3},{8,12},{10,14},{12... | collective-permute-start | bytes 1179656 | tf_op jit(solution)/shard_map/ppermute | solution.py:435
  427.8 26.2 %collective-permute-start.58 = (bf16[128,2560]{1,0:T(8,128)(2,1)S(1)}, bf16[128,2560]{1,0:T(8,128)(2,1)}, u32[]{:S(2)}, u32[]{:S(2)}) collective-permute-start(bf16[128,2560]{1,0:T(8,128)(2,1)S(1)} %maximum_select_fusion.2), channel_id=1, source_target_pairs={{0,2},{2,0},{4,6},{6,4},{1,3},{3,1},{5,7},{7,5},{8,10},{10,8},{12,... | collective-permute-start | bytes 1966088 | tf_op jit(solution)/shard_map/ppermute | solution.py:435
  427.9 23.9 %collective-permute-start.57 = (bf16[256,768]{1,0:T(8,128)(2,1)S(1)}, bf16[256,768]{1,0:T(8,128)(2,1)S(1)}, u32[]{:S(2)}, u32[]{:S(2)}) collective-permute-start(bf16[256,768]{1,0:T(8,128)(2,1)S(1)} %add_convert_fusion.3), channel_id=1, source_target_pairs={{0,2},{2,0},{4,6},{6,4},{1,3},{3,1},{5,7},{7,5},{8,10},{10,8},{12,... | collective-permute-start | bytes 1179656 | tf_op jit(solution)/shard_map/ppermute | solution.py:435
  (104 other events, 628.2 us)
Sparse Core Ops, SparseCore 0:
  9.9 76.2 all-gather.1
  173.4 57.2 reduce-scatter.1
